TPU v7x, 256 devices: a whole 4x4x8 slice. The times are simulated.
256 devices in a mesh: dp: 32 (over y, x, core), expert: 8 (over z).
Axes of the slice: x: 4, y: 4, z: 8, core: 2. Of those that a mesh axis runs over, the one named last changes fastest.
Arguments:
- tokens: bfloat16 [4096, 2048], P('dp'), may hold values from -6 to 6
- route_expert: int32 [4096, 4], P('dp'), may hold values from 0 to 31, all different within a row; in each aligned block of 128 rows (0 to 127, 128 to 255, ...) at most 32 rows name the same one
- route_weight: float32 [4096, 4], P('dp'), may hold values from 0.1 to 1
- gate_weight: bfloat16 [32, 1408, 2048], P('dp', 'expert'), may hold values from -0.125 to 0.125
- up_weight: bfloat16 [32, 1408, 2048], P('dp', 'expert'), may hold values from -0.125 to 0.125
- down_weight: bfloat16 [32, 1408, 2048], P('dp', 'expert'), may hold values from -0.15625 to 0.15625
- gate_scale: float32 [32, 1408], P('dp', 'expert'), may hold values from 0.5 to 2
- up_scale: float32 [32, 1408], P('dp', 'expert'), may hold values from 0.5 to 2
- down_scale: float32 [32, 2048], replicated, may hold values from 0.5 to 2
- cotangent: bfloat16 [4096, 2048], P('dp', 'expert'), may hold values from -6 to 6
Outputs:
- mixed: bfloat16 [4096, 2048], P('dp', 'expert')
- token_grad: bfloat16 [4096, 2048], P('dp', 'expert')
- route_grad: float32 [4096, 4], P('dp')
- gate_grad: float32 [32, 1408, 2048], P('dp', 'expert')
- up_grad: float32 [32, 1408, 2048], P('dp', 'expert')
- down_grad: float32 [32, 1408, 2048], P('dp', 'expert')
Inputs may be any that keep to these rules, and one draw needn't show every extreme that they name: `route_expert`: each row names 4 different experts. Among the 128 rows of one aligned block (the tokens of one index of dp) no expert is named by more than 32 rows, and in some block one expert is named by exactly 32 rows.
All inputs are finite; a program needn't handle non-finite values.
Results may differ from a plain program's by a relative error of at most 0.0058.
Values may be sent and summed in bfloat16 or wider, within the bound.
No kernel may reach another device: no remote copies, remote signals or barrier semaphores. Data moves between devices by JAX's collectives and lax.ppermute only.
A program may use at most 128 MiB of HBM per device.

v0:
```python
import jax
import jax.numpy as jnp
from jax import lax
from jax.sharding import PartitionSpec as P


def local(
    tokens,
    route_expert,
    route_weight,
    gate_weight,
    up_weight,
    down_weight,
    gate_scale,
    up_scale,
    down_scale,
    cotangent,
):
    owners = lax.axis_size("dp")
    tok_rows, width = tokens.shape
    choose = route_expert.shape[1]
    capacity = 2 * tok_rows * choose // owners
    slots = owners * capacity
    assigned = tok_rows * choose
    col_share = width // lax.axis_size("expert")
    col_start = lax.axis_index("expert") * col_share
    flat_expert = route_expert.reshape(-1)
    one_hot = (flat_expert[:, None] == jnp.arange(owners, dtype=jnp.int32)[None, :]).astype(
        jnp.int32
    )
    ranks = jnp.sum((jnp.cumsum(one_hot, axis=0) - 1) * one_hot, axis=1)
    slot_index = flat_expert * capacity + ranks
    slot_token = (
        jnp.zeros((slots,), jnp.int32)
        .at[slot_index]
        .set(jnp.arange(assigned, dtype=jnp.int32) // choose)
    )
    filled = jnp.zeros((slots,), jnp.bool_).at[slot_index].set(True)
    slot_weight = jnp.zeros((slots,), jnp.float32).at[slot_index].set(route_weight.reshape(-1))
    outgoing = jnp.where(
        filled[:, None], jnp.take(tokens, slot_token, axis=0), jnp.zeros((), tokens.dtype)
    )
    arrived = lax.all_to_all(
        outgoing.reshape(owners, capacity, width), "dp", split_axis=0, concat_axis=0, tiled=True
    ).reshape(slots, width)
    gate_local = gate_weight[0]
    up_local = up_weight[0]
    down_local = down_weight[0]
    gate_pre = (
        lax.dot_general(
            arrived, gate_local, (((1,), (1,)), ((), ())), preferred_element_type=jnp.float32
        )
        * gate_scale[0][None, :]
    )
    up_pre = (
        lax.dot_general(
            arrived, up_local, (((1,), (1,)), ((), ())), preferred_element_type=jnp.float32
        )
        * up_scale[0][None, :]
    )
    sigmoid_gate = jax.nn.sigmoid(gate_pre)
    silu_gate = gate_pre * sigmoid_gate
    hidden = (silu_gate * up_pre).astype(jnp.bfloat16)
    summed = lax.psum_scatter(
        lax.dot_general(
            down_local, hidden, (((0,), (1,)), ((), ())), preferred_element_type=jnp.float32
        ),
        "expert",
        scatter_dimension=0,
        tiled=True,
    )
    owner_scale = lax.dynamic_slice(down_scale, (lax.axis_index("dp"), col_start), (1, col_share))[
        0
    ]
    out_cols = (summed * owner_scale[:, None]).astype(jnp.bfloat16)
    returned = lax.all_to_all(
        out_cols.reshape(col_share, owners, capacity), "dp", split_axis=1, concat_axis=1, tiled=True
    ).reshape(col_share, slots)
    picked = (
        jnp.take(returned, slot_index, axis=1)
        .reshape(col_share, tok_rows, choose)
        .astype(jnp.float32)
    )
    mixed = jnp.sum(picked * route_weight[None, :, :], axis=2).T.astype(jnp.bfloat16)
    cot_cols = cotangent.T.astype(jnp.float32)
    route_part = jnp.sum(picked * cot_cols[:, :, None], axis=0)
    route_grad = lax.psum(route_part, "expert")
    slot_scale = jnp.repeat(down_scale, capacity, axis=0)
    full_cot = lax.all_gather(cotangent, "expert", axis=1, tiled=True)
    cot_slots = jnp.take(full_cot, slot_token, axis=0).astype(jnp.float32)
    weighted = (cot_slots * slot_weight[:, None] * slot_scale).astype(jnp.bfloat16)
    out_grad = lax.all_to_all(
        weighted.reshape(owners, capacity, width), "dp", split_axis=0, concat_axis=0, tiled=True
    ).reshape(slots, width)
    hidden_grad = lax.dot_general(
        out_grad, down_local, (((1,), (1,)), ((), ())), preferred_element_type=jnp.float32
    )
    gate_in = (
        hidden_grad
        * up_pre
        * sigmoid_gate
        * (1.0 + gate_pre * (1.0 - sigmoid_gate))
        * gate_scale[0][None, :]
    ).astype(jnp.bfloat16)
    up_in = (hidden_grad * silu_gate * up_scale[0][None, :]).astype(jnp.bfloat16)
    down_grad = lax.dot_general(
        hidden, out_grad, (((0,), (0,)), ((), ())), preferred_element_type=jnp.float32
    )
    gate_grad = lax.dot_general(
        gate_in, arrived, (((0,), (0,)), ((), ())), preferred_element_type=jnp.float32
    )
    up_grad = lax.dot_general(
        up_in, arrived, (((0,), (0,)), ((), ())), preferred_element_type=jnp.float32
    )
    first = lax.dot_general(
        gate_local, gate_in, (((0,), (1,)), ((), ())), preferred_element_type=jnp.float32
    )
    second = lax.dot_general(
        up_local, up_in, (((0,), (1,)), ((), ())), preferred_element_type=jnp.float32
    )
    input_cols = lax.psum_scatter(first + second, "expert", scatter_dimension=0, tiled=True)
    input_home = lax.all_to_all(
        input_cols.reshape(col_share, owners, capacity),
        "dp",
        split_axis=1,
        concat_axis=1,
        tiled=True,
    ).reshape(col_share, slots)
    token_grad = jnp.sum(
        jnp.take(input_home, slot_index, axis=1).reshape(col_share, tok_rows, choose), axis=2
    ).T.astype(jnp.bfloat16)
    return (mixed, token_grad, route_grad, gate_grad[None], up_grad[None], down_grad[None])


def solution(mesh):
    return jax.shard_map(
        local,
        mesh=mesh,
        in_specs=(
            P("dp", None),
            P("dp", None),
            P("dp", None),
            P("dp", "expert", None),
            P("dp", "expert", None),
            P("dp", "expert", None),
            P("dp", "expert"),
            P("dp", "expert"),
            P(),
            P("dp", "expert"),
        ),
        out_specs=(
            P("dp", "expert"),
            P("dp", "expert"),
            P("dp", None),
            P("dp", "expert", None),
            P("dp", "expert", None),
            P("dp", "expert", None),
        ),
        check_vma=False,
    )
```

profile of v0, /device:TPU:2, one launch (start us, length us, event | category | flops | bytes accessed | tf_op | source)
XLA Modules:
  0.0 436.8 jit_solution(8157642740581195982)
XLA Ops:
  7.2 0.9 copy.18
  8.0 0.1 eq.26
  8.2 0.1 reshape.136
  8.3 1.2 reduce-window.6
  9.5 0.2 slice_reduce_fusion
  9.7 0.1 mul.123
  9.8 0.1 fusion.11
  10.0 2.4 scatter_custom_fusion.1
  12.4 0.8 copy.22
  13.2 0.1 reshape.200
  13.3 29.3 %all_gather.3 = bf16[128,2048]{1,0:T(8,128)(2,1)S(1)} all-gather(bf16[128,256]{1,0:T(8,128)(2,1)} %param.21), channel_id=1, replica_groups=mesh['dp'=32,'expert'=8] {'expert'}, dimensions={1}, use_global_device_ids=true | all-gather | bytes 589824 | tf_op jit(solution)/shard_map/all_gather | solution.py:89
  42.7 2.4 scatter_custom_fusion.2
  45.1 6.0 %gather_fusion.3 = bf16[1024,2048]{1,0:T(8,128)(2,1)} fusion(bf16[128,2048]{1,0:T(8,128)(2,1)S(1)} %all_gather.3, s32[1024]{0:T(1024)S(1)} %fusion.13), kind=kCustom, calls=%fused_computation.1.clone | custom fusion | bytes 8392704 | tf_op jit(solution)/shard_map/jit(_take)/gather | solution.py:90
  51.2 4.5 %fusion = bf16[1024,2048]{1,0:T(8,128)(2,1)} fusion(bf16[1024,2048]{1,0:T(8,128)(2,1)} %gather_fusion.3, f32[32,2048]{1,0:T(8,128)S(1)} %copy-done.7, f32[1024]{0:T(1024)S(1)} %scatter_custom_fusion.2, pred[1024]{0:T(1024)(128)(4,1)S(1)} %compare_and_fusion.1), kind=kLoop, calls=%fused_computation.8 | loop fusion | flops 10485760 | bytes 8655872 | tf_op jit(solution)/shard_map/convert_element_type | solution.py:91
  55.6 7.8 %all-to-all-start.2 = ((bf16[32,32,2048]{2,1,0:T(8,128)(2,1)}), bf16[32,32,2048]{2,1,0:T(8,128)(2,1)}, u32[]{:S(2)}, u32[]{:S(2)}) async-start(bf16[32,32,2048]{2,1,0:T(8,128)(2,1)} %bitcast.93), calls=%async_computation.3 | async-start | bytes 8388608 | tf_op jit(solution)/shard_map/all_to_all | solution.py:92
  63.4 6.0 %gather_fusion.2 = bf16[1024,2048]{1,0:T(8,128)(2,1)} fusion(bf16[128,2048]{1,0:T(8,128)(2,1)S(1)} %copy-done.1, s32[1024]{0:T(1024)S(1)} %fusion.13), kind=kCustom, calls=%fused_computation.clone | custom fusion | bytes 8392704 | tf_op jit(solution)/shard_map/jit(_take)/gather | solution.py:41
  69.5 2.4 scatter_custom_fusion
  71.9 4.0 select_select_fusion
  75.9 38.9 %all-to-all-done.2 = bf16[32,32,2048]{2,1,0:T(8,128)(2,1)} async-done(((bf16[32,32,2048]{2,1,0:T(8,128)(2,1)}), bf16[32,32,2048]{2,1,0:T(8,128)(2,1)}, u32[]{:S(2)}, u32[]{:S(2)}) %all-to-all-start.2) | async-done | bytes 4194336 | tf_op jit(solution)/shard_map/all_to_all | solution.py:92
  114.9 7.4 %all-to-all-start = ((bf16[32,32,2048]{2,1,0:T(8,128)(2,1)}), bf16[32,32,2048]{2,1,0:T(8,128)(2,1)}, u32[]{:S(2)}, u32[]{:S(2)}) async-start(bf16[32,32,2048]{2,1,0:T(8,128)(2,1)} %bitcast.92), calls=%async_computation | async-start | bytes 8388608 | tf_op jit(solution)/shard_map/all_to_all | solution.py:43
  122.3 0.2 reduce-scatter.3.cloned.1.call-start
  122.5 4.6 %fusion.1 = f32[1024,176]{0,1:T(8,128)} fusion(bf16[1024,2048]{1,0:T(8,128)(2,1)} %bitcast.18, bf16[1,176,2048]{2,1,0:T(8,128)(2,1)S(1)} %copy-done.5), kind=kOutput, calls=%fused_computation.18 | convolution fusion | flops 738197504 | bytes 5636096 | tf_op jit(solution)/shard_map/dot_general | solution.py:95
  127.1 46.7 %all-to-all-done = bf16[32,32,2048]{2,1,0:T(8,128)(2,1)} async-done(((bf16[32,32,2048]{2,1,0:T(8,128)(2,1)}), bf16[32,32,2048]{2,1,0:T(8,128)(2,1)}, u32[]{:S(2)}, u32[]{:S(2)}) %all-to-all-start) | async-done | bytes 4194336 | tf_op jit(solution)/shard_map/all_to_all | solution.py:43
  173.8 3.8 convolution_multiply_fusion.1
  177.6 4.0 multiply_convert_fusion.3
  181.7 0.7 copy-done.2
  182.4 4.5 %convolution_bitcast_fusion = f32[2048,1024]{0,1:T(8,128)} fusion(bf16[1024,176]{0,1:T(8,128)(2,1)S(1)} %get-tuple-element.15, bf16[1,176,2048]{2,1,0:T(8,128)(2,1)S(1)} %copy-done.5), kind=kOutput, calls=%fused_computation.10 | convolution fusion | flops 738197504 | bytes 9469952 | tf_op jit(solution)/shard_map/dot_general | solution.py:65
  187.0 1.3 fusion.6
  188.3 4.5 %add_bitcast_fusion = f32[2048,1024]{0,1:T(8,128)} fusion(f32[1024,2048]{1,0:T(8,128)S(1)} %fusion.6, bf16[1024,176]{0,1:T(8,128)(2,1)S(1)} %get-tuple-element.17, bf16[1,176,2048]{2,1,0:T(8,128)(2,1)S(1)} %copy-done), kind=kOutput, calls=%fused_computation.9 | convolution fusion | flops 740294656 | bytes 17858560 | tf_op jit(solution)/shard_map/dot_general | solution.py:118
  192.8 0.1 reduce_sum.43
  193.0 85.6 %reduce-scatter.3.cloned.1.call-done = f32[256,1024]{0,1:T(8,128)} async-done(((f32[2048,1024]{0,1:T(8,128)}), f32[256,1024]{0,1:T(8,128)}) %reduce-scatter.3.cloned.1.call-update) | async-done | bytes 1048592 | tf_op jit(solution)/shard_map/reduce_scatter | solution.py:64
  278.6 2.1 multiply_convert_fusion
  280.7 7.4 %all-to-all-start.1 = ((bf16[256,32,32]{0,2,1:T(8,128)(2,1)}), bf16[256,32,32]{0,2,1:T(8,128)(2,1)S(1)}, u32[]{:S(2)}, u32[]{:S(2)}) async-start(bf16[256,32,32]{0,2,1:T(8,128)(2,1)} %bitcast.12), calls=%async_computation.2 | async-start | bytes 1048576 | tf_op jit(solution)/shard_map/all_to_all | solution.py:76
  288.1 0.1 broadcast_in_dim.87
  288.4 0.2 mul.149
  288.6 86.1 %reduce-scatter.5.cloned.1.call-done = f32[256,1024]{0,1:T(8,128)} async-done(((f32[2048,1024]{0,1:T(8,128)}), f32[256,1024]{0,1:T(8,128)}) %reduce-scatter.5.cloned.1.call-update) | async-done | bytes 1048592 | tf_op jit(solution)/shard_map/reduce_scatter | solution.py:121
  374.7 7.4 %all-to-all-start.3 = ((f32[256,32,32]{0,2,1:T(8,128)}), f32[256,32,32]{0,2,1:T(8,128)S(1)}, u32[]{:S(2)}, u32[]{:S(2)}) async-start(f32[256,32,32]{0,2,1:T(8,128)} %bitcast.97), calls=%async_computation.5 | async-start | bytes 2097152 | tf_op jit(solution)/shard_map/all_to_all | solution.py:122
  382.2 4.3 convolution_bitcast_fusion.1
  386.5 4.3 convolution_bitcast_fusion.3
  390.8 4.2 convolution_bitcast_fusion.2
  395.0 1.9 gather_fusion
  397.0 0.2 multiply_reduce_fusion
  397.3 0.1 reduce_sum.48
  397.4 28.7 %psum.7 = f32[128,4]{1,0:T(8,128)S(1)} all-reduce(f32[128,4]{1,0:T(8,128)S(1)} %reduce_sum.48), channel_id=1, replica_groups=mesh['dp'=32,'expert'=8] {'expert'}, use_global_device_ids=true, to_apply=%region_11.13 | all-reduce | flops 512 | bytes 4096 | tf_op jit(solution)/shard_map/psum | solution.py:87
  426.1 0.7 copy.24
  426.7 1.6 gather_fusion.1
  428.3 0.1 gather.18
  428.5 1.4 select_reduce_fusion
  (43 shorter events, 0.5 us)
Async XLA Ops:
  7.2 170.4 %copy-start = (bf16[1,176,2048]{2,1,0:T(8,128)(2,1)S(1)}, bf16[1,176,2048]{2,1,0:T(8,128)(2,1)}, u32[]{:S(2)}) copy-start(bf16[1,176,2048]{2,1,0:T(8,128)(2,1)} %param.16) | copy-start | bytes 2162692
  45.1 6.0 %copy-start.7 = (f32[32,2048]{1,0:T(8,128)S(1)}, f32[32,2048]{1,0:T(8,128)}, u32[]{:S(2)}) copy-start(f32[32,2048]{1,0:T(8,128)} %param.20) | copy-start | bytes 786436
  55.6 7.8 %copy-start.1 = (bf16[128,2048]{1,0:T(8,128)(2,1)S(1)}, bf16[128,2048]{1,0:T(8,128)(2,1)}, u32[]{:S(2)}) copy-start(bf16[128,2048]{1,0:T(8,128)(2,1)} %param.12) | copy-start | bytes 1572868
  55.6 59.2 %all-to-all-start.2 = ((bf16[32,32,2048]{2,1,0:T(8,128)(2,1)}), bf16[32,32,2048]{2,1,0:T(8,128)(2,1)}, u32[]{:S(2)}, u32[]{:S(2)}) async-start(bf16[32,32,2048]{2,1,0:T(8,128)(2,1)} %bitcast.93), calls=%async_computation.3 | async-start | bytes 8388608 | tf_op jit(solution)/shard_map/all_to_all | solution.py:92
  114.9 7.7 %copy-start.5 = (bf16[1,176,2048]{2,1,0:T(8,128)(2,1)S(1)}, bf16[1,176,2048]{2,1,0:T(8,128)(2,1)}, u32[]{:S(2)}) copy-start(bf16[1,176,2048]{2,1,0:T(8,128)(2,1)} %param.17) | copy-start | bytes 2162692
  114.9 58.9 %all-to-all-start = ((bf16[32,32,2048]{2,1,0:T(8,128)(2,1)}), bf16[32,32,2048]{2,1,0:T(8,128)(2,1)}, u32[]{:S(2)}, u32[]{:S(2)}) async-start(bf16[32,32,2048]{2,1,0:T(8,128)(2,1)} %bitcast.92), calls=%async_computation | async-start | bytes 8388608 | tf_op jit(solution)/shard_map/all_to_all | solution.py:43
  122.3 51.5 %copy-start.6 = (bf16[1,176,2048]{2,1,0:T(8,128)(2,1)S(1)}, bf16[1,176,2048]{2,1,0:T(8,128)(2,1)}, u32[]{:S(2)}) copy-start(bf16[1,176,2048]{2,1,0:T(8,128)(2,1)} %param.15) | copy-start | bytes 2162692
  122.3 51.5 %copy-start.9 = (f32[1,176]{1,0:T(1,128)S(1)}, f32[1,176]{1,0:T(1,128)}, u32[]{:S(2)}) copy-start(f32[1,176]{1,0:T(1,128)} %param.18) | copy-start | bytes 2116
  122.3 156.3 %reduce-scatter.3.cloned.1.call-start = ((), (), s32[]{:S(2)}) async-start(), calls=%async_computation.6 | async-start | bytes 9437184 | tf_op jit(solution)/shard_map/reduce_scatter | solution.py:64
  127.1 50.5 %copy-start.10 = (f32[1,176]{1,0:T(1,128)S(1)}, f32[1,176]{1,0:T(1,128)}, u32[]{:S(2)}) copy-start(f32[1,176]{1,0:T(1,128)} %param.19) | copy-start | bytes 2116
  173.8 3.8 copy-start.11
  181.7 0.7 copy-start.2
  181.7 6.6 %copy-start.3 = (bf16[1024,176]{0,1:T(8,128)(2,1)}, bf16[1024,176]{0,1:T(8,128)(2,1)S(1)}, u32[]{:S(2)}) copy-start(bf16[1024,176]{0,1:T(8,128)(2,1)S(1)} %get-tuple-element.17) | copy-start | bytes 1081348
  186.9 187.8 %reduce-scatter.5.cloned.1.call-start = ((), (), s32[]{:S(2)}) async-start(), calls=%async_computation.7 | async-start | bytes 9437184 | tf_op jit(solution)/shard_map/reduce_scatter | solution.py:121
  192.8 95.5 %copy-start.8 = (bf16[128,256]{1,0:T(8,128)(2,1)S(1)}, bf16[128,256]{1,0:T(8,128)(2,1)}, u32[]{:S(2)}) copy-start(bf16[128,256]{1,0:T(8,128)(2,1)} %param.21) | copy-start | bytes 196612
  280.7 94.0 %all-to-all-start.1 = ((bf16[256,32,32]{0,2,1:T(8,128)(2,1)}), bf16[256,32,32]{0,2,1:T(8,128)(2,1)S(1)}, u32[]{:S(2)}, u32[]{:S(2)}) async-start(bf16[256,32,32]{0,2,1:T(8,128)(2,1)} %bitcast.12), calls=%async_computation.2 | async-start | bytes 1048576 | tf_op jit(solution)/shard_map/all_to_all | solution.py:76
  374.7 52.0 %all-to-all-start.3 = ((f32[256,32,32]{0,2,1:T(8,128)}), f32[256,32,32]{0,2,1:T(8,128)S(1)}, u32[]{:S(2)}, u32[]{:S(2)}) async-start(f32[256,32,32]{0,2,1:T(8,128)} %bitcast.97), calls=%async_computation.5 | async-start | bytes 2097152 | tf_op jit(solution)/shard_map/all_to_all | solution.py:122
  386.5 4.3 copy-start.4
Sparse Core Ops, SparseCore 0:
  187.0 91.5 reduce-scatter.2
  281.1 93.5 reduce-scatter.4
where the time goes:
time: 437 us
  waiting for transfers between devices  257 us (59%)
  blocking collectives  58 us (13%)
  matrix products  35.5 us (8%)
  starting transfers between devices  30.3 us (7%)
  local copies, waits for them, and re-layouts  27.5 us (6%)
  between operations  14.4 us (3%)
  other arithmetic  13.6 us (3%)
    reduce_scatter x1, waiting for transfers between devices, local(): lax.psum_scatter(first + second, 'expert', scatter_dimension=0, tiled=True)  86.1 us
    reduce_scatter x1, waiting for transfers between devices, local(): lax.psum_scatter(lax.dot_general(down_local, hidden, (((0,), (1,)), ((),...  85.6 us
    all_to_all x1, waiting for transfers between devices, local(): lax.all_to_all(outgoing.reshape(owners, capacity, width), 'dp', split_axi...  46.7 us
    all_to_all x1, waiting for transfers between devices, local(): lax.all_to_all(weighted.reshape(owners, capacity, width), 'dp', split_axi...  38.9 us
    all_gather x1, blocking collectives, local(): full_cot = lax.all_gather(cotangent, 'expert', axis=1, tiled=True)  29.3 us
    psum x1, blocking collectives, local(): route_grad = lax.psum(route_part, 'expert')  28.7 us
  transfers between devices with their start and end apart: 6, of which 4 were waited for; matrix products, arithmetic and copies ran while one was open for 9% of the time, Pallas kernels for 0%

commit v1 on v0

v1 whole, which is shorter than its diff:
```python
import functools

import jax
import jax.numpy as jnp
from jax import lax
from jax.experimental import pallas as pl
from jax.experimental.pallas import tpu as pltpu
from jax.sharding import PartitionSpec as P


F32 = jnp.float32
BF16 = jnp.bfloat16
NT = (((1,), (1,)), ((), ()))
NN = (((1,), (0,)), ((), ()))
TN = (((0,), (0,)), ((), ()))


def dot(a, b, dims=NN, **kw):
    return lax.dot_general(a, b, dims, preferred_element_type=F32, **kw)


def cost(flops, nbytes):
    return pl.CostEstimate(flops=flops, bytes_accessed=nbytes, transcendentals=0)


def iota(shape, dim):
    return lax.broadcasted_iota(jnp.int32, shape, dim)


def route_kernel(cap, col_ref, re_ref, rw_ref, cot_ref, ds_ref, m_ref, send_ref):
    choose, toks = re_ref.shape
    experts = ds_ref.shape[0]
    expert_id = iota((experts, toks), 0)
    named = jnp.zeros((experts, toks), F32)
    weight = jnp.zeros((experts, toks), F32)
    for k in range(choose):
        hit = re_ref[k : k + 1, :] == expert_id
        named = named + jnp.where(hit, 1.0, 0.0)
        weight = weight + jnp.where(hit, rw_ref[k : k + 1, :], 0.0)
    before = jnp.where(iota((toks, toks), 0) < iota((toks, toks), 1), 1.0, 0.0).astype(BF16)
    rank = dot(named.astype(BF16), before).astype(jnp.int32)
    code = jnp.where(named > 0.0, rank, -1)
    place = iota((cap, toks), 0)
    slot_weight = []
    for e in range(experts):
        hit = code[e : e + 1, :] == place
        m_ref[e * cap : (e + 1) * cap, :] = jnp.where(hit, 1.0, 0.0).astype(BF16)
        slot_weight.append(
            jnp.sum(jnp.where(hit, weight[e : e + 1, :], 0.0), axis=1, keepdims=True)
        )
    group = 8
    for g in range(experts // group):
        rows = dot(m_ref[g * group * cap : (g + 1) * group * cap, :], cot_ref[...])
        for i in range(group):
            e = g * group + i
            send_ref[e * cap : (e + 1) * cap, :] = (
                rows[i * cap : (i + 1) * cap, :] * slot_weight[e] * ds_ref[e : e + 1, :]
            ).astype(BF16)


def home_kernel(cap, re_ref, rw_ref, mt_ref, mh_ref, ml_ref):
    toks, choose = re_ref.shape
    slots = mt_ref.shape[1]
    experts = slots // cap
    expert_id = iota((toks, experts), 1)
    named = jnp.zeros((toks, experts), F32)
    weight = jnp.zeros((toks, experts), F32)
    for k in range(choose):
        hit = re_ref[:, k : k + 1] == expert_id
        named = named + jnp.where(hit, 1.0, 0.0)
        weight = weight + jnp.where(hit, rw_ref[:, k : k + 1], 0.0)
    before = jnp.where(iota((toks, toks), 1) < iota((toks, toks), 0), 1.0, 0.0).astype(BF16)
    rank = dot(before, named.astype(BF16))
    code = jnp.where(named > 0.0, rank, 128.0).astype(BF16)
    low = iota((experts, slots), 0) * cap
    slot = iota((experts, slots), 1)
    spread = jnp.where((slot >= low) & (slot < low + cap), 1.0, 0.0).astype(BF16)
    high = weight.astype(BF16)
    rest = (weight - high.astype(F32)).astype(BF16)
    place = (iota((toks, slots), 1) & (cap - 1)).astype(F32)
    hit = dot(code, spread) == place
    mt_ref[...] = jnp.where(hit, 1.0, 0.0).astype(BF16)
    mh_ref[...] = jnp.where(hit, dot(high, spread), 0.0).astype(BF16)
    ml_ref[...] = jnp.where(hit, dot(rest, spread), 0.0).astype(BF16)


def forward_kernel(
    e_ref, x_ref, gw_ref, uw_ref, dw_ref, gs_ref, us_ref, ds_ref, g_ref, u_ref, h_ref, y_ref
):
    x = x_ref[...]
    g = dot(x, gw_ref[...], NT) * gs_ref[...]
    u = dot(x, uw_ref[...], NT) * us_ref[...]
    g_ref[...] = g
    u_ref[...] = u
    h = (g * jax.nn.sigmoid(g) * u).astype(BF16)
    h_ref[...] = h
    scale = ds_ref[pl.ds(e_ref[0], 1), :]
    y_ref[...] = (dot(h, dw_ref[...]) * scale).astype(BF16)


def backward_kernel(
    o_ref, g_ref, u_ref, gw_ref, uw_ref, dw_ref, gs_ref, us_ref, gi_ref, ui_ref, p_ref
):
    parts, _, share = o_ref.shape
    hg = dot(o_ref[0], dw_ref[:, :share], NT)
    for c in range(1, parts):
        hg = hg + dot(o_ref[c], dw_ref[:, c * share : (c + 1) * share], NT)
    g = g_ref[...]
    u = u_ref[...]
    s = jax.nn.sigmoid(g)
    gi = (hg * u * s * (1.0 + g * (1.0 - s)) * gs_ref[...]).astype(BF16)
    ui = (hg * (g * s) * us_ref[...]).astype(BF16)
    gi_ref[...] = gi
    ui_ref[...] = ui
    for c in range(parts):
        cols = slice(c * share, (c + 1) * share)
        p_ref[c] = (dot(gi, gw_ref[:, cols]) + dot(ui, uw_ref[:, cols])).astype(BF16)


def combine_kernel(cap, z_ref, y_ref, c_ref, mt_ref, mh_ref, ml_ref, re_ref, o_ref, acc_ref):
    step = pl.program_id(0)
    toks, slots = mt_ref.shape
    experts = slots // cap
    y = y_ref[...]
    o_ref[step, :toks, :] = (dot(mh_ref[...], y) + dot(ml_ref[...], y)).astype(BF16)
    product = dot(c_ref[0], y, NT)

    @pl.when(step == 0)
    def _():
        acc_ref[...] = product

    @pl.when(step > 0)
    def _():
        acc_ref[...] += product

    @pl.when(step == pl.num_programs(0) - 1)
    def _():
        held = jnp.where(mt_ref[...].astype(F32) > 0.0, acc_ref[...], 0.0)
        low = iota((experts, slots), 0) * cap
        slot = iota((experts, slots), 1)
        spread = jnp.where((slot >= low) & (slot < low + cap), 1.0, 0.0)
        table = dot(spread, held, NT, precision=lax.Precision.HIGHEST)
        expert_id = iota((experts, toks), 0)
        lines = [
            jnp.sum(jnp.where(re_ref[k : k + 1, :] == expert_id, table, 0.0), axis=0, keepdims=True)
            for k in range(re_ref.shape[0])
        ]
        block = jnp.concatenate(lines + [jnp.zeros_like(lines[0])] * 4, axis=0)
        block = jnp.concatenate([block, jnp.zeros_like(block)], axis=1).astype(BF16)
        for c in range(o_ref.shape[0]):
            o_ref[c, toks:, :] = block


def mixed_kernel(x_ref, o_ref, r_ref):
    choose, toks = r_ref.shape
    total = x_ref[0].astype(F32)
    for c in range(1, x_ref.shape[0]):
        total = total + x_ref[c].astype(F32)
    o_ref[...] = total[:toks, :].astype(BF16)
    r_ref[...] = total[toks : toks + choose, :toks]


def weight_kernel(x_ref, o_ref, gi_ref, ui_ref, h_ref, gg_ref, ug_ref, dg_ref):
    x = x_ref[...]
    gg_ref[...] = dot(gi_ref[...], x, TN)
    ug_ref[...] = dot(ui_ref[...], x, TN)
    dg_ref[...] = dot(h_ref[...], o_ref[0], TN)


def step(
    tokens,
    route_expert,
    route_weight,
    gate_weight,
    up_weight,
    down_weight,
    gate_scale,
    up_scale,
    down_scale,
    cotangent,
):
    owners = lax.axis_size("dp")
    parts = lax.axis_size("expert")
    toks, width = tokens.shape
    choose = route_expert.shape[1]
    cap = 2 * toks * choose // owners
    slots = owners * cap
    share = width // parts
    hid = gate_weight.shape[1]
    gw, uw, dw = gate_weight[0], up_weight[0], down_weight[0]
    mine = lax.axis_index("dp").astype(jnp.int32).reshape(1)
    col = lax.axis_index("expert").astype(jnp.int32).reshape(1)
    full = lambda *shape: pl.BlockSpec(shape, lambda *_: (0,) * len(shape))
    sds = jax.ShapeDtypeStruct

    onehot, cot_send = pl.pallas_call(
        functools.partial(route_kernel, cap),
        name="route",
        grid_spec=pltpu.PrefetchScalarGridSpec(
            num_scalar_prefetch=1,
            grid=(1,),
            in_specs=[
                full(choose, toks),
                full(choose, toks),
                full(toks, share),
                pl.BlockSpec((owners, share), lambda i, c: (0, c[0])),
            ],
            out_specs=[full(slots, toks), full(slots, share)],
        ),
        out_shape=[sds((slots, toks), BF16), sds((slots, share), BF16)],
        cost_estimate=cost(2 * slots * toks * share, 2 * slots * share * 2),
    )(col, route_expert.T, route_weight.T, cotangent, down_scale)
    cot_mine = lax.all_to_all(
        cot_send.reshape(owners, cap, share), "dp", split_axis=0, concat_axis=0, tiled=True
    ).reshape(slots, share)
    tok_send = lax.dot_general(onehot, tokens, NN, preferred_element_type=BF16)
    arrived = lax.all_to_all(
        tok_send.reshape(owners, cap, width), "dp", split_axis=0, concat_axis=0, tiled=True
    ).reshape(slots, width)
    out_grad = lax.all_gather(cot_mine, "expert", axis=0, tiled=False)

    combine, high, rest = pl.pallas_call(
        functools.partial(home_kernel, cap),
        name="home",
        in_specs=[full(toks, choose)] * 2,
        out_specs=[full(toks, slots)] * 3,
        grid=(1,),
        out_shape=[sds((toks, slots), BF16)] * 3,
        cost_estimate=cost(6 * slots * toks * owners, 6 * slots * toks),
    )(route_expert, route_weight)

    block = 256
    row_hid = pl.BlockSpec((block, hid), lambda i, *_: (i, 0))
    row_wide = pl.BlockSpec((block, width), lambda i, *_: (i, 0))
    g, u, h, out_rows = pl.pallas_call(
        forward_kernel,
        name="forward",
        grid_spec=pltpu.PrefetchScalarGridSpec(
            num_scalar_prefetch=1,
            grid=(slots // block,),
            in_specs=[row_wide]
            + [full(hid, width)] * 3
            + [full(1, hid)] * 2
            + [full(owners, width)],
            out_specs=[row_hid, row_hid, row_hid, row_wide],
        ),
        out_shape=[
            sds((slots, hid), F32),
            sds((slots, hid), F32),
            sds((slots, hid), BF16),
            sds((slots, width), BF16),
        ],
        cost_estimate=cost(6 * slots * width * hid, 4 * slots * width),
    )(mine, arrived, gw, uw, dw, gate_scale, up_scale, down_scale)
    returned = lax.all_to_all(
        out_rows.reshape(owners, cap, width), "dp", split_axis=0, concat_axis=0, tiled=True
    ).reshape(slots, width)

    block = 128
    row_hid = pl.BlockSpec((block, hid), lambda i: (i, 0))
    row_parts = pl.BlockSpec((parts, block, share), lambda i: (0, i, 0))
    gate_in, up_in, input_part = pl.pallas_call(
        backward_kernel,
        name="backward",
        grid=(slots // block,),
        in_specs=[row_parts] + [row_hid] * 2 + [full(hid, width)] * 3 + [full(1, hid)] * 2,
        out_specs=[row_hid, row_hid, row_parts],
        out_shape=[
            sds((slots, hid), BF16),
            sds((slots, hid), BF16),
            sds((parts, slots, share), BF16),
        ],
        cost_estimate=cost(6 * slots * width * hid, 4 * slots * width),
    )(out_grad, g, u, gw, uw, dw, gate_scale, up_scale)
    input_cols = lax.psum_scatter(
        input_part.reshape(parts * slots, share), "expert", scatter_dimension=0, tiled=True
    )

    col_wide = pl.BlockSpec((slots, share), lambda i: (0, i))
    col_hid = pl.BlockSpec((hid, share), lambda i: (0, i))
    gate_grad, up_grad, down_grad = pl.pallas_call(
        weight_kernel,
        name="weight",
        grid=(parts,),
        in_specs=[col_wide, pl.BlockSpec((1, slots, share), lambda i: (i, 0, 0))]
        + [full(slots, hid)] * 3,
        out_specs=[col_hid] * 3,
        out_shape=[sds((hid, width), F32)] * 3,
        cost_estimate=cost(6 * slots * width * hid, 4 * slots * width + 12 * hid * width),
    )(arrived, out_grad, gate_in, up_in, h)

    raw = [cotangent] + [
        lax.ppermute(cotangent, "expert", [(i, (i + s) % parts) for i in range(parts)])
        for s in range(1, parts)
    ]
    raw = jnp.stack(raw)
    tail = 8
    mixed_part = pl.pallas_call(
        functools.partial(combine_kernel, cap),
        name="combine",
        grid_spec=pltpu.PrefetchScalarGridSpec(
            num_scalar_prefetch=1,
            grid=(parts,),
            in_specs=[
                pl.BlockSpec((slots, share), lambda i, z: (0, i)),
                pl.BlockSpec((1, toks, share), lambda i, z: ((z[0] + parts - i) % parts, 0, 0)),
            ]
            + [full(toks, slots)] * 3
            + [full(choose, toks)],
            out_specs=full(parts, toks + tail, share),
            scratch_shapes=[pltpu.VMEM((toks, slots), F32)],
        ),
        out_shape=sds((parts, toks + tail, share), BF16),
        cost_estimate=cost(6 * slots * toks * width, 2 * slots * width),
    )(col, returned, raw, combine, high, rest, route_expert.T)
    mixed_all = lax.all_to_all(mixed_part, "expert", split_axis=0, concat_axis=0, tiled=True)
    mixed, route_grad = pl.pallas_call(
        mixed_kernel,
        name="mixed",
        grid=(1,),
        in_specs=[full(parts, toks + tail, share)],
        out_specs=[full(toks, share), full(choose, toks)],
        out_shape=[sds((toks, share), BF16), sds((choose, toks), F32)],
        cost_estimate=cost(parts * toks * share, 2 * parts * toks * share),
    )(mixed_all)
    route_grad = route_grad.T
    input_home = lax.all_to_all(
        input_cols.reshape(owners, cap, share), "dp", split_axis=0, concat_axis=0, tiled=True
    ).reshape(slots, share)
    token_grad = dot(combine, input_home).astype(BF16)
    return (mixed, token_grad, route_grad, gate_grad[None], up_grad[None], down_grad[None])


def solution(mesh):
    return jax.shard_map(
        step,
        mesh=mesh,
        in_specs=(
            P("dp", None),
            P("dp", None),
            P("dp", None),
            P("dp", "expert", None),
            P("dp", "expert", None),
            P("dp", "expert", None),
            P("dp", "expert"),
            P("dp", "expert"),
            P(),
            P("dp", "expert"),
        ),
        out_specs=(
            P("dp", "expert"),
            P("dp", "expert"),
            P("dp", None),
            P("dp", "expert", None),
            P("dp", "expert", None),
            P("dp", "expert", None),
        ),
        check_vma=False,
    )
```

time: 437 us -> 231 us (0.53)
  waiting for transfers between devices: 257 us -> 80.7 us
  Pallas kernels: 0 us -> 44.8 us
  matrix products: 35.5 us -> 5.05 us
  local copies, waits for them, and re-layouts: 27.5 us -> 1.56 us
  other arithmetic: 13.6 us -> 0 us
  blocking collectives: 58 us -> 44.6 us
  starting transfers between devices: 30.3 us -> 37.5 us
    reduce_scatter x2 -> x1, waiting for transfers between devices: 172 us -> 0.01 us  [step(): lax.psum_scatter(input_part.reshape(parts * slots, share), 'expert', scat...]
    pallas_call x0 -> x7, Pallas kernels: none -> 44.8 us  [the longest x1 12.3 us: step(): pl.pallas_call(backward_kernel, name='backward', grid=(slots // block,),...]
    all_to_all x0 -> x2, blocking collectives: none -> 44.6 us  [the longest x1 26.5 us: step(): lax.all_to_all(mixed_part, 'expert', split_axis=0, concat_axis=0, tiled=T...]
    dot_general x9 -> x2, matrix products: 35.5 us -> 5.05 us  [the longest x1 4.18 us: step(): tok_send = lax.dot_general(onehot, tokens, NN, preferred_element_type=BF16)]
    all_gather x1 -> x0, blocking collectives: 29.3 us -> none  [local(): full_cot = lax.all_gather(cotangent, 'expert', axis=1, tiled=True)]
    psum x1 -> x0, blocking collectives: 28.7 us -> none  [local(): route_grad = lax.psum(route_part, 'expert')]
    ppermute x0 -> x7, starting transfers between devices: none -> 18.5 us  [step(): lax.ppermute(cotangent, 'expert', [(i, (i + s) % parts) for i in range(pa...]
    gather x6 -> x0, local copies, waits for them, and re-layouts: 15.8 us -> none  [the longest x1 6.03 us: local(): cot_slots = jnp.take(full_cot, slot_token, axis=0).astype(jnp.float32)]
  transfers between devices with their start and end apart: 6 -> 12, of which waited for: 4 -> 6; matrix products, arithmetic and copies ran while one was open for 9% -> 2% of each run, Pallas kernels for 0% -> 13%
where the time goes in v1:
time: 231 us; the launch traced here: 228 us
  waiting for transfers between devices  80.7 us (35%)
  Pallas kernels  44.8 us (19%)
  blocking collectives  44.6 us (19%)
  starting transfers between devices  37.5 us (16%)
  between operations  14.2 us (6%)
  matrix products  5.05 us (2%)
    all_to_all x1, waiting for transfers between devices, step(): lax.all_to_all(tok_send.reshape(owners, cap, width), 'dp', split_axis=0,...  51.5 us
    all_to_all x1, blocking collectives, step(): lax.all_to_all(mixed_part, 'expert', split_axis=0, concat_axis=0, tiled=T...  26.5 us
    all_to_all x1, waiting for transfers between devices, step(): lax.all_to_all(out_rows.reshape(owners, cap, width), 'dp', split_axis=0,...  21.7 us
    ppermute x7, starting transfers between devices, step(): lax.ppermute(cotangent, 'expert', [(i, (i + s) % parts) for i in range(pa...  18.5 us
    all_to_all x1, blocking collectives, step(): lax.all_to_all(cot_send.reshape(owners, cap, share), 'dp', split_axis=0,...  18.1 us
    pallas_call x1, Pallas kernels, step(): pl.pallas_call(backward_kernel, name='backward', grid=(slots // block,),...  12.3 us
    pallas_call x1, Pallas kernels, step(): pl.pallas_call(weight_kernel, name='weight', grid=(parts,), in_specs=[col...  9.78 us
    pallas_call x1, Pallas kernels, step(): pl.pallas_call(functools.partial(combine_kernel, cap), name='combine', gr...  8.6 us
  transfers between devices with their start and end apart: 12, of which 6 were waited for; matrix products, arithmetic and copies ran while one was open for 2% of the time, Pallas kernels for 13%

profile of v1, /device:TPU:2, one launch (start us, length us, event | category | flops | bytes accessed | tf_op | source)
XLA Modules:
  0.0 228.3 jit_solution(3576283246856777346)
XLA Ops:
  7.2 0.0 copy-start
  7.2 0.0 all-gather.2.cloned.1.call-start
  7.2 2.2 route.1
  9.4 18.1 %all_to_all.25 = bf16[32,32,256]{2,1,0:T(8,128)(2,1)} all-to-all(bf16[32,32,256]{2,1,0:T(8,128)(2,1)} %bitcast.52), channel_id=1, replica_groups=mesh['dp'=32,'expert'=8] {'dp'}, dimensions={0} | all-to-all | bytes 1048576 | tf_op jit(solution)/shard_map/all_to_all | solution.py:213
  27.5 0.0 all-gather.2.cloned.1.call-update
  27.5 0.0 copy-done
  27.5 4.2 %fusion = bf16[1024,2048]{1,0:T(8,128)(2,1)} fusion(bf16[1024,128]{1,0:T(8,128)(2,1)} %get-tuple-element.23, bf16[128,2048]{1,0:T(8,128)(2,1)S(1)} %copy-done), kind=kOutput, calls=%fused_computation.9 | convolution fusion | flops 536870912 | bytes 4980736 | tf_op jit(solution)/shard_map/dot_general | solution.py:216
  31.7 5.9 %all-to-all-start = ((bf16[32,32,2048]{2,1,0:T(8,128)(2,1)}), bf16[32,32,2048]{2,1,0:T(8,128)(2,1)}, u32[]{:S(2)}, u32[]{:S(2)}) async-start(bf16[32,32,2048]{2,1,0:T(8,128)(2,1)} %bitcast.40), calls=%async_computation | async-start | bytes 8388608 | tf_op jit(solution)/shard_map/all_to_all | solution.py:217
  37.6 0.0 reduce-scatter.2.cloned.1.call-start
  37.7 51.5 %all-to-all-done = bf16[32,32,2048]{2,1,0:T(8,128)(2,1)} async-done(((bf16[32,32,2048]{2,1,0:T(8,128)(2,1)}), bf16[32,32,2048]{2,1,0:T(8,128)(2,1)}, u32[]{:S(2)}, u32[]{:S(2)}) %all-to-all-start) | async-done | bytes 4194336 | tf_op jit(solution)/shard_map/all_to_all | solution.py:217
  89.1 8.0 %forward.1 = (f32[1024,176]{1,0:T(8,128)}, f32[1024,176]{1,0:T(8,128)}, bf16[1024,176]{1,0:T(8,128)(2,1)}, bf16[1024,2048]{1,0:T(8,128)(2,1)}) custom-call(s32[1]{0:T(128)} %bitcast.1.e_ref, bf16[1024,2048]{1,0:T(8,128)(2,1)} %bitcast.5.x_ref, bf16[176,2048]{1,0:T(8,128)(2,1)} %bitcast.45, bf16[176,2048]{1,0:T(8,128)(2,1)} %bitcast.47, ...), custom_call_target="tpu_custom_call" | custom-call | flops 2214592512 | bytes 8388608 | tf_op jit(solution)/shard_map/forward/pallas_call | solution.py:235
  97.1 12.3 %backward.1 = (bf16[1024,176]{1,0:T(8,128)(2,1)}, bf16[1024,176]{1,0:T(8,128)(2,1)}, bf16[8,1024,256]{2,1,0:T(8,128)(2,1)}) custom-call(bf16[8,1024,256]{2,1,0:T(8,128)(2,1)} %all-gather.2.cloned.1.call-done.o_ref, f32[1024,176]{1,0:T(8,128)} %get-tuple-element.30.g_ref, f32[1024,176]{1,0:T(8,128)} %get-tuple-element.31.u_ref, bf16[176,2048]{1,0:T(8,128)(2,1)} %bitcast.46, ...), custom_call_target="tpu_custom_call" | custom-call | flops 2214592512 | bytes 8388608 | tf_op jit(solution)/shard_map/backward/pallas_call | solution.py:262
  109.4 0.0 reduce-scatter.2.cloned.1.call-update
  109.4 0.0 copy-start.3
  109.4 0.0 copy-start.4
  109.4 0.0 copy-start.5
  109.4 7.4 %all-to-all-start.1 = ((bf16[32,32,2048]{2,1,0:T(8,128)(2,1)}), bf16[32,32,2048]{2,1,0:T(8,128)(2,1)}, u32[]{:S(2)}, u32[]{:S(2)}) async-start(bf16[32,32,2048]{2,1,0:T(8,128)(2,1)} %bitcast.42), calls=%async_computation.1 | async-start | bytes 8388608 | tf_op jit(solution)/shard_map/all_to_all | solution.py:255
  116.9 0.0 copy-done.3
  116.9 2.0 collective-permute-start
  118.9 3.3 %collective-permute-start.1 = (bf16[128,256]{1,0:T(8,128)(2,1)S(1)}, bf16[128,256]{1,0:T(8,128)(2,1)S(1)}, u32[]{:S(2)}, u32[]{:S(2)}) collective-permute-start(bf16[128,256]{1,0:T(8,128)(2,1)S(1)} %copy-done.3), channel_id=1, source_target_pairs={{0,2},{1,3},{2,4},{3,5},{4,6},{5,7},{6,0},{7,1},{8,10},{9,11},{10,... | collective-permute-start | bytes 196616 | tf_op jit(solution)/shard_map/ppermute | solution.py:293
  122.2 4.0 %collective-permute-start.2 = (bf16[128,256]{1,0:T(8,128)(2,1)S(1)}, bf16[128,256]{1,0:T(8,128)(2,1)S(1)}, u32[]{:S(2)}, u32[]{:S(2)}) collective-permute-start(bf16[128,256]{1,0:T(8,128)(2,1)S(1)} %copy-done.3), channel_id=1, source_target_pairs={{0,3},{1,4},{2,5},{3,6},{4,7},{5,0},{6,1},{7,2},{8,11},{9,12},{10,... | collective-permute-start | bytes 196616 | tf_op jit(solution)/shard_map/ppermute | solution.py:293
  126.2 0.5 collective-permute-start.3
  126.7 4.9 %collective-permute-start.4 = (bf16[128,256]{1,0:T(8,128)(2,1)S(1)}, bf16[128,256]{1,0:T(8,128)(2,1)S(1)}, u32[]{:S(2)}, u32[]{:S(2)}) collective-permute-start(bf16[128,256]{1,0:T(8,128)(2,1)S(1)} %copy-done.3), channel_id=1, source_target_pairs={{0,5},{1,6},{2,7},{3,0},{4,1},{5,2},{6,3},{7,4},{8,13},{9,14},{10,... | collective-permute-start | bytes 196616 | tf_op jit(solution)/shard_map/ppermute | solution.py:293
  131.7 0.0 copy-done.4
  131.7 0.7 copy.18.re_ref
  132.4 0.0 copy-done.5
  132.4 0.7 copy.19.rw_ref
  133.2 2.3 home.1
  135.5 0.0 collective-permute-done
  135.5 2.7 %collective-permute-start.5 = (bf16[128,256]{1,0:T(8,128)(2,1)S(1)}, bf16[128,256]{1,0:T(8,128)(2,1)S(1)}, u32[]{:S(2)}, u32[]{:S(2)}) collective-permute-start(bf16[128,256]{1,0:T(8,128)(2,1)S(1)} %copy-done.3), channel_id=1, source_target_pairs={{0,6},{1,7},{2,0},{3,1},{4,2},{5,3},{6,4},{7,5},{8,14},{9,15},{10,... | collective-permute-start | bytes 196616 | tf_op jit(solution)/shard_map/ppermute | solution.py:293
  138.1 0.0 collective-permute-done.1
  138.1 1.1 collective-permute-start.6
  139.2 0.0 collective-permute-done.2
  139.2 0.6 collective-permute-done.3
  139.8 3.5 %collective-permute-done.4 = bf16[128,256]{1,0:T(8,128)(2,1)S(1)} collective-permute-done((bf16[128,256]{1,0:T(8,128)(2,1)S(1)}, bf16[128,256]{1,0:T(8,128)(2,1)S(1)}, u32[]{:S(2)}, u32[]{:S(2)}) %collective-permute-start.4) | collective-permute-done | bytes 65568 | tf_op jit(solution)/shard_map/ppermute | solution.py:293
  143.4 1.2 collective-permute-done.5
  144.6 2.1 collective-permute-done.6
  146.7 21.7 %all-to-all-done.1 = bf16[32,32,2048]{2,1,0:T(8,128)(2,1)} async-done(((bf16[32,32,2048]{2,1,0:T(8,128)(2,1)}), bf16[32,32,2048]{2,1,0:T(8,128)(2,1)}, u32[]{:S(2)}, u32[]{:S(2)}) %all-to-all-start.1) | async-done | bytes 4194336 | tf_op jit(solution)/shard_map/all_to_all | solution.py:255
  168.4 0.0 copy-done.2
  168.4 8.6 %combine.1 = bf16[8,136,256]{2,1,0:T(8,128)(2,1)} custom-call(s32[1]{0:T(128)} %bitcast.col_ref.z_ref, bf16[1024,2048]{1,0:T(8,128)(2,1)} %bitcast.10.y_ref, bf16[8,128,256]{2,1,0:T(8,128)(2,1)} %copy-done.2, bf16[128,1024]{1,0:T(8,128)(2,1)} %get-tuple-element.25.mt_ref, bf16[128,1024]{1,0:T(8,128)(2,1)} %get-tuple-element.26.mh_ref, ...), custom_call_target="tpu_custom_call" | custom-call | flops 1610612736 | bytes 4194304 | tf_op jit(solution)/shard_map/combine/pallas_call | solution.py:298
  177.0 26.5 %all_to_all.26.x_ref = bf16[8,136,256]{2,1,0:T(8,128)(2,1)} all-to-all(bf16[8,136,256]{2,1,0:T(8,128)(2,1)} %combine.1), channel_id=1, replica_groups=mesh['dp'=32,'expert'=8] {'expert'}, dimensions={0} | all-to-all | bytes 1114112 | tf_op jit(solution)/shard_map/all_to_all | solution.py:316
  203.5 5.6 %all-to-all-start.4 = ((bf16[32,32,256]{2,1,0:T(8,128)(2,1)}), bf16[32,32,256]{2,1,0:T(8,128)(2,1)S(1)}, u32[]{:S(2)}, u32[]{:S(2)}) async-start(bf16[32,32,256]{2,1,0:T(8,128)(2,1)} %bitcast.51), calls=%async_computation.5 | async-start | bytes 1048576 | tf_op jit(solution)/shard_map/all_to_all | solution.py:327
  209.1 0.0 copy-start.1
  209.1 9.8 %weight.1 = (f32[176,2048]{1,0:T(8,128)}, f32[176,2048]{1,0:T(8,128)}, f32[176,2048]{1,0:T(8,128)}) custom-call(bf16[1024,2048]{1,0:T(8,128)(2,1)} %bitcast.5.x_ref, bf16[8,1024,256]{2,1,0:T(8,128)(2,1)} %all-gather.2.cloned.1.call-done.o_ref, bf16[1024,176]{1,0:T(8,128)(2,1)} %get-tuple-element.34.gi_ref, bf16[1024,176]{1,0:T(8,128)(2,1)} %get-tuple-element.35.ui_ref, ...), custom_call_target="tpu_custom_call" | custom-call | flops 2214592512 | bytes 12713984 | tf_op jit(solution)/shard_map/weight/pallas_call | solution.py:281
  218.9 1.8 mixed.1
  220.6 0.0 all-to-all-done.4
  220.6 0.0 copy-done.1
  220.6 0.9 convolution_convert_fusion
  (11 shorter events, 0.0 us)
Async XLA Ops:
  7.2 20.4 %copy-start = (bf16[128,2048]{1,0:T(8,128)(2,1)S(1)}, bf16[128,2048]{1,0:T(8,128)(2,1)}, u32[]{:S(2)}) copy-start(bf16[128,2048]{1,0:T(8,128)(2,1)} %param.10) | copy-start | bytes 1572868
  7.2 89.9 %all-gather.2.cloned.1.call-start = ((), (), s32[]{:S(2)}) async-start(), calls=%async_computation.6 | async-start | bytes 4718592 | tf_op jit(solution)/shard_map/all_gather | solution.py:220
  31.7 57.4 %all-to-all-start = ((bf16[32,32,2048]{2,1,0:T(8,128)(2,1)}), bf16[32,32,2048]{2,1,0:T(8,128)(2,1)}, u32[]{:S(2)}, u32[]{:S(2)}) async-start(bf16[32,32,2048]{2,1,0:T(8,128)(2,1)} %bitcast.40), calls=%async_computation | async-start | bytes 8388608 | tf_op jit(solution)/shard_map/all_to_all | solution.py:217
  37.6 165.9 %reduce-scatter.2.cloned.1.call-start = ((), (), s32[]{:S(2)}) async-start(), calls=%async_computation.7 | async-start | bytes 4718592 | tf_op jit(solution)/shard_map/reduce_scatter | solution.py:275
  109.4 7.5 %copy-start.3 = (bf16[128,256]{1,0:T(8,128)(2,1)S(1)}, bf16[128,256]{1,0:T(8,128)(2,1)}, u32[]{:S(2)}) copy-start(bf16[128,256]{1,0:T(8,128)(2,1)} %cot_ref.1) | copy-start | bytes 196612
  109.4 22.3 %copy-start.4 = (s32[128,4]{0,1:T(4,128)S(1)}, s32[128,4]{0,1:T(4,128)}, u32[]{:S(2)}) copy-start(s32[128,4]{0,1:T(4,128)} %param.11) | copy-start | bytes 6148
  109.4 23.0 %copy-start.5 = (f32[128,4]{0,1:T(4,128)S(1)}, f32[128,4]{0,1:T(4,128)}, u32[]{:S(2)}) copy-start(f32[128,4]{0,1:T(4,128)} %param.12) | copy-start | bytes 6148
  109.4 59.0 %all-to-all-start.1 = ((bf16[32,32,2048]{2,1,0:T(8,128)(2,1)}), bf16[32,32,2048]{2,1,0:T(8,128)(2,1)}, u32[]{:S(2)}, u32[]{:S(2)}) async-start(bf16[32,32,2048]{2,1,0:T(8,128)(2,1)} %bitcast.42), calls=%async_computation.1 | async-start | bytes 8388608 | tf_op jit(solution)/shard_map/all_to_all | solution.py:255
  116.9 18.6 %collective-permute-start = (bf16[128,256]{1,0:T(8,128)(2,1)S(1)}, bf16[128,256]{1,0:T(8,128)(2,1)S(1)}, u32[]{:S(2)}, u32[]{:S(2)}) collective-permute-start(bf16[128,256]{1,0:T(8,128)(2,1)S(1)} %copy-done.3), channel_id=1, source_target_pairs={{0,1},{1,2},{2,3},{3,4},{4,5},{5,6},{6,7},{7,0},{8,9},{9,10},{10,1... | collective-permute-start | bytes 196616 | tf_op jit(solution)/shard_map/ppermute | solution.py:293
  118.9 19.2 %collective-permute-start.1 = (bf16[128,256]{1,0:T(8,128)(2,1)S(1)}, bf16[128,256]{1,0:T(8,128)(2,1)S(1)}, u32[]{:S(2)}, u32[]{:S(2)}) collective-permute-start(bf16[128,256]{1,0:T(8,128)(2,1)S(1)} %copy-done.3), channel_id=1, source_target_pairs={{0,2},{1,3},{2,4},{3,5},{4,6},{5,7},{6,0},{7,1},{8,10},{9,11},{10,... | collective-permute-start | bytes 196616 | tf_op jit(solution)/shard_map/ppermute | solution.py:293
  122.2 17.1 %collective-permute-start.2 = (bf16[128,256]{1,0:T(8,128)(2,1)S(1)}, bf16[128,256]{1,0:T(8,128)(2,1)S(1)}, u32[]{:S(2)}, u32[]{:S(2)}) collective-permute-start(bf16[128,256]{1,0:T(8,128)(2,1)S(1)} %copy-done.3), channel_id=1, source_target_pairs={{0,3},{1,4},{2,5},{3,6},{4,7},{5,0},{6,1},{7,2},{8,11},{9,12},{10,... | collective-permute-start | bytes 196616 | tf_op jit(solution)/shard_map/ppermute | solution.py:293
  126.2 13.6 %collective-permute-start.3 = (bf16[128,256]{1,0:T(8,128)(2,1)S(1)}, bf16[128,256]{1,0:T(8,128)(2,1)S(1)}, u32[]{:S(2)}, u32[]{:S(2)}) collective-permute-start(bf16[128,256]{1,0:T(8,128)(2,1)S(1)} %copy-done.3), channel_id=1, source_target_pairs={{0,4},{1,5},{2,6},{3,7},{4,0},{5,1},{6,2},{7,3},{8,12},{9,13},{10,... | collective-permute-start | bytes 196616 | tf_op jit(solution)/shard_map/ppermute | solution.py:293
  126.7 16.6 %collective-permute-start.4 = (bf16[128,256]{1,0:T(8,128)(2,1)S(1)}, bf16[128,256]{1,0:T(8,128)(2,1)S(1)}, u32[]{:S(2)}, u32[]{:S(2)}) collective-permute-start(bf16[128,256]{1,0:T(8,128)(2,1)S(1)} %copy-done.3), channel_id=1, source_target_pairs={{0,5},{1,6},{2,7},{3,0},{4,1},{5,2},{6,3},{7,4},{8,13},{9,14},{10,... | collective-permute-start | bytes 196616 | tf_op jit(solution)/shard_map/ppermute | solution.py:293
  135.5 9.1 %collective-permute-start.5 = (bf16[128,256]{1,0:T(8,128)(2,1)S(1)}, bf16[128,256]{1,0:T(8,128)(2,1)S(1)}, u32[]{:S(2)}, u32[]{:S(2)}) collective-permute-start(bf16[128,256]{1,0:T(8,128)(2,1)S(1)} %copy-done.3), channel_id=1, source_target_pairs={{0,6},{1,7},{2,0},{3,1},{4,2},{5,3},{6,4},{7,5},{8,14},{9,15},{10,... | collective-permute-start | bytes 196616 | tf_op jit(solution)/shard_map/ppermute | solution.py:293
  138.1 8.5 %collective-permute-start.6 = (bf16[128,256]{1,0:T(8,128)(2,1)S(1)}, bf16[128,256]{1,0:T(8,128)(2,1)S(1)}, u32[]{:S(2)}, u32[]{:S(2)}) collective-permute-start(bf16[128,256]{1,0:T(8,128)(2,1)S(1)} %copy-done.3), channel_id=1, source_target_pairs={{0,7},{1,0},{2,1},{3,2},{4,3},{5,4},{6,5},{7,6},{8,15},{9,8},{10,9... | collective-permute-start | bytes 196616 | tf_op jit(solution)/shard_map/ppermute | solution.py:293
  146.7 21.7 %copy-start.2 = (bf16[8,128,256]{2,1,0:T(8,128)(2,1)}, bf16[8,128,256]{2,1,0:T(8,128)(2,1)S(1)}, u32[]{:S(2)}) copy-start(bf16[8,128,256]{2,1,0:T(8,128)(2,1)S(1)} %bitcast_dynamic-update-slice_fusion.c_ref) | copy-start | bytes 1572868
  203.5 17.1 %all-to-all-start.4 = ((bf16[32,32,256]{2,1,0:T(8,128)(2,1)}), bf16[32,32,256]{2,1,0:T(8,128)(2,1)S(1)}, u32[]{:S(2)}, u32[]{:S(2)}) async-start(bf16[32,32,256]{2,1,0:T(8,128)(2,1)} %bitcast.51), calls=%async_computation.5 | async-start | bytes 1048576 | tf_op jit(solution)/shard_map/all_to_all | solution.py:327
  209.1 11.6 %copy-start.1 = (bf16[128,1024]{1,0:T(8,128)(2,1)S(1)}, bf16[128,1024]{1,0:T(8,128)(2,1)}, u32[]{:S(2)}) copy-start(bf16[128,1024]{1,0:T(8,128)(2,1)} %get-tuple-element.25.mt_ref) | copy-start | bytes 786436
Sparse Core Ops, SparseCore 0:
  27.6 54.9 all-gather.1
  109.5 65.9 reduce-scatter.1

commit v2 on v1

--- a/solution.py
+++ b/solution.py
@@ -98,13 +98,18 @@
     y_ref[...] = (dot(h, dw_ref[...]) * scale).astype(BF16)
 
 
-def backward_kernel(
-    o_ref, g_ref, u_ref, gw_ref, uw_ref, dw_ref, gs_ref, us_ref, gi_ref, ui_ref, p_ref
-):
-    parts, _, share = o_ref.shape
-    hg = dot(o_ref[0], dw_ref[:, :share], NT)
+def backward_kernel(parts, z_ref, *refs):
+    o_refs = refs[:parts]
+    g_ref, u_ref, gw_ref, uw_ref, dw_ref, gs_ref, us_ref, gi_ref, ui_ref, p_ref = refs[parts:]
+    share = p_ref.shape[2]
+
+    def cols(c):
+        at = lax.rem(z_ref[0] + c, parts)
+        return pl.ds(pl.multiple_of(at * share, share), share)
+
+    hg = dot(o_refs[0][...], dw_ref[:, cols(0)], NT)
     for c in range(1, parts):
-        hg = hg + dot(o_ref[c], dw_ref[:, c * share : (c + 1) * share], NT)
+        hg = hg + dot(o_refs[c][...], dw_ref[:, cols(parts - c)], NT)
     g = g_ref[...]
     u = u_ref[...]
     s = jax.nn.sigmoid(g)
@@ -113,8 +118,7 @@
     gi_ref[...] = gi
     ui_ref[...] = ui
     for c in range(parts):
-        cols = slice(c * share, (c + 1) * share)
-        p_ref[c] = (dot(gi, gw_ref[:, cols]) + dot(ui, uw_ref[:, cols])).astype(BF16)
+        p_ref[c] = (dot(gi, gw_ref[:, cols(c)]) + dot(ui, uw_ref[:, cols(c)])).astype(BF16)
 
 
 def combine_kernel(cap, z_ref, y_ref, c_ref, mt_ref, mh_ref, ml_ref, re_ref, o_ref, acc_ref):
@@ -122,8 +126,10 @@
     toks, slots = mt_ref.shape
     experts = slots // cap
     y = y_ref[...]
-    o_ref[step, :toks, :] = (dot(mh_ref[...], y) + dot(ml_ref[...], y)).astype(BF16)
-    product = dot(c_ref[0], y, NT)
+    parts = o_ref.shape[0]
+    at = lax.rem(z_ref[0] + parts - step, parts)
+    o_ref[at, :toks, :] = (dot(mh_ref[...], y) + dot(ml_ref[...], y)).astype(BF16)
+    product = dot(c_ref[...].reshape(toks, y.shape[1]), y, NT)
 
     @pl.when(step == 0)
     def _():
@@ -160,11 +166,62 @@
     r_ref[...] = total[toks : toks + choose, :toks]
 
 
-def weight_kernel(x_ref, o_ref, gi_ref, ui_ref, h_ref, gg_ref, ug_ref, dg_ref):
+def weight_kernel(x_ref, *refs):
+    gi_refs, ui_refs, gg_ref, ug_ref = refs[:2], refs[2:4], refs[4], refs[5]
     x = x_ref[...]
-    gg_ref[...] = dot(gi_ref[...], x, TN)
-    ug_ref[...] = dot(ui_ref[...], x, TN)
-    dg_ref[...] = dot(h_ref[...], o_ref[0], TN)
+    gg_ref[...] = dot(jnp.concatenate([r[...] for r in gi_refs], axis=0), x, TN)
+    ug_ref[...] = dot(jnp.concatenate([r[...] for r in ui_refs], axis=0), x, TN)
+
+
+def down_kernel(parts, z_ref, h_ref, *refs):
+    dg_ref = refs[-1]
+    share = refs[0].shape[1]
+    rows = h_ref.shape[0] // 2
+    h = h_ref[...]
+    for c in range(parts):
+        o = jnp.concatenate([refs[c][:rows, :], refs[parts + c][:rows, :]], axis=0)
+        at = lax.rem(z_ref[0] + (parts - c), parts)
+        dg_ref[:, pl.ds(pl.multiple_of(at * share, share), share)] = dot(h, o, TN)
+
+
+def shift(x, by):
+    size = lax.axis_size("expert")
+    return lax.ppermute(x, "expert", [(i, (i + by) % size) for i in range(size)])
+
+
+def ring_gather(first, second):
+    size = lax.axis_size("expert")
+    half = size // 2
+    pieces = [[None] * size, [None] * size]
+    for j, (x, ups) in enumerate(((first, half), (second, half - 1))):
+        pieces[j][0] = x
+        up = down = x
+        for k in range(1, half + 1):
+            if k <= ups:
+                up = shift(up, 1)
+                pieces[j][k] = up
+            if k <= size - 1 - ups:
+                down = shift(down, -1)
+                pieces[j][size - k] = down
+    return pieces
+
+
+def add(*terms):
+    return sum(t.astype(F32) for t in terms).astype(BF16)
+
+
+def ring_scatter(halves):
+    sums = []
+    for parts, ups in zip(halves, (4, 3)):
+        size = parts.shape[0]
+        up = shift(parts[ups], 1)
+        down = shift(parts[ups + 1], -1)
+        for k in range(ups - 1, 0, -1):
+            up = shift(add(up, parts[k]), 1)
+        for k in range(ups + 2, size):
+            down = shift(add(down, parts[k]), -1)
+        sums.append(add(up, down, parts[0]))
+    return jnp.concatenate(sums, axis=0)
 
 
 def step(
@@ -217,7 +274,11 @@
     arrived = lax.all_to_all(
         tok_send.reshape(owners, cap, width), "dp", split_axis=0, concat_axis=0, tiled=True
     ).reshape(slots, width)
-    out_grad = lax.all_gather(cot_mine, "expert", axis=0, tiled=False)
+    rows, raw = slots // 2, toks // 2
+    out_grad = ring_gather(
+        jnp.concatenate([cot_mine[:rows], cotangent[:raw]], axis=0),
+        jnp.concatenate([cot_mine[rows:], cotangent[raw:]], axis=0),
+    )
 
     combine, high, rest = pl.pallas_call(
         functools.partial(home_kernel, cap),
@@ -256,44 +317,64 @@
         out_rows.reshape(owners, cap, width), "dp", split_axis=0, concat_axis=0, tiled=True
     ).reshape(slots, width)
 
-    block = 128
-    row_hid = pl.BlockSpec((block, hid), lambda i: (i, 0))
-    row_parts = pl.BlockSpec((parts, block, share), lambda i: (0, i, 0))
-    gate_in, up_in, input_part = pl.pallas_call(
-        backward_kernel,
-        name="backward",
-        grid=(slots // block,),
-        in_specs=[row_parts] + [row_hid] * 2 + [full(hid, width)] * 3 + [full(1, hid)] * 2,
-        out_specs=[row_hid, row_hid, row_parts],
-        out_shape=[
-            sds((slots, hid), BF16),
-            sds((slots, hid), BF16),
-            sds((parts, slots, share), BF16),
-        ],
-        cost_estimate=cost(6 * slots * width * hid, 4 * slots * width),
-    )(out_grad, g, u, gw, uw, dw, gate_scale, up_scale)
-    input_cols = lax.psum_scatter(
-        input_part.reshape(parts * slots, share), "expert", scatter_dimension=0, tiled=True
-    )
-
-    col_wide = pl.BlockSpec((slots, share), lambda i: (0, i))
+    block = 256
+    per = rows // block
+    halves = []
+    for j in range(2):
+        row_in = pl.BlockSpec((block, hid), lambda i, z, j=j: (i + j * per, 0))
+        row_out = pl.BlockSpec((block, hid), lambda i, z: (i, 0))
+        halves.append(
+            pl.pallas_call(
+                functools.partial(backward_kernel, parts),
+                name="backward",
+                grid_spec=pltpu.PrefetchScalarGridSpec(
+                    num_scalar_prefetch=1,
+                    grid=(per,),
+                    in_specs=[pl.BlockSpec((block, share), lambda i, z: (i, 0))] * parts
+                    + [row_in] * 2
+                    + [full(hid, width)] * 3
+                    + [full(1, hid)] * 2,
+                    out_specs=[
+                        row_out,
+                        row_out,
+                        pl.BlockSpec((parts, block, share), lambda i, z: (0, i, 0)),
+                    ],
+                ),
+                out_shape=[
+                    sds((rows, hid), BF16),
+                    sds((rows, hid), BF16),
+                    sds((parts, rows, share), BF16),
+                ],
+                cost_estimate=cost(3 * slots * width * hid, 2 * slots * width),
+            )(col, *out_grad[j], g, u, gw, uw, dw, gate_scale, up_scale)
+        )
+    input_cols = ring_scatter([half[2] for half in halves])
+
     col_hid = pl.BlockSpec((hid, share), lambda i: (0, i))
-    gate_grad, up_grad, down_grad = pl.pallas_call(
+    gate_grad, up_grad = pl.pallas_call(
         weight_kernel,
         name="weight",
         grid=(parts,),
-        in_specs=[col_wide, pl.BlockSpec((1, slots, share), lambda i: (i, 0, 0))]
-        + [full(slots, hid)] * 3,
-        out_specs=[col_hid] * 3,
-        out_shape=[sds((hid, width), F32)] * 3,
-        cost_estimate=cost(6 * slots * width * hid, 4 * slots * width + 12 * hid * width),
-    )(arrived, out_grad, gate_in, up_in, h)
-
-    raw = [cotangent] + [
-        lax.ppermute(cotangent, "expert", [(i, (i + s) % parts) for i in range(parts)])
-        for s in range(1, parts)
-    ]
-    raw = jnp.stack(raw)
+        in_specs=[pl.BlockSpec((slots, share), lambda i: (0, i))] + [full(rows, hid)] * 4,
+        out_specs=[col_hid] * 2,
+        out_shape=[sds((hid, width), F32)] * 2,
+        cost_estimate=cost(4 * slots * width * hid, 2 * slots * width + 8 * hid * width),
+    )(arrived, halves[0][0], halves[1][0], halves[0][1], halves[1][1])
+    down_grad = pl.pallas_call(
+        functools.partial(down_kernel, parts),
+        name="down",
+        grid_spec=pltpu.PrefetchScalarGridSpec(
+            num_scalar_prefetch=1,
+            grid=(1,),
+            in_specs=[full(slots, hid)] + [full(rows + raw, share)] * (2 * parts),
+            out_specs=full(hid, width),
+        ),
+        out_shape=sds((hid, width), F32),
+        cost_estimate=cost(2 * slots * width * hid, 2 * slots * width + 4 * hid * width),
+    )(col, h, *out_grad[0], *out_grad[1])
+
+    raw_all = jnp.stack([o[rows:] for pair in zip(*out_grad) for o in pair])
+    raw_all = raw_all.reshape(parts, 2, raw, share)
     tail = 8
     mixed_part = pl.pallas_call(
         functools.partial(combine_kernel, cap),
@@ -302,8 +383,8 @@
             num_scalar_prefetch=1,
             grid=(parts,),
             in_specs=[
-                pl.BlockSpec((slots, share), lambda i, z: (0, i)),
-                pl.BlockSpec((1, toks, share), lambda i, z: ((z[0] + parts - i) % parts, 0, 0)),
+                pl.BlockSpec((slots, share), lambda i, z: (0, lax.rem(z[0] + parts - i, parts))),
+                pl.BlockSpec((None, 2, raw, share), lambda i, z: (i, 0, 0, 0)),
             ]
             + [full(toks, slots)] * 3
             + [full(choose, toks)],
@@ -312,7 +393,7 @@
         ),
         out_shape=sds((parts, toks + tail, share), BF16),
         cost_estimate=cost(6 * slots * toks * width, 2 * slots * width),
-    )(col, returned, raw, combine, high, rest, route_expert.T)
+    )(col, returned, raw_all, combine, high, rest, route_expert.T)
     mixed_all = lax.all_to_all(mixed_part, "expert", split_axis=0, concat_axis=0, tiled=True)
     mixed, route_grad = pl.pallas_call(
         mixed_kernel,

time: 231 us -> 209 us (0.905)
  starting transfers between devices: 37.5 us -> 83.5 us
  blocking collectives: 44.6 us -> 0 us
  waiting for transfers between devices: 80.7 us -> 44.4 us
  local copies, waits for them, and re-layouts: 1.56 us -> 21.2 us
  between operations: 14.2 us -> 0.99 us
  Pallas kernels: 44.8 us -> 48.7 us
  other arithmetic: 0 us -> 2.66 us
    all_to_all x1, waiting for transfers between devices: 51.5 us -> 4.68 us  [step(): lax.all_to_all(tok_send.reshape(owners, cap, width), 'dp', split_axis=0,...]
    all_to_all x2 -> x0, blocking collectives: 44.6 us -> none  [the longest x1 26.5 us: step(): lax.all_to_all(mixed_part, 'expert', split_axis=0, concat_axis=0, tiled=T...]
    ppermute x7 -> x28, starting transfers between devices: 18.5 us -> 50.7 us  [shift(): lax.ppermute(x, 'expert', [(i, (i + by) % size) for i in range(size)])]
    all_to_all x1, waiting for transfers between devices: 21.7 us -> 0.01 us  [step(): lax.all_to_all(out_rows.reshape(owners, cap, width), 'dp', split_axis=0,...]
    ppermute x7 -> x28, waiting for transfers between devices: 7.42 us -> 28.9 us  [shift(): lax.ppermute(x, 'expert', [(i, (i + by) % size) for i in range(size)])]
    unnamed x21 -> x55, local copies, waits for them, and re-layouts: 1.56 us -> 17.5 us
    all_to_all x0 -> x2, starting transfers between devices: none -> 12 us  [the longest x1 7.62 us: step(): lax.all_to_all(cot_send.reshape(owners, cap, share), 'dp', split_axis=0,...]
    all_to_all x0 -> x2, waiting for transfers between devices: none -> 10.8 us  [the longest x1 6.16 us: step(): lax.all_to_all(cot_send.reshape(owners, cap, share), 'dp', split_axis=0,...]
  transfers between devices with their start and end apart: 12 -> 33, of which waited for: 6 -> 21; matrix products, arithmetic and copies ran while one was open for 2% -> 13% of each run, Pallas kernels for 13% -> 22%
where the time goes in v2:
time: 209 us; the launch traced here: 207 us
  starting transfers between devices  83.5 us (40%)
  Pallas kernels  48.7 us (23%)
  waiting for transfers between devices  44.4 us (21%)
  local copies, waits for them, and re-layouts  21.2 us (10%)
  matrix products  5.07 us (2%)
  other arithmetic  2.66 us (1%)
    ppermute x28, starting transfers between devices, shift(): lax.ppermute(x, 'expert', [(i, (i + by) % size) for i in range(size)])  50.7 us
    ppermute x28, waiting for transfers between devices, shift(): lax.ppermute(x, 'expert', [(i, (i + by) % size) for i in range(size)])  28.9 us
    unnamed x55, local copies, waits for them, and re-layouts  17.5 us
    pallas_call x2, Pallas kernels, step(): pl.pallas_call(functools.partial(backward_kernel, parts), name='backward'...  13 us
    pallas_call x1, Pallas kernels, step(): pl.pallas_call(functools.partial(combine_kernel, cap), name='combine', gr...  8.55 us
    pallas_call x1, Pallas kernels, step(): pl.pallas_call(weight_kernel, name='weight', grid=(parts,), in_specs=[pl....  8.43 us
    pallas_call x1, Pallas kernels, step(): pl.pallas_call(forward_kernel, name='forward', grid_spec=pltpu.PrefetchSc...  8.02 us
    all_to_all x1, starting transfers between devices, step(): lax.all_to_all(cot_send.reshape(owners, cap, share), 'dp', split_axis=0,...  7.62 us
  transfers between devices with their start and end apart: 33, of which 21 were waited for; matrix products, arithmetic and copies ran while one was open for 13% of the time, Pallas kernels for 22%

profile of v2, /device:TPU:2, one launch (start us, length us, event | category | flops | bytes accessed | tf_op | source)
XLA Modules:
  0.0 206.5 jit_solution(609237529238168177)
XLA Ops:
  0.7 2.2 %route.1 = (bf16[1024,128]{1,0:T(8,128)(2,1)}, bf16[1024,256]{1,0:T(8,128)(2,1)}) custom-call(s32[1]{0:T(128)} %bitcast.col_ref.z_ref, s32[4,128]{1,0:T(4,128)} %bitcast.146, f32[4,128]{1,0:T(4,128)} %bitcast.148, bf16[128,256]{1,0:T(8,128)(2,1)} %cot_ref.1, f32[32,2048]{1,0:T(8,128)} %ds_ref.3), custom_call_target="tpu_custom_call" | custom-call | flops 67108864 | bytes 1048576 | tf_op jit(solution)/shard_map/route/pallas_call | solution.py:253
  2.8 7.6 %all-to-all-start.2 = ((bf16[32,32,256]{2,1,0:T(8,128)(2,1)}), bf16[32,32,256]{2,1,0:T(8,128)(2,1)S(1)}, u32[]{:S(2)}, u32[]{:S(2)}) async-start(bf16[32,32,256]{2,1,0:T(8,128)(2,1)} %bitcast.145), calls=%async_computation.2 | async-start | bytes 1048576 | tf_op jit(solution)/shard_map/all_to_all | solution.py:270
  10.5 4.2 %fusion.14 = bf16[1024,2048]{1,0:T(8,128)(2,1)} fusion(bf16[1024,128]{1,0:T(8,128)(2,1)} %get-tuple-element.25, bf16[128,2048]{1,0:T(8,128)(2,1)S(1)} %copy-done), kind=kOutput, calls=%fused_computation.64 | convolution fusion | flops 536870912 | bytes 4980736 | tf_op jit(solution)/shard_map/dot_general | solution.py:273
  14.7 6.2 %all-to-all-done.2 = bf16[32,32,256]{2,1,0:T(8,128)(2,1)S(1)} async-done(((bf16[32,32,256]{2,1,0:T(8,128)(2,1)}), bf16[32,32,256]{2,1,0:T(8,128)(2,1)S(1)}, u32[]{:S(2)}, u32[]{:S(2)}) %all-to-all-start.2) | async-done | bytes 524320 | tf_op jit(solution)/shard_map/all_to_all | solution.py:270
  20.8 6.0 %all-to-all-start = ((bf16[32,32,2048]{2,1,0:T(8,128)(2,1)}), bf16[32,32,2048]{2,1,0:T(8,128)(2,1)}, u32[]{:S(2)}, u32[]{:S(2)}) async-start(bf16[32,32,2048]{2,1,0:T(8,128)(2,1)} %bitcast.129), calls=%async_computation | async-start | bytes 8388608 | tf_op jit(solution)/shard_map/all_to_all | solution.py:274
  27.0 2.0 collective-permute-start
  29.0 4.0 %collective-permute-start.7 = (bf16[576,256]{1,0:T(8,128)(2,1)S(1)}, bf16[576,256]{1,0:T(8,128)(2,1)S(1)}, u32[]{:S(2)}, u32[]{:S(2)}) collective-permute-start(bf16[576,256]{1,0:T(8,128)(2,1)S(1)} %pad_maximum_fusion.2.refs_0_.refs_8_), channel_id=1, source_target_pairs={{0,7},{1,0},{2,1},{3,2},{4,3},{5,4},{6,5},{7,6},{8,15},{9,8},{10,9... | collective-permute-start | bytes 884744 | tf_op jit(solution)/shard_map/ppermute | solution.py:189
  35.8 2.3 %home.1 = (bf16[128,1024]{1,0:T(8,128)(2,1)}, bf16[128,1024]{1,0:T(8,128)(2,1)}, bf16[128,1024]{1,0:T(8,128)(2,1)}) custom-call(s32[128,4]{1,0:T(8,128)} %copy.16.re_ref, f32[128,4]{1,0:T(8,128)} %copy.17.rw_ref), custom_call_target="tpu_custom_call" | custom-call | flops 25165824 | bytes 786432 | tf_op jit(solution)/shard_map/home/pallas_call | solution.py:283
  38.0 3.2 %collective-permute-start.11 = (bf16[576,256]{1,0:T(8,128)(2,1)S(1)}, bf16[576,256]{1,0:T(8,128)(2,1)S(1)}, u32[]{:S(2)}, u32[]{:S(2)}) collective-permute-start(bf16[576,256]{1,0:T(8,128)(2,1)S(1)} %pad_maximum_fusion.1.refs_0_), channel_id=1, source_target_pairs={{0,7},{1,0},{2,1},{3,2},{4,3},{5,4},{6,5},{7,6},{8,15},{9,8},{10,9... | collective-permute-start | bytes 884744 | tf_op jit(solution)/shard_map/ppermute | solution.py:189
  41.3 3.2 %collective-permute-start.8 = (bf16[576,256]{1,0:T(8,128)(2,1)S(1)}, bf16[576,256]{1,0:T(8,128)(2,1)S(1)}, u32[]{:S(2)}, u32[]{:S(2)}) collective-permute-start(bf16[576,256]{1,0:T(8,128)(2,1)S(1)} %collective-permute-done.7.refs_7_.refs_15_), channel_id=1, source_target_pairs={{0,7},{1,0},{2,1},{3,2},{4,3},{5,4},{6,5},{7,6},{8,15},{9,8},{10,9... | collective-permute-start | bytes 884744 | tf_op jit(solution)/shard_map/ppermute | solution.py:189
  45.1 2.0 collective-permute-done.1.refs_1_.refs_9_
  48.7 3.7 %collective-permute-start.12 = (bf16[576,256]{1,0:T(8,128)(2,1)S(1)}, bf16[576,256]{1,0:T(8,128)(2,1)}, u32[]{:S(2)}, u32[]{:S(2)}) collective-permute-start(bf16[576,256]{1,0:T(8,128)(2,1)S(1)} %collective-permute-done.11.refs_7_), channel_id=1, source_target_pairs={{0,7},{1,0},{2,1},{3,2},{4,3},{5,4},{6,5},{7,6},{8,15},{9,8},{10,9... | collective-permute-start | bytes 884744 | tf_op jit(solution)/shard_map/ppermute | solution.py:189
  53.4 1.6 collective-permute-done.8.refs_6_.refs_14_
  55.0 3.7 %collective-permute-start.9 = (bf16[576,256]{1,0:T(8,128)(2,1)S(1)}, bf16[576,256]{1,0:T(8,128)(2,1)}, u32[]{:S(2)}, u32[]{:S(2)}) collective-permute-start(bf16[576,256]{1,0:T(8,128)(2,1)S(1)} %collective-permute-done.8.refs_6_.refs_14_), channel_id=1, source_target_pairs={{0,7},{1,0},{2,1},{3,2},{4,3},{5,4},{6,5},{7,6},{8,15},{9,8},{10,9... | collective-permute-start | bytes 884744 | tf_op jit(solution)/shard_map/ppermute | solution.py:189
  61.3 3.8 %collective-permute-start.13 = (bf16[576,256]{1,0:T(8,128)(2,1)}, bf16[576,256]{1,0:T(8,128)(2,1)}, u32[]{:S(2)}, u32[]{:S(2)}) collective-permute-start(bf16[576,256]{1,0:T(8,128)(2,1)} %collective-permute-done.12.refs_6_), channel_id=1, source_target_pairs={{0,7},{1,0},{2,1},{3,2},{4,3},{5,4},{6,5},{7,6},{8,15},{9,8},{10,9... | collective-permute-start | bytes 884744 | tf_op jit(solution)/shard_map/ppermute | solution.py:189
  66.1 1.6 collective-permute-done.9.refs_5_.refs_13_
  67.6 3.8 %collective-permute-start.10 = (bf16[576,256]{1,0:T(8,128)(2,1)}, bf16[576,256]{1,0:T(8,128)(2,1)}, u32[]{:S(2)}, u32[]{:S(2)}) collective-permute-start(bf16[576,256]{1,0:T(8,128)(2,1)} %collective-permute-done.9.refs_5_.refs_13_), channel_id=1, source_target_pairs={{0,7},{1,0},{2,1},{3,2},{4,3},{5,4},{6,5},{7,6},{8,15},{9,8},{10,9... | collective-permute-start | bytes 884744 | tf_op jit(solution)/shard_map/ppermute | solution.py:189
  73.7 4.7 %all-to-all-done = bf16[32,32,2048]{2,1,0:T(8,128)(2,1)} async-done(((bf16[32,32,2048]{2,1,0:T(8,128)(2,1)}), bf16[32,32,2048]{2,1,0:T(8,128)(2,1)}, u32[]{:S(2)}, u32[]{:S(2)}) %all-to-all-start) | async-done | bytes 4194336 | tf_op jit(solution)/shard_map/all_to_all | solution.py:274
  78.4 8.0 %forward.1 = (f32[1024,176]{1,0:T(8,128)}, f32[1024,176]{1,0:T(8,128)}, bf16[1024,176]{1,0:T(8,128)(2,1)}, bf16[1024,2048]{1,0:T(8,128)(2,1)}) custom-call(s32[1]{0:T(128)} %bitcast.1.e_ref, bf16[1024,2048]{1,0:T(8,128)(2,1)} %bitcast.5.x_ref, bf16[176,2048]{1,0:T(8,128)(2,1)} %bitcast.131, bf16[176,2048]{1,0:T(8,128)(2,1)} %bitcast.134, ...), custom_call_target="tpu_custom_call" | custom-call | flops 2214592512 | bytes 8388608 | tf_op jit(solution)/shard_map/forward/pallas_call | solution.py:296
  86.5 7.3 %all-to-all-start.1 = ((bf16[32,32,2048]{2,1,0:T(8,128)(2,1)}), bf16[32,32,2048]{2,1,0:T(8,128)(2,1)}, u32[]{:S(2)}, u32[]{:S(2)}) async-start(bf16[32,32,2048]{2,1,0:T(8,128)(2,1)} %bitcast.130), calls=%async_computation.1 | async-start | bytes 8388608 | tf_op jit(solution)/shard_map/all_to_all | solution.py:316
  93.8 1.4 constant_dynamic-update-slice_fusion.7
  95.2 1.4 constant_dynamic-update-slice_fusion.6
  96.6 6.5 %backward.3 = (bf16[512,176]{1,0:T(8,128)(2,1)}, bf16[512,176]{1,0:T(8,128)(2,1)}, bf16[8,512,256]{2,1,0:T(8,128)(2,1)}) custom-call(s32[1]{0:T(128)} %bitcast.col_ref.z_ref, bf16[576,256]{1,0:T(8,128)(2,1)} %copy-done.2, bf16[576,256]{1,0:T(8,128)(2,1)} %copy-done.8, bf16[576,256]{1,0:T(8,128)(2,1)} %copy-done.12, bf16[576,256]{1,0:T(8,128)(2,1)} %copy-done.14, ...), custom_call_target="tpu_custom_call" | custom-call | flops 1107296256 | bytes 4194304 | tf_op jit(solution)/shard_map/backward/pallas_call | solution.py:327
  104.1 5.9 %collective-permute-start.24 = (bf16[512,256]{1,0:T(8,128)(2,1)S(1)}, bf16[512,256]{1,0:T(8,128)(2,1)S(1)}, u32[]{:S(2)}, u32[]{:S(2)}) collective-permute-start(bf16[512,256]{1,0:T(8,128)(2,1)S(1)} %get-tuple-element.55), channel_id=1, source_target_pairs={{0,7},{1,0},{2,1},{3,2},{4,3},{5,4},{6,5},{7,6},{8,15},{9,8},{10,9... | collective-permute-start | bytes 786440 | tf_op jit(solution)/shard_map/ppermute | solution.py:189
  110.1 6.5 %backward.2 = (bf16[512,176]{1,0:T(8,128)(2,1)}, bf16[512,176]{1,0:T(8,128)(2,1)}, bf16[8,512,256]{2,1,0:T(8,128)(2,1)}) custom-call(s32[1]{0:T(128)} %bitcast.col_ref.z_ref, bf16[576,256]{1,0:T(8,128)(2,1)} %copy-done.1, bf16[576,256]{1,0:T(8,128)(2,1)} %copy-done.6, bf16[576,256]{1,0:T(8,128)(2,1)} %copy-done.10, bf16[576,256]{1,0:T(8,128)(2,1)} %copy-done.13, ...), custom_call_target="tpu_custom_call" | custom-call | flops 1107296256 | bytes 4194304 | tf_op jit(solution)/shard_map/backward/pallas_call | solution.py:327
  119.3 3.2 %collective-permute-start.18 = (bf16[512,256]{1,0:T(8,128)(2,1)S(1)}, bf16[512,256]{1,0:T(8,128)(2,1)S(1)}, u32[]{:S(2)}, u32[]{:S(2)}) collective-permute-start(bf16[512,256]{1,0:T(8,128)(2,1)S(1)} %get-tuple-element.49), channel_id=1, source_target_pairs={{0,7},{1,0},{2,1},{3,2},{4,3},{5,4},{6,5},{7,6},{8,15},{9,8},{10,9... | collective-permute-start | bytes 786440 | tf_op jit(solution)/shard_map/ppermute | solution.py:189
  122.6 2.1 %collective-permute-start.25 = (bf16[512,256]{1,0:T(8,128)(2,1)S(1)}, bf16[512,256]{1,0:T(8,128)(2,1)S(1)}, u32[]{:S(2)}, u32[]{:S(2)}) collective-permute-start(bf16[512,256]{1,0:T(8,128)(2,1)S(1)} %fusion.3), channel_id=1, source_target_pairs={{0,7},{1,0},{2,1},{3,2},{4,3},{5,4},{6,5},{7,6},{8,15},{9,8},{10,9... | collective-permute-start | bytes 786440 | tf_op jit(solution)/shard_map/ppermute | solution.py:189
  124.7 3.6 %collective-permute-done.14 = bf16[512,256]{1,0:T(8,128)(2,1)S(1)} collective-permute-done((bf16[512,256]{1,0:T(8,128)(2,1)S(1)}, bf16[512,256]{1,0:T(8,128)(2,1)S(1)}, u32[]{:S(2)}, u32[]{:S(2)}) %collective-permute-start.14) | collective-permute-done | bytes 262176 | tf_op jit(solution)/shard_map/ppermute | solution.py:189
  129.4 1.4 constant_dynamic-update-slice_fusion.4
  130.7 3.1 %collective-permute-done.21 = bf16[512,256]{1,0:T(8,128)(2,1)S(1)} collective-permute-done((bf16[512,256]{1,0:T(8,128)(2,1)S(1)}, bf16[512,256]{1,0:T(8,128)(2,1)S(1)}, u32[]{:S(2)}, u32[]{:S(2)}) %collective-permute-start.21) | collective-permute-done | bytes 262176 | tf_op jit(solution)/shard_map/ppermute | solution.py:189
  134.2 3.4 %collective-permute-start.26 = (bf16[512,256]{1,0:T(8,128)(2,1)S(1)}, bf16[512,256]{1,0:T(8,128)(2,1)S(1)}, u32[]{:S(2)}, u32[]{:S(2)}) collective-permute-start(bf16[512,256]{1,0:T(8,128)(2,1)S(1)} %get-tuple-element.53), channel_id=1, source_target_pairs={{0,7},{1,0},{2,1},{3,2},{4,3},{5,4},{6,5},{7,6},{8,15},{9,8},{10,9... | collective-permute-start | bytes 786440 | tf_op jit(solution)/shard_map/ppermute | solution.py:189
  137.6 2.1 %collective-permute-done.15 = bf16[512,256]{1,0:T(8,128)(2,1)S(1)} collective-permute-done((bf16[512,256]{1,0:T(8,128)(2,1)S(1)}, bf16[512,256]{1,0:T(8,128)(2,1)S(1)}, u32[]{:S(2)}, u32[]{:S(2)}) %collective-permute-start.15) | collective-permute-done | bytes 262176 | tf_op jit(solution)/shard_map/ppermute | solution.py:189
  140.0 3.2 %collective-permute-start.19 = (bf16[512,256]{1,0:T(8,128)(2,1)S(1)}, bf16[512,256]{1,0:T(8,128)(2,1)S(1)}, u32[]{:S(2)}, u32[]{:S(2)}) collective-permute-start(bf16[512,256]{1,0:T(8,128)(2,1)S(1)} %get-tuple-element.47), channel_id=1, source_target_pairs={{0,7},{1,0},{2,1},{3,2},{4,3},{5,4},{6,5},{7,6},{8,15},{9,8},{10,9... | collective-permute-start | bytes 786440 | tf_op jit(solution)/shard_map/ppermute | solution.py:189
  145.5 2.2 %collective-permute-start.27 = (bf16[512,256]{1,0:T(8,128)(2,1)S(1)}, bf16[512,256]{1,0:T(8,128)(2,1)S(1)}, u32[]{:S(2)}, u32[]{:S(2)}) collective-permute-start(bf16[512,256]{1,0:T(8,128)(2,1)S(1)} %get-tuple-element.51), channel_id=1, source_target_pairs={{0,7},{1,0},{2,1},{3,2},{4,3},{5,4},{6,5},{7,6},{8,15},{9,8},{10,9... | collective-permute-start | bytes 786440 | tf_op jit(solution)/shard_map/ppermute | solution.py:189
  147.7 3.3 %collective-permute-done.16 = bf16[512,256]{1,0:T(8,128)(2,1)S(1)} collective-permute-done((bf16[512,256]{1,0:T(8,128)(2,1)S(1)}, bf16[512,256]{1,0:T(8,128)(2,1)S(1)}, u32[]{:S(2)}, u32[]{:S(2)}) %collective-permute-start.16) | collective-permute-done | bytes 262176 | tf_op jit(solution)/shard_map/ppermute | solution.py:189
  151.1 2.7 %collective-permute-start.20 = (bf16[512,256]{1,0:T(8,128)(2,1)S(1)}, bf16[512,256]{1,0:T(8,128)(2,1)S(1)}, u32[]{:S(2)}, u32[]{:S(2)}) collective-permute-start(bf16[512,256]{1,0:T(8,128)(2,1)S(1)} %get-tuple-element.45), channel_id=1, source_target_pairs={{0,7},{1,0},{2,1},{3,2},{4,3},{5,4},{6,5},{7,6},{8,15},{9,8},{10,9... | collective-permute-start | bytes 786440 | tf_op jit(solution)/shard_map/ppermute | solution.py:189
  155.5 1.8 collective-permute-done.23
  157.4 1.6 collective-permute-done.20
  159.0 2.4 %collective-permute-done.17 = bf16[512,256]{1,0:T(8,128)(2,1)S(1)} collective-permute-done((bf16[512,256]{1,0:T(8,128)(2,1)S(1)}, bf16[512,256]{1,0:T(8,128)(2,1)S(1)}, u32[]{:S(2)}, u32[]{:S(2)}) %collective-permute-start.17) | collective-permute-done | bytes 262176 | tf_op jit(solution)/shard_map/ppermute | solution.py:189
  162.3 7.5 %all-to-all-start.4 = ((bf16[32,32,256]{2,1,0:T(8,128)(2,1)}), bf16[32,32,256]{2,1,0:T(8,128)(2,1)S(1)}, u32[]{:S(2)}, u32[]{:S(2)}) async-start(bf16[32,32,256]{2,1,0:T(8,128)(2,1)} %bitcast.47), calls=%async_computation.4 | async-start | bytes 1048576 | tf_op jit(solution)/shard_map/all_to_all | solution.py:408
  169.8 1.4 constant_dynamic-update-slice_fusion.1
  171.2 1.4 constant_dynamic-update-slice_fusion
  172.6 8.6 %combine.1 = bf16[8,136,256]{2,1,0:T(8,128)(2,1)} custom-call(s32[1]{0:T(128)} %bitcast.col_ref.z_ref, bf16[1024,2048]{1,0:T(8,128)(2,1)} %bitcast.10.y_ref, bf16[8,2,64,256]{3,2,1,0:T(8,128)(2,1)} %bitcast.144, bf16[128,1024]{1,0:T(8,128)(2,1)} %get-tuple-element.28.mt_ref, bf16[128,1024]{1,0:T(8,128)(2,1)} %get-tuple-element.29.mh_ref, ...), custom_call_target="tpu_custom_call" | custom-call | flops 1610612736 | bytes 4194304 | tf_op jit(solution)/shard_map/combine/pallas_call | solution.py:379
  181.1 4.3 %all-to-all-start.3 = ((bf16[8,136,256]{2,1,0:T(8,128)(2,1)}), bf16[8,136,256]{2,1,0:T(8,128)(2,1)S(1)}, u32[]{:S(2)}, u32[]{:S(2)}) async-start(bf16[8,136,256]{2,1,0:T(8,128)(2,1)} %combine.1), calls=%async_computation.3 | async-start | bytes 1114112 | tf_op jit(solution)/shard_map/all_to_all | solution.py:397
  185.5 4.5 %down.1 = f32[176,2048]{1,0:T(8,128)} custom-call(s32[1]{0:T(128)} %bitcast.col_ref.z_ref, bf16[1024,176]{1,0:T(8,128)(2,1)} %get-tuple-element.43.h_ref, bf16[576,256]{1,0:T(8,128)(2,1)} %copy-done.1, bf16[576,256]{1,0:T(8,128)(2,1)} %copy-done.6, bf16[576,256]{1,0:T(8,128)(2,1)} %copy-done.10, bf16[576,256]{1,0:T(8,128)(2,1)} %copy-done.13, ...), custom_call_target="tpu_custom_call" | custom-call | flops 738197504 | bytes 5636096 | tf_op jit(solution)/shard_map/down/pallas_call | solution.py:363
  190.0 8.4 %weight.1 = (f32[176,2048]{1,0:T(8,128)}, f32[176,2048]{1,0:T(8,128)}) custom-call(bf16[1024,2048]{1,0:T(8,128)(2,1)} %bitcast.5.x_ref, bf16[512,176]{1,0:T(8,128)(2,1)} %get-tuple-element.37.refs_0_, bf16[512,176]{1,0:T(8,128)(2,1)} %get-tuple-element.38.refs_1_, bf16[512,176]{1,0:T(8,128)(2,1)} %get-tuple-element.39.refs_2_, ...), custom_call_target="tpu_custom_call" | custom-call | flops 1476395008 | bytes 7077888 | tf_op jit(solution)/shard_map/weight/pallas_call | solution.py:354
  199.3 4.6 %all-to-all-done.3.x_ref = bf16[8,136,256]{2,1,0:T(8,128)(2,1)S(1)} async-done(((bf16[8,136,256]{2,1,0:T(8,128)(2,1)}), bf16[8,136,256]{2,1,0:T(8,128)(2,1)S(1)}, u32[]{:S(2)}, u32[]{:S(2)}) %all-to-all-start.3) | async-done | bytes 557088 | tf_op jit(solution)/shard_map/all_to_all | solution.py:397
  204.8 1.8 mixed.1
  (100 shorter events, 24.3 us)
Async XLA Ops:
  0.6 9.8 %copy-start = (bf16[128,2048]{1,0:T(8,128)(2,1)S(1)}, bf16[128,2048]{1,0:T(8,128)(2,1)}, u32[]{:S(2)}) copy-start(bf16[128,2048]{1,0:T(8,128)(2,1)} %param.10) | copy-start | bytes 1572868
  2.8 18.0 %all-to-all-start.2 = ((bf16[32,32,256]{2,1,0:T(8,128)(2,1)}), bf16[32,32,256]{2,1,0:T(8,128)(2,1)S(1)}, u32[]{:S(2)}, u32[]{:S(2)}) async-start(bf16[32,32,256]{2,1,0:T(8,128)(2,1)} %bitcast.145), calls=%async_computation.2 | async-start | bytes 1048576 | tf_op jit(solution)/shard_map/all_to_all | solution.py:270
  20.8 57.6 %all-to-all-start = ((bf16[32,32,2048]{2,1,0:T(8,128)(2,1)}), bf16[32,32,2048]{2,1,0:T(8,128)(2,1)}, u32[]{:S(2)}, u32[]{:S(2)}) async-start(bf16[32,32,2048]{2,1,0:T(8,128)(2,1)} %bitcast.129), calls=%async_computation | async-start | bytes 8388608 | tf_op jit(solution)/shard_map/all_to_all | solution.py:274
  26.9 8.1 %copy-start.18 = (f32[128,4]{0,1:T(4,128)S(1)}, f32[128,4]{0,1:T(4,128)}, u32[]{:S(2)}) copy-start(f32[128,4]{0,1:T(4,128)} %param.12) | copy-start | bytes 6148
  27.0 59.4 %copy-start.1 = (bf16[576,256]{1,0:T(8,128)(2,1)}, bf16[576,256]{1,0:T(8,128)(2,1)S(1)}, u32[]{:S(2)}) copy-start(bf16[576,256]{1,0:T(8,128)(2,1)S(1)} %pad_maximum_fusion.1.refs_0_) | copy-start | bytes 884740
  27.0 14.3 %collective-permute-start = (bf16[576,256]{1,0:T(8,128)(2,1)S(1)}, bf16[576,256]{1,0:T(8,128)(2,1)S(1)}, u32[]{:S(2)}, u32[]{:S(2)}) collective-permute-start(bf16[576,256]{1,0:T(8,128)(2,1)S(1)} %pad_maximum_fusion.1.refs_0_), channel_id=1, source_target_pairs={{0,1},{1,2},{2,3},{3,4},{4,5},{5,6},{6,7},{7,0},{8,9},{9,10},{10,1... | collective-permute-start | bytes 884744 | tf_op jit(solution)/shard_map/ppermute | solution.py:189
  29.0 57.4 %copy-start.2 = (bf16[576,256]{1,0:T(8,128)(2,1)}, bf16[576,256]{1,0:T(8,128)(2,1)S(1)}, u32[]{:S(2)}) copy-start(bf16[576,256]{1,0:T(8,128)(2,1)S(1)} %pad_maximum_fusion.2.refs_0_.refs_8_) | copy-start | bytes 884740
  29.0 12.3 %collective-permute-start.7 = (bf16[576,256]{1,0:T(8,128)(2,1)S(1)}, bf16[576,256]{1,0:T(8,128)(2,1)S(1)}, u32[]{:S(2)}, u32[]{:S(2)}) collective-permute-start(bf16[576,256]{1,0:T(8,128)(2,1)S(1)} %pad_maximum_fusion.2.refs_0_.refs_8_), channel_id=1, source_target_pairs={{0,7},{1,0},{2,1},{3,2},{4,3},{5,4},{6,5},{7,6},{8,15},{9,8},{10,9... | collective-permute-start | bytes 884744 | tf_op jit(solution)/shard_map/ppermute | solution.py:189
  33.7 13.5 %collective-permute-start.1 = (bf16[576,256]{1,0:T(8,128)(2,1)S(1)}, bf16[576,256]{1,0:T(8,128)(2,1)S(1)}, u32[]{:S(2)}, u32[]{:S(2)}) collective-permute-start(bf16[576,256]{1,0:T(8,128)(2,1)S(1)} %pad_maximum_fusion.2.refs_0_.refs_8_), channel_id=1, source_target_pairs={{0,1},{1,2},{2,3},{3,4},{4,5},{5,6},{6,7},{7,0},{8,9},{9,10},{10,1... | collective-permute-start | bytes 884744 | tf_op jit(solution)/shard_map/ppermute | solution.py:189
  38.0 10.6 %collective-permute-start.11 = (bf16[576,256]{1,0:T(8,128)(2,1)S(1)}, bf16[576,256]{1,0:T(8,128)(2,1)S(1)}, u32[]{:S(2)}, u32[]{:S(2)}) collective-permute-start(bf16[576,256]{1,0:T(8,128)(2,1)S(1)} %pad_maximum_fusion.1.refs_0_), channel_id=1, source_target_pairs={{0,7},{1,0},{2,1},{3,2},{4,3},{5,4},{6,5},{7,6},{8,15},{9,8},{10,9... | collective-permute-start | bytes 884744 | tf_op jit(solution)/shard_map/ppermute | solution.py:189
  41.3 45.2 %copy-start.6 = (bf16[576,256]{1,0:T(8,128)(2,1)}, bf16[576,256]{1,0:T(8,128)(2,1)S(1)}, u32[]{:S(2)}) copy-start(bf16[576,256]{1,0:T(8,128)(2,1)S(1)} %collective-permute-done.refs_1_) | copy-start | bytes 884740
  41.3 12.2 %collective-permute-start.2 = (bf16[576,256]{1,0:T(8,128)(2,1)S(1)}, bf16[576,256]{1,0:T(8,128)(2,1)S(1)}, u32[]{:S(2)}, u32[]{:S(2)}) collective-permute-start(bf16[576,256]{1,0:T(8,128)(2,1)S(1)} %collective-permute-done.refs_1_), channel_id=1, source_target_pairs={{0,1},{1,2},{2,3},{3,4},{4,5},{5,6},{6,7},{7,0},{8,9},{9,10},{10,1... | collective-permute-start | bytes 884744 | tf_op jit(solution)/shard_map/ppermute | solution.py:189
  41.3 45.1 %copy-start.7 = (bf16[576,256]{1,0:T(8,128)(2,1)}, bf16[576,256]{1,0:T(8,128)(2,1)S(1)}, u32[]{:S(2)}) copy-start(bf16[576,256]{1,0:T(8,128)(2,1)S(1)} %collective-permute-done.7.refs_7_.refs_15_) | copy-start | bytes 884740
  41.3 13.7 %collective-permute-start.8 = (bf16[576,256]{1,0:T(8,128)(2,1)S(1)}, bf16[576,256]{1,0:T(8,128)(2,1)S(1)}, u32[]{:S(2)}, u32[]{:S(2)}) collective-permute-start(bf16[576,256]{1,0:T(8,128)(2,1)S(1)} %collective-permute-done.7.refs_7_.refs_15_), channel_id=1, source_target_pairs={{0,7},{1,0},{2,1},{3,2},{4,3},{5,4},{6,5},{7,6},{8,15},{9,8},{10,9... | collective-permute-start | bytes 884744 | tf_op jit(solution)/shard_map/ppermute | solution.py:189
  47.1 39.3 %copy-start.8 = (bf16[576,256]{1,0:T(8,128)(2,1)}, bf16[576,256]{1,0:T(8,128)(2,1)S(1)}, u32[]{:S(2)}) copy-start(bf16[576,256]{1,0:T(8,128)(2,1)S(1)} %collective-permute-done.1.refs_1_.refs_9_) | copy-start | bytes 884740
  47.1 12.6 %collective-permute-start.3 = (bf16[576,256]{1,0:T(8,128)(2,1)S(1)}, bf16[576,256]{1,0:T(8,128)(2,1)S(1)}, u32[]{:S(2)}, u32[]{:S(2)}) collective-permute-start(bf16[576,256]{1,0:T(8,128)(2,1)S(1)} %collective-permute-done.1.refs_1_.refs_9_), channel_id=1, source_target_pairs={{0,1},{1,2},{2,3},{3,4},{4,5},{5,6},{6,7},{7,0},{8,9},{9,10},{10,1... | collective-permute-start | bytes 884744 | tf_op jit(solution)/shard_map/ppermute | solution.py:189
  48.7 37.8 %copy-start.9 = (bf16[576,256]{1,0:T(8,128)(2,1)}, bf16[576,256]{1,0:T(8,128)(2,1)S(1)}, u32[]{:S(2)}) copy-start(bf16[576,256]{1,0:T(8,128)(2,1)S(1)} %collective-permute-done.11.refs_7_) | copy-start | bytes 884740
  48.7 12.6 %collective-permute-start.12 = (bf16[576,256]{1,0:T(8,128)(2,1)S(1)}, bf16[576,256]{1,0:T(8,128)(2,1)}, u32[]{:S(2)}, u32[]{:S(2)}) collective-permute-start(bf16[576,256]{1,0:T(8,128)(2,1)S(1)} %collective-permute-done.11.refs_7_), channel_id=1, source_target_pairs={{0,7},{1,0},{2,1},{3,2},{4,3},{5,4},{6,5},{7,6},{8,15},{9,8},{10,9... | collective-permute-start | bytes 884744 | tf_op jit(solution)/shard_map/ppermute | solution.py:189
  53.4 33.0 %copy-start.10 = (bf16[576,256]{1,0:T(8,128)(2,1)}, bf16[576,256]{1,0:T(8,128)(2,1)S(1)}, u32[]{:S(2)}) copy-start(bf16[576,256]{1,0:T(8,128)(2,1)S(1)} %collective-permute-done.2.refs_2_) | copy-start | bytes 884740
  53.4 12.6 %collective-permute-start.4 = (bf16[576,256]{1,0:T(8,128)(2,1)S(1)}, bf16[576,256]{1,0:T(8,128)(2,1)S(1)}, u32[]{:S(2)}, u32[]{:S(2)}) collective-permute-start(bf16[576,256]{1,0:T(8,128)(2,1)S(1)} %collective-permute-done.2.refs_2_), channel_id=1, source_target_pairs={{0,1},{1,2},{2,3},{3,4},{4,5},{5,6},{6,7},{7,0},{8,9},{9,10},{10,1... | collective-permute-start | bytes 884744 | tf_op jit(solution)/shard_map/ppermute | solution.py:189
  55.0 31.5 %copy-start.11 = (bf16[576,256]{1,0:T(8,128)(2,1)}, bf16[576,256]{1,0:T(8,128)(2,1)S(1)}, u32[]{:S(2)}) copy-start(bf16[576,256]{1,0:T(8,128)(2,1)S(1)} %collective-permute-done.8.refs_6_.refs_14_) | copy-start | bytes 884740
  55.0 12.6 %collective-permute-start.9 = (bf16[576,256]{1,0:T(8,128)(2,1)S(1)}, bf16[576,256]{1,0:T(8,128)(2,1)}, u32[]{:S(2)}, u32[]{:S(2)}) collective-permute-start(bf16[576,256]{1,0:T(8,128)(2,1)S(1)} %collective-permute-done.8.refs_6_.refs_14_), channel_id=1, source_target_pairs={{0,7},{1,0},{2,1},{3,2},{4,3},{5,4},{6,5},{7,6},{8,15},{9,8},{10,9... | collective-permute-start | bytes 884744 | tf_op jit(solution)/shard_map/ppermute | solution.py:189
  59.8 26.7 %copy-start.12 = (bf16[576,256]{1,0:T(8,128)(2,1)}, bf16[576,256]{1,0:T(8,128)(2,1)S(1)}, u32[]{:S(2)}) copy-start(bf16[576,256]{1,0:T(8,128)(2,1)S(1)} %collective-permute-done.3.refs_2_.refs_10_) | copy-start | bytes 884740
  59.8 12.6 %collective-permute-start.5 = (bf16[576,256]{1,0:T(8,128)(2,1)S(1)}, bf16[576,256]{1,0:T(8,128)(2,1)S(1)}, u32[]{:S(2)}, u32[]{:S(2)}) collective-permute-start(bf16[576,256]{1,0:T(8,128)(2,1)S(1)} %collective-permute-done.3.refs_2_.refs_10_), channel_id=1, source_target_pairs={{0,1},{1,2},{2,3},{3,4},{4,5},{5,6},{6,7},{7,0},{8,9},{9,10},{10,1... | collective-permute-start | bytes 884744 | tf_op jit(solution)/shard_map/ppermute | solution.py:189
  61.3 48.8 %collective-permute-start.13 = (bf16[576,256]{1,0:T(8,128)(2,1)}, bf16[576,256]{1,0:T(8,128)(2,1)}, u32[]{:S(2)}, u32[]{:S(2)}) collective-permute-start(bf16[576,256]{1,0:T(8,128)(2,1)} %collective-permute-done.12.refs_6_), channel_id=1, source_target_pairs={{0,7},{1,0},{2,1},{3,2},{4,3},{5,4},{6,5},{7,6},{8,15},{9,8},{10,9... | collective-permute-start | bytes 884744 | tf_op jit(solution)/shard_map/ppermute | solution.py:189
  66.1 20.4 %copy-start.13 = (bf16[576,256]{1,0:T(8,128)(2,1)}, bf16[576,256]{1,0:T(8,128)(2,1)S(1)}, u32[]{:S(2)}) copy-start(bf16[576,256]{1,0:T(8,128)(2,1)S(1)} %collective-permute-done.4.refs_3_) | copy-start | bytes 884740
  66.1 27.7 %collective-permute-start.6 = (bf16[576,256]{1,0:T(8,128)(2,1)S(1)}, bf16[576,256]{1,0:T(8,128)(2,1)}, u32[]{:S(2)}, u32[]{:S(2)}) collective-permute-start(bf16[576,256]{1,0:T(8,128)(2,1)S(1)} %collective-permute-done.4.refs_3_), channel_id=1, source_target_pairs={{0,1},{1,2},{2,3},{3,4},{4,5},{5,6},{6,7},{7,0},{8,9},{9,10},{10,1... | collective-permute-start | bytes 884744 | tf_op jit(solution)/shard_map/ppermute | solution.py:189
  67.6 27.6 %collective-permute-start.10 = (bf16[576,256]{1,0:T(8,128)(2,1)}, bf16[576,256]{1,0:T(8,128)(2,1)}, u32[]{:S(2)}, u32[]{:S(2)}) collective-permute-start(bf16[576,256]{1,0:T(8,128)(2,1)} %collective-permute-done.9.refs_5_.refs_13_), channel_id=1, source_target_pairs={{0,7},{1,0},{2,1},{3,2},{4,3},{5,4},{6,5},{7,6},{8,15},{9,8},{10,9... | collective-permute-start | bytes 884744 | tf_op jit(solution)/shard_map/ppermute | solution.py:189
  86.5 75.8 %all-to-all-start.1 = ((bf16[32,32,2048]{2,1,0:T(8,128)(2,1)}), bf16[32,32,2048]{2,1,0:T(8,128)(2,1)}, u32[]{:S(2)}, u32[]{:S(2)}) async-start(bf16[32,32,2048]{2,1,0:T(8,128)(2,1)} %bitcast.130), calls=%async_computation.1 | async-start | bytes 8388608 | tf_op jit(solution)/shard_map/all_to_all | solution.py:316
  104.1 18.4 %copy-start.4 = (bf16[8,512,256]{2,1,0:T(8,128)(2,1)S(1)}, bf16[8,512,256]{2,1,0:T(8,128)(2,1)}, u32[]{:S(2)}) copy-start(bf16[8,512,256]{2,1,0:T(8,128)(2,1)} %get-tuple-element.35) | copy-start | bytes 6291460
  104.1 18.4 %collective-permute-start.24 = (bf16[512,256]{1,0:T(8,128)(2,1)S(1)}, bf16[512,256]{1,0:T(8,128)(2,1)S(1)}, u32[]{:S(2)}, u32[]{:S(2)}) collective-permute-start(bf16[512,256]{1,0:T(8,128)(2,1)S(1)} %get-tuple-element.55), channel_id=1, source_target_pairs={{0,7},{1,0},{2,1},{3,2},{4,3},{5,4},{6,5},{7,6},{8,15},{9,8},{10,9... | collective-permute-start | bytes 786440 | tf_op jit(solution)/shard_map/ppermute | solution.py:189
  116.6 23.2 %copy-start.5 = (bf16[8,512,256]{2,1,0:T(8,128)(2,1)S(1)}, bf16[8,512,256]{2,1,0:T(8,128)(2,1)}, u32[]{:S(2)}) copy-start(bf16[8,512,256]{2,1,0:T(8,128)(2,1)} %get-tuple-element.34) | copy-start | bytes 6291460
  117.8 10.5 %collective-permute-start.14 = (bf16[512,256]{1,0:T(8,128)(2,1)S(1)}, bf16[512,256]{1,0:T(8,128)(2,1)S(1)}, u32[]{:S(2)}, u32[]{:S(2)}) collective-permute-start(bf16[512,256]{1,0:T(8,128)(2,1)S(1)} %get-tuple-element.48), channel_id=1, source_target_pairs={{0,1},{1,2},{2,3},{3,4},{4,5},{5,6},{6,7},{7,0},{8,9},{9,10},{10,1... | collective-permute-start | bytes 786440 | tf_op jit(solution)/shard_map/ppermute | solution.py:189
  119.3 14.6 %collective-permute-start.21 = (bf16[512,256]{1,0:T(8,128)(2,1)S(1)}, bf16[512,256]{1,0:T(8,128)(2,1)S(1)}, u32[]{:S(2)}, u32[]{:S(2)}) collective-permute-start(bf16[512,256]{1,0:T(8,128)(2,1)S(1)} %get-tuple-element.54), channel_id=1, source_target_pairs={{0,1},{1,2},{2,3},{3,4},{4,5},{5,6},{6,7},{7,0},{8,9},{9,10},{10,1... | collective-permute-start | bytes 786440 | tf_op jit(solution)/shard_map/ppermute | solution.py:189
  119.3 18.4 %collective-permute-start.18 = (bf16[512,256]{1,0:T(8,128)(2,1)S(1)}, bf16[512,256]{1,0:T(8,128)(2,1)S(1)}, u32[]{:S(2)}, u32[]{:S(2)}) collective-permute-start(bf16[512,256]{1,0:T(8,128)(2,1)S(1)} %get-tuple-element.49), channel_id=1, source_target_pairs={{0,7},{1,0},{2,1},{3,2},{4,3},{5,4},{6,5},{7,6},{8,15},{9,8},{10,9... | collective-permute-start | bytes 786440 | tf_op jit(solution)/shard_map/ppermute | solution.py:189
  122.6 11.3 %collective-permute-start.25 = (bf16[512,256]{1,0:T(8,128)(2,1)S(1)}, bf16[512,256]{1,0:T(8,128)(2,1)S(1)}, u32[]{:S(2)}, u32[]{:S(2)}) collective-permute-start(bf16[512,256]{1,0:T(8,128)(2,1)S(1)} %fusion.3), channel_id=1, source_target_pairs={{0,7},{1,0},{2,1},{3,2},{4,3},{5,4},{6,5},{7,6},{8,15},{9,8},{10,9... | collective-permute-start | bytes 786440 | tf_op jit(solution)/shard_map/ppermute | solution.py:189
  129.3 10.5 %collective-permute-start.15 = (bf16[512,256]{1,0:T(8,128)(2,1)S(1)}, bf16[512,256]{1,0:T(8,128)(2,1)S(1)}, u32[]{:S(2)}, u32[]{:S(2)}) collective-permute-start(bf16[512,256]{1,0:T(8,128)(2,1)S(1)} %fusion.11), channel_id=1, source_target_pairs={{0,1},{1,2},{2,3},{3,4},{4,5},{5,6},{6,7},{7,0},{8,9},{9,10},{10,1... | collective-permute-start | bytes 786440 | tf_op jit(solution)/shard_map/ppermute | solution.py:189
  134.0 11.4 %collective-permute-start.22 = (bf16[512,256]{1,0:T(8,128)(2,1)S(1)}, bf16[512,256]{1,0:T(8,128)(2,1)S(1)}, u32[]{:S(2)}, u32[]{:S(2)}) collective-permute-start(bf16[512,256]{1,0:T(8,128)(2,1)S(1)} %get-tuple-element.52), channel_id=1, source_target_pairs={{0,1},{1,2},{2,3},{3,4},{4,5},{5,6},{6,7},{7,0},{8,9},{9,10},{10,1... | collective-permute-start | bytes 786440 | tf_op jit(solution)/shard_map/ppermute | solution.py:189
  134.2 11.1 %collective-permute-start.26 = (bf16[512,256]{1,0:T(8,128)(2,1)S(1)}, bf16[512,256]{1,0:T(8,128)(2,1)S(1)}, u32[]{:S(2)}, u32[]{:S(2)}) collective-permute-start(bf16[512,256]{1,0:T(8,128)(2,1)S(1)} %get-tuple-element.53), channel_id=1, source_target_pairs={{0,7},{1,0},{2,1},{3,2},{4,3},{5,4},{6,5},{7,6},{8,15},{9,8},{10,9... | collective-permute-start | bytes 786440 | tf_op jit(solution)/shard_map/ppermute | solution.py:189
  139.9 11.1 %collective-permute-start.16 = (bf16[512,256]{1,0:T(8,128)(2,1)S(1)}, bf16[512,256]{1,0:T(8,128)(2,1)S(1)}, u32[]{:S(2)}, u32[]{:S(2)}) collective-permute-start(bf16[512,256]{1,0:T(8,128)(2,1)S(1)} %get-tuple-element.46), channel_id=1, source_target_pairs={{0,1},{1,2},{2,3},{3,4},{4,5},{5,6},{6,7},{7,0},{8,9},{9,10},{10,1... | collective-permute-start | bytes 786440 | tf_op jit(solution)/shard_map/ppermute | solution.py:189
  140.0 11.0 %collective-permute-start.19 = (bf16[512,256]{1,0:T(8,128)(2,1)S(1)}, bf16[512,256]{1,0:T(8,128)(2,1)S(1)}, u32[]{:S(2)}, u32[]{:S(2)}) collective-permute-start(bf16[512,256]{1,0:T(8,128)(2,1)S(1)} %get-tuple-element.47), channel_id=1, source_target_pairs={{0,7},{1,0},{2,1},{3,2},{4,3},{5,4},{6,5},{7,6},{8,15},{9,8},{10,9... | collective-permute-start | bytes 786440 | tf_op jit(solution)/shard_map/ppermute | solution.py:189
  145.5 10.0 %collective-permute-start.27 = (bf16[512,256]{1,0:T(8,128)(2,1)S(1)}, bf16[512,256]{1,0:T(8,128)(2,1)S(1)}, u32[]{:S(2)}, u32[]{:S(2)}) collective-permute-start(bf16[512,256]{1,0:T(8,128)(2,1)S(1)} %get-tuple-element.51), channel_id=1, source_target_pairs={{0,7},{1,0},{2,1},{3,2},{4,3},{5,4},{6,5},{7,6},{8,15},{9,8},{10,9... | collective-permute-start | bytes 786440 | tf_op jit(solution)/shard_map/ppermute | solution.py:189
  147.7 9.6 %collective-permute-start.23 = (bf16[512,256]{1,0:T(8,128)(2,1)S(1)}, bf16[512,256]{1,0:T(8,128)(2,1)S(1)}, u32[]{:S(2)}, u32[]{:S(2)}) collective-permute-start(bf16[512,256]{1,0:T(8,128)(2,1)S(1)} %get-tuple-element.50), channel_id=1, source_target_pairs={{0,1},{1,2},{2,3},{3,4},{4,5},{5,6},{6,7},{7,0},{8,9},{9,10},{10,1... | collective-permute-start | bytes 786440 | tf_op jit(solution)/shard_map/ppermute | solution.py:189
  151.1 7.9 %collective-permute-start.20 = (bf16[512,256]{1,0:T(8,128)(2,1)S(1)}, bf16[512,256]{1,0:T(8,128)(2,1)S(1)}, u32[]{:S(2)}, u32[]{:S(2)}) collective-permute-start(bf16[512,256]{1,0:T(8,128)(2,1)S(1)} %get-tuple-element.45), channel_id=1, source_target_pairs={{0,7},{1,0},{2,1},{3,2},{4,3},{5,4},{6,5},{7,6},{8,15},{9,8},{10,9... | collective-permute-start | bytes 786440 | tf_op jit(solution)/shard_map/ppermute | solution.py:189
  153.8 7.6 %collective-permute-start.17 = (bf16[512,256]{1,0:T(8,128)(2,1)S(1)}, bf16[512,256]{1,0:T(8,128)(2,1)S(1)}, u32[]{:S(2)}, u32[]{:S(2)}) collective-permute-start(bf16[512,256]{1,0:T(8,128)(2,1)S(1)} %get-tuple-element.44), channel_id=1, source_target_pairs={{0,1},{1,2},{2,3},{3,4},{4,5},{5,6},{6,7},{7,0},{8,9},{9,10},{10,1... | collective-permute-start | bytes 786440 | tf_op jit(solution)/shard_map/ppermute | solution.py:189
  162.3 18.8 %all-to-all-start.4 = ((bf16[32,32,256]{2,1,0:T(8,128)(2,1)}), bf16[32,32,256]{2,1,0:T(8,128)(2,1)S(1)}, u32[]{:S(2)}, u32[]{:S(2)}) async-start(bf16[32,32,256]{2,1,0:T(8,128)(2,1)} %bitcast.47), calls=%async_computation.4 | async-start | bytes 1048576 | tf_op jit(solution)/shard_map/all_to_all | solution.py:408
  181.1 22.8 %all-to-all-start.3 = ((bf16[8,136,256]{2,1,0:T(8,128)(2,1)}), bf16[8,136,256]{2,1,0:T(8,128)(2,1)S(1)}, u32[]{:S(2)}, u32[]{:S(2)}) async-start(bf16[8,136,256]{2,1,0:T(8,128)(2,1)} %combine.1), calls=%async_computation.3 | async-start | bytes 1114112 | tf_op jit(solution)/shard_map/all_to_all | solution.py:397
  190.0 8.4 %copy-start.15 = (bf16[128,1024]{1,0:T(8,128)(2,1)S(1)}, bf16[128,1024]{1,0:T(8,128)(2,1)}, u32[]{:S(2)}) copy-start(bf16[128,1024]{1,0:T(8,128)(2,1)} %get-tuple-element.28.mt_ref) | copy-start | bytes 786436
  (4 other events, 15.0 us)

commit v3 on v2

--- a/solution.py
+++ b/solution.py
@@ -58,7 +58,7 @@
             ).astype(BF16)
 
 
-def home_kernel(cap, re_ref, rw_ref, mt_ref, mh_ref, ml_ref):
+def home_kernel(cap, re_ref, rw_ref, mt_ref, mw_ref):
     toks, choose = re_ref.shape
     slots = mt_ref.shape[1]
     experts = slots // cap
@@ -80,8 +80,8 @@
     place = (iota((toks, slots), 1) & (cap - 1)).astype(F32)
     hit = dot(code, spread) == place
     mt_ref[...] = jnp.where(hit, 1.0, 0.0).astype(BF16)
-    mh_ref[...] = jnp.where(hit, dot(high, spread), 0.0).astype(BF16)
-    ml_ref[...] = jnp.where(hit, dot(rest, spread), 0.0).astype(BF16)
+    mw_ref[:toks, :] = jnp.where(hit, dot(high, spread), 0.0).astype(BF16)
+    mw_ref[toks:, :] = jnp.where(hit, dot(rest, spread), 0.0).astype(BF16)
 
 
 def forward_kernel(
@@ -100,8 +100,9 @@
 
 def backward_kernel(parts, z_ref, *refs):
     o_refs = refs[:parts]
-    g_ref, u_ref, gw_ref, uw_ref, dw_ref, gs_ref, us_ref, gi_ref, ui_ref, p_ref = refs[parts:]
-    share = p_ref.shape[2]
+    g_ref, u_ref, gw_ref, uw_ref, dw_ref, gs_ref, us_ref, gi_ref, ui_ref = refs[parts:-parts]
+    p_refs = refs[-parts:]
+    share = p_refs[0].shape[1]
 
     def cols(c):
         at = lax.rem(z_ref[0] + c, parts)
@@ -118,30 +119,38 @@
     gi_ref[...] = gi
     ui_ref[...] = ui
     for c in range(parts):
-        p_ref[c] = (dot(gi, gw_ref[:, cols(c)]) + dot(ui, uw_ref[:, cols(c)])).astype(BF16)
-
-
-def combine_kernel(cap, z_ref, y_ref, c_ref, mt_ref, mh_ref, ml_ref, re_ref, o_ref, acc_ref):
+        p_refs[c][...] = (dot(gi, gw_ref[:, cols(c)]) + dot(ui, uw_ref[:, cols(c)])).astype(BF16)
+
+
+def combine_kernel(cap, parts, z_ref, y_ref, mt_ref, mw_ref, re_ref, *refs):
+    o_ref, acc_ref, prod_ref = refs[2 * parts :]
     step = pl.program_id(0)
     toks, slots = mt_ref.shape
     experts = slots // cap
-    y = y_ref[...]
-    parts = o_ref.shape[0]
-    at = lax.rem(z_ref[0] + parts - step, parts)
-    o_ref[at, :toks, :] = (dot(mh_ref[...], y) + dot(ml_ref[...], y)).astype(BF16)
-    product = dot(c_ref[...].reshape(toks, y.shape[1]), y, NT)
+    block = y_ref.shape[0]
+    share = refs[0].shape[1]
+    part = dot(mw_ref[...], y_ref[...])
 
     @pl.when(step == 0)
     def _():
-        acc_ref[...] = product
+        acc_ref[...] = part
 
     @pl.when(step > 0)
     def _():
-        acc_ref[...] += product
+        acc_ref[...] += part
+
+    prod = None
+    for k in range(parts):
+        at = lax.rem(z_ref[0] + (parts - k), parts)
+        cols = pl.ds(pl.multiple_of(at * share, share), share)
+        c = jnp.concatenate([refs[k][...], refs[parts + k][...]], axis=0)
+        term = dot(c, y_ref[:, cols], NT)
+        prod = term if prod is None else prod + term
+    prod_ref[:, pl.ds(pl.multiple_of(step * block, block), block)] = prod
 
     @pl.when(step == pl.num_programs(0) - 1)
     def _():
-        held = jnp.where(mt_ref[...].astype(F32) > 0.0, acc_ref[...], 0.0)
+        held = jnp.where(mt_ref[...].astype(F32) > 0.0, prod_ref[...], 0.0)
         low = iota((experts, slots), 0) * cap
         slot = iota((experts, slots), 1)
         spread = jnp.where((slot >= low) & (slot < low + cap), 1.0, 0.0)
@@ -151,10 +160,12 @@
             jnp.sum(jnp.where(re_ref[k : k + 1, :] == expert_id, table, 0.0), axis=0, keepdims=True)
             for k in range(re_ref.shape[0])
         ]
-        block = jnp.concatenate(lines + [jnp.zeros_like(lines[0])] * 4, axis=0)
-        block = jnp.concatenate([block, jnp.zeros_like(block)], axis=1).astype(BF16)
-        for c in range(o_ref.shape[0]):
-            o_ref[c, toks:, :] = block
+        tail = jnp.concatenate(lines + [jnp.zeros_like(lines[0])] * 4, axis=0)
+        tail = jnp.concatenate([tail, jnp.zeros_like(tail)], axis=1).astype(BF16)
+        for c in range(parts):
+            cols = slice(c * share, (c + 1) * share)
+            o_ref[c, :toks, :] = (acc_ref[:toks, cols] + acc_ref[toks:, cols]).astype(BF16)
+            o_ref[c, toks:, :] = tail
 
 
 def mixed_kernel(x_ref, o_ref, r_ref):
@@ -213,7 +224,7 @@
 def ring_scatter(halves):
     sums = []
     for parts, ups in zip(halves, (4, 3)):
-        size = parts.shape[0]
+        size = len(parts)
         up = shift(parts[ups], 1)
         down = shift(parts[ups + 1], -1)
         for k in range(ups - 1, 0, -1):
@@ -280,13 +291,13 @@
         jnp.concatenate([cot_mine[rows:], cotangent[raw:]], axis=0),
     )
 
-    combine, high, rest = pl.pallas_call(
+    combine, weighted = pl.pallas_call(
         functools.partial(home_kernel, cap),
         name="home",
         in_specs=[full(toks, choose)] * 2,
-        out_specs=[full(toks, slots)] * 3,
+        out_specs=[full(toks, slots), full(2 * toks, slots)],
         grid=(1,),
-        out_shape=[sds((toks, slots), BF16)] * 3,
+        out_shape=[sds((toks, slots), BF16), sds((2 * toks, slots), BF16)],
         cost_estimate=cost(6 * slots * toks * owners, 6 * slots * toks),
     )(route_expert, route_weight)
 
@@ -334,21 +345,14 @@
                     + [row_in] * 2
                     + [full(hid, width)] * 3
                     + [full(1, hid)] * 2,
-                    out_specs=[
-                        row_out,
-                        row_out,
-                        pl.BlockSpec((parts, block, share), lambda i, z: (0, i, 0)),
-                    ],
+                    out_specs=[row_out] * 2
+                    + [pl.BlockSpec((block, share), lambda i, z: (i, 0))] * parts,
                 ),
-                out_shape=[
-                    sds((rows, hid), BF16),
-                    sds((rows, hid), BF16),
-                    sds((parts, rows, share), BF16),
-                ],
+                out_shape=[sds((rows, hid), BF16)] * 2 + [sds((rows, share), BF16)] * parts,
                 cost_estimate=cost(3 * slots * width * hid, 2 * slots * width),
             )(col, *out_grad[j], g, u, gw, uw, dw, gate_scale, up_scale)
         )
-    input_cols = ring_scatter([half[2] for half in halves])
+    input_cols = ring_scatter([half[2:] for half in halves])
 
     col_hid = pl.BlockSpec((hid, share), lambda i: (0, i))
     gate_grad, up_grad = pl.pallas_call(
@@ -373,30 +377,30 @@
         cost_estimate=cost(2 * slots * width * hid, 2 * slots * width + 4 * hid * width),
     )(col, h, *out_grad[0], *out_grad[1])
 
-    raw_all = jnp.stack([o[rows:] for pair in zip(*out_grad) for o in pair])
-    raw_all = raw_all.reshape(parts, 2, raw, share)
     tail = 8
     mixed_part = pl.pallas_call(
-        functools.partial(combine_kernel, cap),
+        functools.partial(combine_kernel, cap, parts),
         name="combine",
         grid_spec=pltpu.PrefetchScalarGridSpec(
             num_scalar_prefetch=1,
-            grid=(parts,),
+            grid=(slots // block,),
             in_specs=[
-                pl.BlockSpec((slots, share), lambda i, z: (0, lax.rem(z[0] + parts - i, parts))),
-                pl.BlockSpec((None, 2, raw, share), lambda i, z: (i, 0, 0, 0)),
+                pl.BlockSpec((block, width), lambda i, z: (i, 0)),
+                full(toks, slots),
+                pl.BlockSpec((2 * toks, block), lambda i, z: (0, i)),
+                full(choose, toks),
             ]
-            + [full(toks, slots)] * 3
-            + [full(choose, toks)],
+            + [pl.BlockSpec((raw, share), lambda i, z: (rows // raw, 0))] * (2 * parts),
             out_specs=full(parts, toks + tail, share),
-            scratch_shapes=[pltpu.VMEM((toks, slots), F32)],
+            scratch_shapes=[pltpu.VMEM((2 * toks, width), F32), pltpu.VMEM((toks, slots), F32)],
         ),
         out_shape=sds((parts, toks + tail, share), BF16),
         cost_estimate=cost(6 * slots * toks * width, 2 * slots * width),
-    )(col, returned, raw_all, combine, high, rest, route_expert.T)
+    )(col, returned, combine, weighted, route_expert.T, *out_grad[0], *out_grad[1])
     mixed_all = lax.all_to_all(mixed_part, "expert", split_axis=0, concat_axis=0, tiled=True)
     mixed, route_grad = pl.pallas_call(
         mixed_kernel,
+        compiler_params=pltpu.CompilerParams(vmem_limit_bytes=8 << 20),
         name="mixed",
         grid=(1,),
         in_specs=[full(parts, toks + tail, share)],

time: 209 us -> 228 us (1.091)
  waiting for transfers between devices: 44.4 us -> 85.4 us
  local copies, waits for them, and re-layouts: 21.2 us -> 2.4 us
  starting transfers between devices: 83.5 us -> 80.8 us
    all_to_all x1, waiting for transfers between devices: 4.68 us -> 33.2 us  [step(): lax.all_to_all(tok_send.reshape(owners, cap, width), 'dp', split_axis=0,...]
    unnamed x55 -> x60, local copies, waits for them, and re-layouts: 17.5 us -> 2.36 us
    ppermute x28, waiting for transfers between devices: 28.9 us -> 41.4 us  [shift(): lax.ppermute(x, 'expert', [(i, (i + by) % size) for i in range(size)])]
    ppermute x28, starting transfers between devices: 50.7 us -> 47.2 us  [shift(): lax.ppermute(x, 'expert', [(i, (i + by) % size) for i in range(size)])]
  transfers between devices with their start and end apart: 33 -> 33, of which waited for: 21 -> 13; matrix products, arithmetic and copies ran while one was open for 13% -> 5% of each run, Pallas kernels for 22% -> 20%
where the time goes in v3:
time: 228 us; the launch traced here: 226 us
  waiting for transfers between devices  85.4 us (37%)
  starting transfers between devices  80.8 us (35%)
  Pallas kernels  47.8 us (21%)
  matrix products  5.09 us (2%)
  other arithmetic  3.63 us (2%)
  local copies, waits for them, and re-layouts  2.4 us (1%)
    ppermute x28, starting transfers between devices, shift(): lax.ppermute(x, 'expert', [(i, (i + by) % size) for i in range(size)])  47.2 us
    ppermute x28, waiting for transfers between devices, shift(): lax.ppermute(x, 'expert', [(i, (i + by) % size) for i in range(size)])  41.4 us
    all_to_all x1, waiting for transfers between devices, step(): lax.all_to_all(tok_send.reshape(owners, cap, width), 'dp', split_axis=0,...  33.2 us
    pallas_call x2, Pallas kernels, step(): pl.pallas_call(functools.partial(backward_kernel, parts), name='backward'...  12.6 us
    pallas_call x1, Pallas kernels, step(): pl.pallas_call(functools.partial(combine_kernel, cap, parts), name='combi...  8.98 us
    pallas_call x1, Pallas kernels, step(): pl.pallas_call(weight_kernel, name='weight', grid=(parts,), in_specs=[pl....  8.43 us
    pallas_call x1, Pallas kernels, step(): pl.pallas_call(forward_kernel, name='forward', grid_spec=pltpu.PrefetchSc...  8.03 us
    all_to_all x1, starting transfers between devices, step(): lax.all_to_all(cot_send.reshape(owners, cap, share), 'dp', split_axis=0,...  7.62 us
  transfers between devices with their start and end apart: 33, of which 13 were waited for; matrix products, arithmetic and copies ran while one was open for 5% of the time, Pallas kernels for 20%

profile of v3, /device:TPU:2, one launch (start us, length us, event | category | flops | bytes accessed | tf_op | source)
XLA Modules:
  0.0 226.3 jit_solution(5298211912784733079)
XLA Ops:
  0.7 2.2 route.1
  2.8 7.6 %all-to-all-start.2 = ((bf16[32,32,256]{2,1,0:T(8,128)(2,1)}), bf16[32,32,256]{2,1,0:T(8,128)(2,1)S(1)}, u32[]{:S(2)}, u32[]{:S(2)}) async-start(bf16[32,32,256]{2,1,0:T(8,128)(2,1)} %bitcast.39), calls=%async_computation.2 | async-start | bytes 1048576 | tf_op jit(solution)/shard_map/all_to_all | solution.py:281
  10.5 4.2 %fusion.2 = bf16[1024,2048]{1,0:T(8,128)(2,1)} fusion(bf16[1024,128]{1,0:T(8,128)(2,1)} %get-tuple-element.38, bf16[128,2048]{1,0:T(8,128)(2,1)S(1)} %copy-done), kind=kOutput, calls=%fused_computation.18 | convolution fusion | flops 536870912 | bytes 4980736 | tf_op jit(solution)/shard_map/dot_general | solution.py:284
  14.7 6.1 %all-to-all-done.2 = bf16[32,32,256]{2,1,0:T(8,128)(2,1)S(1)} async-done(((bf16[32,32,256]{2,1,0:T(8,128)(2,1)}), bf16[32,32,256]{2,1,0:T(8,128)(2,1)S(1)}, u32[]{:S(2)}, u32[]{:S(2)}) %all-to-all-start.2) | async-done | bytes 524320 | tf_op jit(solution)/shard_map/all_to_all | solution.py:281
  20.8 6.0 %all-to-all-start = ((bf16[32,32,2048]{2,1,0:T(8,128)(2,1)}), bf16[32,32,2048]{2,1,0:T(8,128)(2,1)}, u32[]{:S(2)}, u32[]{:S(2)}) async-start(bf16[32,32,2048]{2,1,0:T(8,128)(2,1)} %bitcast.24), calls=%async_computation | async-start | bytes 8388608 | tf_op jit(solution)/shard_map/all_to_all | solution.py:285
  27.0 5.9 %collective-permute-start.10 = (bf16[576,256]{1,0:T(8,128)(2,1)S(1)}, bf16[576,256]{1,0:T(8,128)(2,1)S(1)}, u32[]{:S(2)}, u32[]{:S(2)}) collective-permute-start(bf16[576,256]{1,0:T(8,128)(2,1)S(1)} %pad_maximum_fusion.2.refs_8_.refs_0_), channel_id=1, source_target_pairs={{0,7},{1,0},{2,1},{3,2},{4,3},{5,4},{6,5},{7,6},{8,15},{9,8},{10,9... | collective-permute-start | bytes 884744 | tf_op jit(solution)/shard_map/ppermute | solution.py:200
  33.1 6.3 %collective-permute-done.10.refs_15_.refs_7_ = bf16[576,256]{1,0:T(8,128)(2,1)S(1)} collective-permute-done((bf16[576,256]{1,0:T(8,128)(2,1)S(1)}, bf16[576,256]{1,0:T(8,128)(2,1)S(1)}, u32[]{:S(2)}, u32[]{:S(2)}) %collective-permute-start.10) | collective-permute-done | bytes 294944 | tf_op jit(solution)/shard_map/ppermute | solution.py:200
  39.5 3.7 %collective-permute-start.11 = (bf16[576,256]{1,0:T(8,128)(2,1)S(1)}, bf16[576,256]{1,0:T(8,128)(2,1)S(1)}, u32[]{:S(2)}, u32[]{:S(2)}) collective-permute-start(bf16[576,256]{1,0:T(8,128)(2,1)S(1)} %collective-permute-done.10.refs_15_.refs_7_), channel_id=1, source_target_pairs={{0,7},{1,0},{2,1},{3,2},{4,3},{5,4},{6,5},{7,6},{8,15},{9,8},{10,9... | collective-permute-start | bytes 884744 | tf_op jit(solution)/shard_map/ppermute | solution.py:200
  43.2 0.9 collective-permute-done.refs_1_
  44.1 1.1 collective-permute-start.1
  45.2 33.2 %all-to-all-done = bf16[32,32,2048]{2,1,0:T(8,128)(2,1)} async-done(((bf16[32,32,2048]{2,1,0:T(8,128)(2,1)}), bf16[32,32,2048]{2,1,0:T(8,128)(2,1)}, u32[]{:S(2)}, u32[]{:S(2)}) %all-to-all-start) | async-done | bytes 4194336 | tf_op jit(solution)/shard_map/all_to_all | solution.py:285
  78.4 8.0 %forward.1 = (f32[1024,176]{1,0:T(8,128)}, f32[1024,176]{1,0:T(8,128)}, bf16[1024,176]{1,0:T(8,128)(2,1)}, bf16[1024,2048]{1,0:T(8,128)(2,1)}) custom-call(s32[1]{0:T(128)} %bitcast.1.e_ref, bf16[1024,2048]{1,0:T(8,128)(2,1)} %bitcast.5.x_ref, bf16[176,2048]{1,0:T(8,128)(2,1)} %bitcast.26, bf16[176,2048]{1,0:T(8,128)(2,1)} %bitcast.29, ...), custom_call_target="tpu_custom_call" | custom-call | flops 2214592512 | bytes 8388608 | tf_op jit(solution)/shard_map/forward/pallas_call | solution.py:307
  86.4 7.3 %all-to-all-start.1 = ((bf16[32,32,2048]{2,1,0:T(8,128)(2,1)}), bf16[32,32,2048]{2,1,0:T(8,128)(2,1)}, u32[]{:S(2)}, u32[]{:S(2)}) async-start(bf16[32,32,2048]{2,1,0:T(8,128)(2,1)} %bitcast.25), calls=%async_computation.1 | async-start | bytes 8388608 | tf_op jit(solution)/shard_map/all_to_all | solution.py:327
  93.8 2.0 collective-permute-start.8
  95.8 4.0 %collective-permute-start.12 = (bf16[576,256]{1,0:T(8,128)(2,1)S(1)}, bf16[576,256]{1,0:T(8,128)(2,1)S(1)}, u32[]{:S(2)}, u32[]{:S(2)}) collective-permute-start(bf16[576,256]{1,0:T(8,128)(2,1)S(1)} %collective-permute-done.11.refs_14_.refs_6_), channel_id=1, source_target_pairs={{0,7},{1,0},{2,1},{3,2},{4,3},{5,4},{6,5},{7,6},{8,15},{9,8},{10,9... | collective-permute-start | bytes 884744 | tf_op jit(solution)/shard_map/ppermute | solution.py:200
  99.8 1.9 collective-permute-start.5
  101.9 5.7 %collective-permute-done.8.refs_10_.refs_2_ = bf16[576,256]{1,0:T(8,128)(2,1)S(1)} collective-permute-done((bf16[576,256]{1,0:T(8,128)(2,1)S(1)}, bf16[576,256]{1,0:T(8,128)(2,1)S(1)}, u32[]{:S(2)}, u32[]{:S(2)}) %collective-permute-start.8) | collective-permute-done | bytes 294944 | tf_op jit(solution)/shard_map/ppermute | solution.py:200
  107.6 3.3 %collective-permute-start.13 = (bf16[576,256]{1,0:T(8,128)(2,1)S(1)}, bf16[576,256]{1,0:T(8,128)(2,1)S(1)}, u32[]{:S(2)}, u32[]{:S(2)}) collective-permute-start(bf16[576,256]{1,0:T(8,128)(2,1)S(1)} %collective-permute-done.12.refs_13_.refs_5_), channel_id=1, source_target_pairs={{0,7},{1,0},{2,1},{3,2},{4,3},{5,4},{6,5},{7,6},{8,15},{9,8},{10,9... | collective-permute-start | bytes 884744 | tf_op jit(solution)/shard_map/ppermute | solution.py:200
  110.9 2.6 %collective-permute-done.5.refs_6_ = bf16[576,256]{1,0:T(8,128)(2,1)S(1)} collective-permute-done((bf16[576,256]{1,0:T(8,128)(2,1)S(1)}, bf16[576,256]{1,0:T(8,128)(2,1)S(1)}, u32[]{:S(2)}, u32[]{:S(2)}) %collective-permute-start.5) | collective-permute-done | bytes 294944 | tf_op jit(solution)/shard_map/ppermute | solution.py:200
  113.5 3.7 %collective-permute-start.6 = (bf16[576,256]{1,0:T(8,128)(2,1)S(1)}, bf16[576,256]{1,0:T(8,128)(2,1)}, u32[]{:S(2)}, u32[]{:S(2)}) collective-permute-start(bf16[576,256]{1,0:T(8,128)(2,1)S(1)} %collective-permute-done.5.refs_6_), channel_id=1, source_target_pairs={{0,7},{1,0},{2,1},{3,2},{4,3},{5,4},{6,5},{7,6},{8,15},{9,8},{10,9... | collective-permute-start | bytes 884744 | tf_op jit(solution)/shard_map/ppermute | solution.py:200
  117.2 2.8 %collective-permute-done.9.refs_11_.refs_3_ = bf16[576,256]{1,0:T(8,128)(2,1)S(1)} collective-permute-done((bf16[576,256]{1,0:T(8,128)(2,1)S(1)}, bf16[576,256]{1,0:T(8,128)(2,1)S(1)}, u32[]{:S(2)}, u32[]{:S(2)}) %collective-permute-start.9) | collective-permute-done | bytes 294944 | tf_op jit(solution)/shard_map/ppermute | solution.py:200
  120.0 0.7 copy-done.13
  120.8 6.3 %backward.3 = (bf16[512,176]{1,0:T(8,128)(2,1)}, bf16[512,176]{1,0:T(8,128)(2,1)}, bf16[512,256]{1,0:T(8,128)(2,1)}, bf16[512,256]{1,0:T(8,128)(2,1)}, bf16[512,...) custom-call(s32[1]{0:T(128)} %bitcast.col_ref.z_ref, ...), custom_call_target="tpu_custom_call" | custom-call | flops 1107296256 | bytes 4194304 | tf_op jit(solution)/shard_map/backward/pallas_call | solution.py:338
  127.1 3.5 %collective-permute-start.24 = (bf16[512,256]{1,0:T(8,128)(2,1)}, bf16[512,256]{1,0:T(8,128)(2,1)S(1)}, u32[]{:S(2)}, u32[]{:S(2)}) collective-permute-start(bf16[512,256]{1,0:T(8,128)(2,1)} %get-tuple-element.57), channel_id=1, source_target_pairs={{0,7},{1,0},{2,1},{3,2},{4,3},{5,4},{6,5},{7,6},{8,15},{9,8},{10,9... | collective-permute-start | bytes 786440 | tf_op jit(solution)/shard_map/ppermute | solution.py:200
  130.7 6.4 %backward.2 = (bf16[512,176]{1,0:T(8,128)(2,1)}, bf16[512,176]{1,0:T(8,128)(2,1)}, bf16[512,256]{1,0:T(8,128)(2,1)}, bf16[512,256]{1,0:T(8,128)(2,1)}, bf16[512,...) custom-call(s32[1]{0:T(128)} %bitcast.col_ref.z_ref, ...), custom_call_target="tpu_custom_call" | custom-call | flops 1107296256 | bytes 4194304 | tf_op jit(solution)/shard_map/backward/pallas_call | solution.py:338
  137.1 3.3 %collective-permute-start.18 = (bf16[512,256]{1,0:T(8,128)(2,1)}, bf16[512,256]{1,0:T(8,128)(2,1)S(1)}, u32[]{:S(2)}, u32[]{:S(2)}) collective-permute-start(bf16[512,256]{1,0:T(8,128)(2,1)} %get-tuple-element.50), channel_id=1, source_target_pairs={{0,7},{1,0},{2,1},{3,2},{4,3},{5,4},{6,5},{7,6},{8,15},{9,8},{10,9... | collective-permute-start | bytes 786440 | tf_op jit(solution)/shard_map/ppermute | solution.py:200
  140.5 3.3 %collective-permute-start.25 = (bf16[512,256]{1,0:T(8,128)(2,1)S(1)}, bf16[512,256]{1,0:T(8,128)(2,1)S(1)}, u32[]{:S(2)}, u32[]{:S(2)}) collective-permute-start(bf16[512,256]{1,0:T(8,128)(2,1)S(1)} %add_convert_fusion.3), channel_id=1, source_target_pairs={{0,7},{1,0},{2,1},{3,2},{4,3},{5,4},{6,5},{7,6},{8,15},{9,8},{10,9... | collective-permute-start | bytes 786440 | tf_op jit(solution)/shard_map/ppermute | solution.py:200
  144.0 3.5 %collective-permute-done.18 = bf16[512,256]{1,0:T(8,128)(2,1)S(1)} collective-permute-done((bf16[512,256]{1,0:T(8,128)(2,1)}, bf16[512,256]{1,0:T(8,128)(2,1)S(1)}, u32[]{:S(2)}, u32[]{:S(2)}) %collective-permute-start.18) | collective-permute-done | bytes 262176 | tf_op jit(solution)/shard_map/ppermute | solution.py:200
  147.4 1.0 add_convert_fusion.8
  148.4 3.7 %collective-permute-start.19 = (bf16[512,256]{1,0:T(8,128)(2,1)S(1)}, bf16[512,256]{1,0:T(8,128)(2,1)S(1)}, u32[]{:S(2)}, u32[]{:S(2)}) collective-permute-start(bf16[512,256]{1,0:T(8,128)(2,1)S(1)} %add_convert_fusion.8), channel_id=1, source_target_pairs={{0,7},{1,0},{2,1},{3,2},{4,3},{5,4},{6,5},{7,6},{8,15},{9,8},{10,9... | collective-permute-start | bytes 786440 | tf_op jit(solution)/shard_map/ppermute | solution.py:200
  152.1 1.0 add_convert_fusion.11
  153.3 3.7 %collective-permute-start.26 = (bf16[512,256]{1,0:T(8,128)(2,1)S(1)}, bf16[512,256]{1,0:T(8,128)(2,1)S(1)}, u32[]{:S(2)}, u32[]{:S(2)}) collective-permute-start(bf16[512,256]{1,0:T(8,128)(2,1)S(1)} %add_convert_fusion.2), channel_id=1, source_target_pairs={{0,7},{1,0},{2,1},{3,2},{4,3},{5,4},{6,5},{7,6},{8,15},{9,8},{10,9... | collective-permute-start | bytes 786440 | tf_op jit(solution)/shard_map/ppermute | solution.py:200
  157.2 6.4 %collective-permute-done.15 = bf16[512,256]{1,0:T(8,128)(2,1)S(1)} collective-permute-done((bf16[512,256]{1,0:T(8,128)(2,1)S(1)}, bf16[512,256]{1,0:T(8,128)(2,1)S(1)}, u32[]{:S(2)}, u32[]{:S(2)}) %collective-permute-start.15) | collective-permute-done | bytes 262176 | tf_op jit(solution)/shard_map/ppermute | solution.py:200
  163.8 3.3 %collective-permute-start.27 = (bf16[512,256]{1,0:T(8,128)(2,1)S(1)}, bf16[512,256]{1,0:T(8,128)(2,1)S(1)}, u32[]{:S(2)}, u32[]{:S(2)}) collective-permute-start(bf16[512,256]{1,0:T(8,128)(2,1)S(1)} %add_convert_fusion.1), channel_id=1, source_target_pairs={{0,7},{1,0},{2,1},{3,2},{4,3},{5,4},{6,5},{7,6},{8,15},{9,8},{10,9... | collective-permute-start | bytes 786440 | tf_op jit(solution)/shard_map/ppermute | solution.py:200
  167.3 5.7 %collective-permute-done.16 = bf16[512,256]{1,0:T(8,128)(2,1)S(1)} collective-permute-done((bf16[512,256]{1,0:T(8,128)(2,1)S(1)}, bf16[512,256]{1,0:T(8,128)(2,1)S(1)}, u32[]{:S(2)}, u32[]{:S(2)}) %collective-permute-start.16) | collective-permute-done | bytes 262176 | tf_op jit(solution)/shard_map/ppermute | solution.py:200
  173.8 6.9 %collective-permute-done.17 = bf16[512,256]{1,0:T(8,128)(2,1)S(1)} collective-permute-done((bf16[512,256]{1,0:T(8,128)(2,1)S(1)}, bf16[512,256]{1,0:T(8,128)(2,1)S(1)}, u32[]{:S(2)}, u32[]{:S(2)}) %collective-permute-start.17) | collective-permute-done | bytes 262176 | tf_op jit(solution)/shard_map/ppermute | solution.py:200
  180.8 0.8 pad_maximum_fusion
  181.7 7.5 %all-to-all-start.4 = ((bf16[32,32,256]{2,1,0:T(8,128)(2,1)}), bf16[32,32,256]{2,1,0:T(8,128)(2,1)S(1)}, u32[]{:S(2)}, u32[]{:S(2)}) async-start(bf16[32,32,256]{2,1,0:T(8,128)(2,1)} %bitcast.14), calls=%async_computation.4 | async-start | bytes 1048576 | tf_op jit(solution)/shard_map/all_to_all | solution.py:412
  189.2 0.7 copy.16.re_ref
  189.9 0.7 copy.17.rw_ref
  190.7 2.3 %home.1 = (bf16[128,1024]{1,0:T(8,128)(2,1)}, bf16[256,1024]{1,0:T(8,128)(2,1)}) custom-call(s32[128,4]{1,0:T(8,128)} %copy.16.re_ref, f32[128,4]{1,0:T(8,128)} %copy.17.rw_ref), custom_call_target="tpu_custom_call" | custom-call | flops 25165824 | bytes 786432 | tf_op jit(solution)/shard_map/home/pallas_call | solution.py:294
  193.0 9.0 %combine.1 = bf16[8,136,256]{2,1,0:T(8,128)(2,1)} custom-call(s32[1]{0:T(128)} %bitcast.col_ref.z_ref, bf16[1024,2048]{1,0:T(8,128)(2,1)} %bitcast.10.y_ref, bf16[128,1024]{1,0:T(8,128)(2,1)} %get-tuple-element.40.mt_ref, bf16[256,1024]{1,0:T(8,128)(2,1)} %get-tuple-element.41.mw_ref, s32[4,128]{1,0:T(4,128)} %bitcast.41, bf16[576,256]{1,0:T(8,128)(2,1)} %copy-done.2, ...), custom_call_target="tpu_custom_call" | custom-call | flops 1610612736 | bytes 4194304 | tf_op jit(solution)/shard_map/combine/pallas_call | solution.py:381
  202.0 5.2 %all-to-all-start.3 = ((bf16[8,136,256]{2,1,0:T(8,128)(2,1)}), bf16[8,136,256]{2,1,0:T(8,128)(2,1)S(1)}, u32[]{:S(2)}, u32[]{:S(2)}) async-start(bf16[8,136,256]{2,1,0:T(8,128)(2,1)} %combine.1), calls=%async_computation.3 | async-start | bytes 1114112 | tf_op jit(solution)/shard_map/all_to_all | solution.py:400
  207.1 4.5 %down.1 = f32[176,2048]{1,0:T(8,128)} custom-call(s32[1]{0:T(128)} %bitcast.col_ref.z_ref, bf16[1024,176]{1,0:T(8,128)(2,1)} %get-tuple-element.69.h_ref, bf16[576,256]{1,0:T(8,128)(2,1)} %copy-done.2, bf16[576,256]{1,0:T(8,128)(2,1)} %copy-done.4, bf16[576,256]{1,0:T(8,128)(2,1)} %copy-done.8, bf16[576,256]{1,0:T(8,128)(2,1)} %copy-done.12, ...), custom_call_target="tpu_custom_call" | custom-call | flops 738197504 | bytes 5636096 | tf_op jit(solution)/shard_map/down/pallas_call | solution.py:367
  211.6 8.4 %weight.1 = (f32[176,2048]{1,0:T(8,128)}, f32[176,2048]{1,0:T(8,128)}) custom-call(bf16[1024,2048]{1,0:T(8,128)(2,1)} %bitcast.5.x_ref, bf16[512,176]{1,0:T(8,128)(2,1)} %get-tuple-element.63.refs_0_, bf16[512,176]{1,0:T(8,128)(2,1)} %get-tuple-element.64.refs_1_, bf16[512,176]{1,0:T(8,128)(2,1)} %get-tuple-element.65.refs_2_, ...), custom_call_target="tpu_custom_call" | custom-call | flops 1476395008 | bytes 7077888 | tf_op jit(solution)/shard_map/weight/pallas_call | solution.py:358
  220.1 0.9 convolution_convert_fusion
  220.9 4.6 %all-to-all-done.3.x_ref = bf16[8,136,256]{2,1,0:T(8,128)(2,1)S(1)} async-done(((bf16[8,136,256]{2,1,0:T(8,128)(2,1)}), bf16[8,136,256]{2,1,0:T(8,128)(2,1)S(1)}, u32[]{:S(2)}, u32[]{:S(2)}) %all-to-all-start.3) | async-done | bytes 557088 | tf_op jit(solution)/shard_map/all_to_all | solution.py:400
  225.6 0.7 mixed.1
  (106 shorter events, 2.4 us)
Async XLA Ops:
  2.8 18.0 %all-to-all-start.2 = ((bf16[32,32,256]{2,1,0:T(8,128)(2,1)}), bf16[32,32,256]{2,1,0:T(8,128)(2,1)S(1)}, u32[]{:S(2)}, u32[]{:S(2)}) async-start(bf16[32,32,256]{2,1,0:T(8,128)(2,1)} %bitcast.39), calls=%async_computation.2 | async-start | bytes 1048576 | tf_op jit(solution)/shard_map/all_to_all | solution.py:281
  20.8 57.6 %all-to-all-start = ((bf16[32,32,2048]{2,1,0:T(8,128)(2,1)}), bf16[32,32,2048]{2,1,0:T(8,128)(2,1)}, u32[]{:S(2)}, u32[]{:S(2)}) async-start(bf16[32,32,2048]{2,1,0:T(8,128)(2,1)} %bitcast.24), calls=%async_computation | async-start | bytes 8388608 | tf_op jit(solution)/shard_map/all_to_all | solution.py:285
  27.0 59.5 %copy-start.1 = (bf16[576,256]{1,0:T(8,128)(2,1)}, bf16[576,256]{1,0:T(8,128)(2,1)S(1)}, u32[]{:S(2)}) copy-start(bf16[576,256]{1,0:T(8,128)(2,1)S(1)} %pad_maximum_fusion.2.refs_8_.refs_0_) | copy-start | bytes 884740
  27.0 12.5 %collective-permute-start.10 = (bf16[576,256]{1,0:T(8,128)(2,1)S(1)}, bf16[576,256]{1,0:T(8,128)(2,1)S(1)}, u32[]{:S(2)}, u32[]{:S(2)}) collective-permute-start(bf16[576,256]{1,0:T(8,128)(2,1)S(1)} %pad_maximum_fusion.2.refs_8_.refs_0_), channel_id=1, source_target_pairs={{0,7},{1,0},{2,1},{3,2},{4,3},{5,4},{6,5},{7,6},{8,15},{9,8},{10,9... | collective-permute-start | bytes 884744 | tf_op jit(solution)/shard_map/ppermute | solution.py:200
  32.9 53.5 %copy-start.2 = (bf16[576,256]{1,0:T(8,128)(2,1)}, bf16[576,256]{1,0:T(8,128)(2,1)S(1)}, u32[]{:S(2)}) copy-start(bf16[576,256]{1,0:T(8,128)(2,1)S(1)} %pad_maximum_fusion.1.refs_0_) | copy-start | bytes 884740
  32.9 11.2 %collective-permute-start = (bf16[576,256]{1,0:T(8,128)(2,1)S(1)}, bf16[576,256]{1,0:T(8,128)(2,1)S(1)}, u32[]{:S(2)}, u32[]{:S(2)}) collective-permute-start(bf16[576,256]{1,0:T(8,128)(2,1)S(1)} %pad_maximum_fusion.1.refs_0_), channel_id=1, source_target_pairs={{0,1},{1,2},{2,3},{3,4},{4,5},{5,6},{6,7},{7,0},{8,9},{9,10},{10,1... | collective-permute-start | bytes 884744 | tf_op jit(solution)/shard_map/ppermute | solution.py:200
  33.0 60.7 %collective-permute-start.7 = (bf16[576,256]{1,0:T(8,128)(2,1)S(1)}, bf16[576,256]{1,0:T(8,128)(2,1)S(1)}, u32[]{:S(2)}, u32[]{:S(2)}) collective-permute-start(bf16[576,256]{1,0:T(8,128)(2,1)S(1)} %pad_maximum_fusion.2.refs_8_.refs_0_), channel_id=1, source_target_pairs={{0,1},{1,2},{2,3},{3,4},{4,5},{5,6},{6,7},{7,0},{8,9},{9,10},{10,1... | collective-permute-start | bytes 884744 | tf_op jit(solution)/shard_map/ppermute | solution.py:200
  39.4 47.0 %copy-start.3 = (bf16[576,256]{1,0:T(8,128)(2,1)}, bf16[576,256]{1,0:T(8,128)(2,1)S(1)}, u32[]{:S(2)}) copy-start(bf16[576,256]{1,0:T(8,128)(2,1)S(1)} %collective-permute-done.10.refs_15_.refs_7_) | copy-start | bytes 884740
  39.5 56.3 %collective-permute-start.11 = (bf16[576,256]{1,0:T(8,128)(2,1)S(1)}, bf16[576,256]{1,0:T(8,128)(2,1)S(1)}, u32[]{:S(2)}, u32[]{:S(2)}) collective-permute-start(bf16[576,256]{1,0:T(8,128)(2,1)S(1)} %collective-permute-done.10.refs_15_.refs_7_), channel_id=1, source_target_pairs={{0,7},{1,0},{2,1},{3,2},{4,3},{5,4},{6,5},{7,6},{8,15},{9,8},{10,9... | collective-permute-start | bytes 884744 | tf_op jit(solution)/shard_map/ppermute | solution.py:200
  43.1 56.7 %collective-permute-start.4 = (bf16[576,256]{1,0:T(8,128)(2,1)S(1)}, bf16[576,256]{1,0:T(8,128)(2,1)S(1)}, u32[]{:S(2)}, u32[]{:S(2)}) collective-permute-start(bf16[576,256]{1,0:T(8,128)(2,1)S(1)} %pad_maximum_fusion.1.refs_0_), channel_id=1, source_target_pairs={{0,7},{1,0},{2,1},{3,2},{4,3},{5,4},{6,5},{7,6},{8,15},{9,8},{10,9... | collective-permute-start | bytes 884744 | tf_op jit(solution)/shard_map/ppermute | solution.py:200
  44.1 42.3 %copy-start.4 = (bf16[576,256]{1,0:T(8,128)(2,1)}, bf16[576,256]{1,0:T(8,128)(2,1)S(1)}, u32[]{:S(2)}) copy-start(bf16[576,256]{1,0:T(8,128)(2,1)S(1)} %collective-permute-done.refs_1_) | copy-start | bytes 884740
  44.1 57.7 %collective-permute-start.1 = (bf16[576,256]{1,0:T(8,128)(2,1)S(1)}, bf16[576,256]{1,0:T(8,128)(2,1)S(1)}, u32[]{:S(2)}, u32[]{:S(2)}) collective-permute-start(bf16[576,256]{1,0:T(8,128)(2,1)S(1)} %collective-permute-done.refs_1_), channel_id=1, source_target_pairs={{0,1},{1,2},{2,3},{3,4},{4,5},{5,6},{6,7},{7,0},{8,9},{9,10},{10,1... | collective-permute-start | bytes 884744 | tf_op jit(solution)/shard_map/ppermute | solution.py:200
  86.4 95.2 %all-to-all-start.1 = ((bf16[32,32,2048]{2,1,0:T(8,128)(2,1)}), bf16[32,32,2048]{2,1,0:T(8,128)(2,1)}, u32[]{:S(2)}, u32[]{:S(2)}) async-start(bf16[32,32,2048]{2,1,0:T(8,128)(2,1)} %bitcast.25), calls=%async_computation.1 | async-start | bytes 8388608 | tf_op jit(solution)/shard_map/all_to_all | solution.py:327
  93.8 13.8 %collective-permute-start.8 = (bf16[576,256]{1,0:T(8,128)(2,1)S(1)}, bf16[576,256]{1,0:T(8,128)(2,1)S(1)}, u32[]{:S(2)}, u32[]{:S(2)}) collective-permute-start(bf16[576,256]{1,0:T(8,128)(2,1)S(1)} %collective-permute-done.7.refs_9_.refs_1_), channel_id=1, source_target_pairs={{0,1},{1,2},{2,3},{3,4},{4,5},{5,6},{6,7},{7,0},{8,9},{9,10},{10,1... | collective-permute-start | bytes 884744 | tf_op jit(solution)/shard_map/ppermute | solution.py:200
  95.8 11.8 %collective-permute-start.12 = (bf16[576,256]{1,0:T(8,128)(2,1)S(1)}, bf16[576,256]{1,0:T(8,128)(2,1)S(1)}, u32[]{:S(2)}, u32[]{:S(2)}) collective-permute-start(bf16[576,256]{1,0:T(8,128)(2,1)S(1)} %collective-permute-done.11.refs_14_.refs_6_), channel_id=1, source_target_pairs={{0,7},{1,0},{2,1},{3,2},{4,3},{5,4},{6,5},{7,6},{8,15},{9,8},{10,9... | collective-permute-start | bytes 884744 | tf_op jit(solution)/shard_map/ppermute | solution.py:200
  99.8 30.8 %copy-start.7 = (bf16[576,256]{1,0:T(8,128)(2,1)}, bf16[576,256]{1,0:T(8,128)(2,1)S(1)}, u32[]{:S(2)}) copy-start(bf16[576,256]{1,0:T(8,128)(2,1)S(1)} %collective-permute-done.4.refs_7_) | copy-start | bytes 884740
  99.8 13.7 %collective-permute-start.5 = (bf16[576,256]{1,0:T(8,128)(2,1)S(1)}, bf16[576,256]{1,0:T(8,128)(2,1)S(1)}, u32[]{:S(2)}, u32[]{:S(2)}) collective-permute-start(bf16[576,256]{1,0:T(8,128)(2,1)S(1)} %collective-permute-done.4.refs_7_), channel_id=1, source_target_pairs={{0,7},{1,0},{2,1},{3,2},{4,3},{5,4},{6,5},{7,6},{8,15},{9,8},{10,9... | collective-permute-start | bytes 884744 | tf_op jit(solution)/shard_map/ppermute | solution.py:200
  101.8 28.9 %copy-start.8 = (bf16[576,256]{1,0:T(8,128)(2,1)}, bf16[576,256]{1,0:T(8,128)(2,1)S(1)}, u32[]{:S(2)}) copy-start(bf16[576,256]{1,0:T(8,128)(2,1)S(1)} %collective-permute-done.1.refs_2_) | copy-start | bytes 884740
  101.8 15.5 %collective-permute-start.2 = (bf16[576,256]{1,0:T(8,128)(2,1)S(1)}, bf16[576,256]{1,0:T(8,128)(2,1)S(1)}, u32[]{:S(2)}, u32[]{:S(2)}) collective-permute-start(bf16[576,256]{1,0:T(8,128)(2,1)S(1)} %collective-permute-done.1.refs_2_), channel_id=1, source_target_pairs={{0,1},{1,2},{2,3},{3,4},{4,5},{5,6},{6,7},{7,0},{8,9},{9,10},{10,1... | collective-permute-start | bytes 884744 | tf_op jit(solution)/shard_map/ppermute | solution.py:200
  107.6 12.4 %collective-permute-start.9 = (bf16[576,256]{1,0:T(8,128)(2,1)S(1)}, bf16[576,256]{1,0:T(8,128)(2,1)S(1)}, u32[]{:S(2)}, u32[]{:S(2)}) collective-permute-start(bf16[576,256]{1,0:T(8,128)(2,1)S(1)} %collective-permute-done.8.refs_10_.refs_2_), channel_id=1, source_target_pairs={{0,1},{1,2},{2,3},{3,4},{4,5},{5,6},{6,7},{7,0},{8,9},{9,10},{10,1... | collective-permute-start | bytes 884744 | tf_op jit(solution)/shard_map/ppermute | solution.py:200
  107.6 12.4 %collective-permute-start.13 = (bf16[576,256]{1,0:T(8,128)(2,1)S(1)}, bf16[576,256]{1,0:T(8,128)(2,1)S(1)}, u32[]{:S(2)}, u32[]{:S(2)}) collective-permute-start(bf16[576,256]{1,0:T(8,128)(2,1)S(1)} %collective-permute-done.12.refs_13_.refs_5_), channel_id=1, source_target_pairs={{0,7},{1,0},{2,1},{3,2},{4,3},{5,4},{6,5},{7,6},{8,15},{9,8},{10,9... | collective-permute-start | bytes 884744 | tf_op jit(solution)/shard_map/ppermute | solution.py:200
  113.5 17.1 %collective-permute-start.6 = (bf16[576,256]{1,0:T(8,128)(2,1)S(1)}, bf16[576,256]{1,0:T(8,128)(2,1)}, u32[]{:S(2)}, u32[]{:S(2)}) collective-permute-start(bf16[576,256]{1,0:T(8,128)(2,1)S(1)} %collective-permute-done.5.refs_6_), channel_id=1, source_target_pairs={{0,7},{1,0},{2,1},{3,2},{4,3},{5,4},{6,5},{7,6},{8,15},{9,8},{10,9... | collective-permute-start | bytes 884744 | tf_op jit(solution)/shard_map/ppermute | solution.py:200
  117.2 13.4 %collective-permute-start.3 = (bf16[576,256]{1,0:T(8,128)(2,1)S(1)}, bf16[576,256]{1,0:T(8,128)(2,1)}, u32[]{:S(2)}, u32[]{:S(2)}) collective-permute-start(bf16[576,256]{1,0:T(8,128)(2,1)S(1)} %collective-permute-done.2.refs_3_), channel_id=1, source_target_pairs={{0,1},{1,2},{2,3},{3,4},{4,5},{5,6},{6,7},{7,0},{8,9},{9,10},{10,1... | collective-permute-start | bytes 884744 | tf_op jit(solution)/shard_map/ppermute | solution.py:200
  127.1 13.3 %collective-permute-start.24 = (bf16[512,256]{1,0:T(8,128)(2,1)}, bf16[512,256]{1,0:T(8,128)(2,1)S(1)}, u32[]{:S(2)}, u32[]{:S(2)}) collective-permute-start(bf16[512,256]{1,0:T(8,128)(2,1)} %get-tuple-element.57), channel_id=1, source_target_pairs={{0,7},{1,0},{2,1},{3,2},{4,3},{5,4},{6,5},{7,6},{8,15},{9,8},{10,9... | collective-permute-start | bytes 786440 | tf_op jit(solution)/shard_map/ppermute | solution.py:200
  130.6 26.4 %copy-start.19 = (bf16[512,256]{1,0:T(8,128)(2,1)S(1)}, bf16[512,256]{1,0:T(8,128)(2,1)}, u32[]{:S(2)}) copy-start(bf16[512,256]{1,0:T(8,128)(2,1)} %get-tuple-element.56) | copy-start | bytes 786436
  130.6 13.2 %collective-permute-start.21 = (bf16[512,256]{1,0:T(8,128)(2,1)}, bf16[512,256]{1,0:T(8,128)(2,1)S(1)}, u32[]{:S(2)}, u32[]{:S(2)}) collective-permute-start(bf16[512,256]{1,0:T(8,128)(2,1)} %get-tuple-element.54), channel_id=1, source_target_pairs={{0,1},{1,2},{2,3},{3,4},{4,5},{5,6},{6,7},{7,0},{8,9},{9,10},{10,1... | collective-permute-start | bytes 786440 | tf_op jit(solution)/shard_map/ppermute | solution.py:200
  137.1 26.5 %copy-start.21 = (bf16[512,256]{1,0:T(8,128)(2,1)S(1)}, bf16[512,256]{1,0:T(8,128)(2,1)}, u32[]{:S(2)}) copy-start(bf16[512,256]{1,0:T(8,128)(2,1)} %get-tuple-element.48) | copy-start | bytes 786436
  137.1 26.7 %copy-start.16 = (bf16[512,256]{1,0:T(8,128)(2,1)S(1)}, bf16[512,256]{1,0:T(8,128)(2,1)}, u32[]{:S(2)}) copy-start(bf16[512,256]{1,0:T(8,128)(2,1)} %get-tuple-element.60) | copy-start | bytes 786436
  137.1 30.0 %copy-start.18 = (bf16[512,256]{1,0:T(8,128)(2,1)S(1)}, bf16[512,256]{1,0:T(8,128)(2,1)}, u32[]{:S(2)}) copy-start(bf16[512,256]{1,0:T(8,128)(2,1)} %get-tuple-element.52) | copy-start | bytes 786436
  137.1 35.9 %copy-start.17 = (bf16[512,256]{1,0:T(8,128)(2,1)S(1)}, bf16[512,256]{1,0:T(8,128)(2,1)}, u32[]{:S(2)}) copy-start(bf16[512,256]{1,0:T(8,128)(2,1)} %get-tuple-element.49) | copy-start | bytes 786436
  137.1 36.1 %copy-start.25 = (bf16[512,256]{1,0:T(8,128)(2,1)S(1)}, bf16[512,256]{1,0:T(8,128)(2,1)}, u32[]{:S(2)}) copy-start(bf16[512,256]{1,0:T(8,128)(2,1)} %get-tuple-element.61) | copy-start | bytes 786436
  137.1 10.3 %collective-permute-start.18 = (bf16[512,256]{1,0:T(8,128)(2,1)}, bf16[512,256]{1,0:T(8,128)(2,1)S(1)}, u32[]{:S(2)}, u32[]{:S(2)}) collective-permute-start(bf16[512,256]{1,0:T(8,128)(2,1)} %get-tuple-element.50), channel_id=1, source_target_pairs={{0,7},{1,0},{2,1},{3,2},{4,3},{5,4},{6,5},{7,6},{8,15},{9,8},{10,9... | collective-permute-start | bytes 786440 | tf_op jit(solution)/shard_map/ppermute | solution.py:200
  140.4 11.7 %collective-permute-start.14 = (bf16[512,256]{1,0:T(8,128)(2,1)}, bf16[512,256]{1,0:T(8,128)(2,1)S(1)}, u32[]{:S(2)}, u32[]{:S(2)}) collective-permute-start(bf16[512,256]{1,0:T(8,128)(2,1)} %get-tuple-element.46), channel_id=1, source_target_pairs={{0,1},{1,2},{2,3},{3,4},{4,5},{5,6},{6,7},{7,0},{8,9},{9,10},{10,1... | collective-permute-start | bytes 786440 | tf_op jit(solution)/shard_map/ppermute | solution.py:200
  140.5 40.3 %copy-start.26 = (bf16[512,256]{1,0:T(8,128)(2,1)S(1)}, bf16[512,256]{1,0:T(8,128)(2,1)}, u32[]{:S(2)}) copy-start(bf16[512,256]{1,0:T(8,128)(2,1)} %get-tuple-element.53) | copy-start | bytes 786436
  140.5 12.7 %collective-permute-start.25 = (bf16[512,256]{1,0:T(8,128)(2,1)S(1)}, bf16[512,256]{1,0:T(8,128)(2,1)S(1)}, u32[]{:S(2)}, u32[]{:S(2)}) collective-permute-start(bf16[512,256]{1,0:T(8,128)(2,1)S(1)} %add_convert_fusion.3), channel_id=1, source_target_pairs={{0,7},{1,0},{2,1},{3,2},{4,3},{5,4},{6,5},{7,6},{8,15},{9,8},{10,9... | collective-permute-start | bytes 786440 | tf_op jit(solution)/shard_map/ppermute | solution.py:200
  143.9 13.1 %collective-permute-start.22 = (bf16[512,256]{1,0:T(8,128)(2,1)S(1)}, bf16[512,256]{1,0:T(8,128)(2,1)S(1)}, u32[]{:S(2)}, u32[]{:S(2)}) collective-permute-start(bf16[512,256]{1,0:T(8,128)(2,1)S(1)} %add_convert_fusion.5), channel_id=1, source_target_pairs={{0,1},{1,2},{2,3},{3,4},{4,5},{5,6},{6,7},{7,0},{8,9},{9,10},{10,1... | collective-permute-start | bytes 786440 | tf_op jit(solution)/shard_map/ppermute | solution.py:200
  148.4 18.7 %collective-permute-start.19 = (bf16[512,256]{1,0:T(8,128)(2,1)S(1)}, bf16[512,256]{1,0:T(8,128)(2,1)S(1)}, u32[]{:S(2)}, u32[]{:S(2)}) collective-permute-start(bf16[512,256]{1,0:T(8,128)(2,1)S(1)} %add_convert_fusion.8), channel_id=1, source_target_pairs={{0,7},{1,0},{2,1},{3,2},{4,3},{5,4},{6,5},{7,6},{8,15},{9,8},{10,9... | collective-permute-start | bytes 786440 | tf_op jit(solution)/shard_map/ppermute | solution.py:200
  153.1 10.5 %collective-permute-start.15 = (bf16[512,256]{1,0:T(8,128)(2,1)S(1)}, bf16[512,256]{1,0:T(8,128)(2,1)S(1)}, u32[]{:S(2)}, u32[]{:S(2)}) collective-permute-start(bf16[512,256]{1,0:T(8,128)(2,1)S(1)} %add_convert_fusion.11), channel_id=1, source_target_pairs={{0,1},{1,2},{2,3},{3,4},{4,5},{5,6},{6,7},{7,0},{8,9},{9,10},{10,1... | collective-permute-start | bytes 786440 | tf_op jit(solution)/shard_map/ppermute | solution.py:200
  153.3 35.9 %copy-start.27 = (s32[128,4]{0,1:T(4,128)S(1)}, s32[128,4]{0,1:T(4,128)}, u32[]{:S(2)}) copy-start(s32[128,4]{0,1:T(4,128)} %param.11) | copy-start | bytes 6148
  153.3 36.6 %copy-start.28 = (f32[128,4]{0,1:T(4,128)S(1)}, f32[128,4]{0,1:T(4,128)}, u32[]{:S(2)}) copy-start(f32[128,4]{0,1:T(4,128)} %param.12) | copy-start | bytes 6148
  153.3 10.4 %collective-permute-start.26 = (bf16[512,256]{1,0:T(8,128)(2,1)S(1)}, bf16[512,256]{1,0:T(8,128)(2,1)S(1)}, u32[]{:S(2)}, u32[]{:S(2)}) collective-permute-start(bf16[512,256]{1,0:T(8,128)(2,1)S(1)} %add_convert_fusion.2), channel_id=1, source_target_pairs={{0,7},{1,0},{2,1},{3,2},{4,3},{5,4},{6,5},{7,6},{8,15},{9,8},{10,9... | collective-permute-start | bytes 786440 | tf_op jit(solution)/shard_map/ppermute | solution.py:200
  157.1 16.1 %collective-permute-start.23 = (bf16[512,256]{1,0:T(8,128)(2,1)S(1)}, bf16[512,256]{1,0:T(8,128)(2,1)S(1)}, u32[]{:S(2)}, u32[]{:S(2)}) collective-permute-start(bf16[512,256]{1,0:T(8,128)(2,1)S(1)} %add_convert_fusion.4), channel_id=1, source_target_pairs={{0,1},{1,2},{2,3},{3,4},{4,5},{5,6},{6,7},{7,0},{8,9},{9,10},{10,1... | collective-permute-start | bytes 786440 | tf_op jit(solution)/shard_map/ppermute | solution.py:200
  163.6 9.3 %collective-permute-start.16 = (bf16[512,256]{1,0:T(8,128)(2,1)S(1)}, bf16[512,256]{1,0:T(8,128)(2,1)S(1)}, u32[]{:S(2)}, u32[]{:S(2)}) collective-permute-start(bf16[512,256]{1,0:T(8,128)(2,1)S(1)} %add_convert_fusion.10), channel_id=1, source_target_pairs={{0,1},{1,2},{2,3},{3,4},{4,5},{5,6},{6,7},{7,0},{8,9},{9,10},{10,1... | collective-permute-start | bytes 786440 | tf_op jit(solution)/shard_map/ppermute | solution.py:200
  163.8 9.3 %collective-permute-start.27 = (bf16[512,256]{1,0:T(8,128)(2,1)S(1)}, bf16[512,256]{1,0:T(8,128)(2,1)S(1)}, u32[]{:S(2)}, u32[]{:S(2)}) collective-permute-start(bf16[512,256]{1,0:T(8,128)(2,1)S(1)} %add_convert_fusion.1), channel_id=1, source_target_pairs={{0,7},{1,0},{2,1},{3,2},{4,3},{5,4},{6,5},{7,6},{8,15},{9,8},{10,9... | collective-permute-start | bytes 786440 | tf_op jit(solution)/shard_map/ppermute | solution.py:200
  167.2 6.6 %collective-permute-start.20 = (bf16[512,256]{1,0:T(8,128)(2,1)S(1)}, bf16[512,256]{1,0:T(8,128)(2,1)S(1)}, u32[]{:S(2)}, u32[]{:S(2)}) collective-permute-start(bf16[512,256]{1,0:T(8,128)(2,1)S(1)} %add_convert_fusion.7), channel_id=1, source_target_pairs={{0,7},{1,0},{2,1},{3,2},{4,3},{5,4},{6,5},{7,6},{8,15},{9,8},{10,9... | collective-permute-start | bytes 786440 | tf_op jit(solution)/shard_map/ppermute | solution.py:200
  173.1 7.7 %collective-permute-start.17 = (bf16[512,256]{1,0:T(8,128)(2,1)S(1)}, bf16[512,256]{1,0:T(8,128)(2,1)S(1)}, u32[]{:S(2)}, u32[]{:S(2)}) collective-permute-start(bf16[512,256]{1,0:T(8,128)(2,1)S(1)} %add_convert_fusion.9), channel_id=1, source_target_pairs={{0,1},{1,2},{2,3},{3,4},{4,5},{5,6},{6,7},{7,0},{8,9},{9,10},{10,1... | collective-permute-start | bytes 786440 | tf_op jit(solution)/shard_map/ppermute | solution.py:200
  181.7 20.3 %all-to-all-start.4 = ((bf16[32,32,256]{2,1,0:T(8,128)(2,1)}), bf16[32,32,256]{2,1,0:T(8,128)(2,1)S(1)}, u32[]{:S(2)}, u32[]{:S(2)}) async-start(bf16[32,32,256]{2,1,0:T(8,128)(2,1)} %bitcast.14), calls=%async_computation.4 | async-start | bytes 1048576 | tf_op jit(solution)/shard_map/all_to_all | solution.py:412
  202.0 23.6 %all-to-all-start.3 = ((bf16[8,136,256]{2,1,0:T(8,128)(2,1)}), bf16[8,136,256]{2,1,0:T(8,128)(2,1)S(1)}, u32[]{:S(2)}, u32[]{:S(2)}) async-start(bf16[8,136,256]{2,1,0:T(8,128)(2,1)} %combine.1), calls=%async_computation.3 | async-start | bytes 1114112 | tf_op jit(solution)/shard_map/all_to_all | solution.py:400
  (14 other events, 184.4 us)

commit v4 on v3

--- a/solution.py
+++ b/solution.py
@@ -184,7 +184,7 @@
     ug_ref[...] = dot(jnp.concatenate([r[...] for r in ui_refs], axis=0), x, TN)
 
 
-def down_kernel(parts, z_ref, h_ref, *refs):
+def down_kernel(parts, z_ref, h_ref, _, *refs):
     dg_ref = refs[-1]
     share = refs[0].shape[1]
     rows = h_ref.shape[0] // 2
@@ -291,6 +291,9 @@
         jnp.concatenate([cot_mine[rows:], cotangent[raw:]], axis=0),
     )
 
+    last = (out_grad[0][4], out_grad[0][5], out_grad[1][3], out_grad[1][4])
+    marker = add(*(o[:8, :128] for o in last))
+
     combine, weighted = pl.pallas_call(
         functools.partial(home_kernel, cap),
         name="home",
@@ -370,12 +373,12 @@
         grid_spec=pltpu.PrefetchScalarGridSpec(
             num_scalar_prefetch=1,
             grid=(1,),
-            in_specs=[full(slots, hid)] + [full(rows + raw, share)] * (2 * parts),
+            in_specs=[full(slots, hid), full(8, 128)] + [full(rows + raw, share)] * (2 * parts),
             out_specs=full(hid, width),
         ),
         out_shape=sds((hid, width), F32),
         cost_estimate=cost(2 * slots * width * hid, 2 * slots * width + 4 * hid * width),
-    )(col, h, *out_grad[0], *out_grad[1])
+    )(col, h, marker, *out_grad[0], *out_grad[1])
 
     tail = 8
     mixed_part = pl.pallas_call(

time: 228 us -> 229 us (level)
  no operation moved by 1% of the time
where the time goes in v4:
time: 229 us; the launch traced here: 227 us
  waiting for transfers between devices  83.6 us (37%)
  starting transfers between devices  81.1 us (35%)
  Pallas kernels  47.8 us (21%)
  matrix products  5.08 us (2%)
  other arithmetic  4.93 us (2%)
  local copies, waits for them, and re-layouts  3.83 us (2%)
    ppermute x28, starting transfers between devices, shift(): lax.ppermute(x, 'expert', [(i, (i + by) % size) for i in range(size)])  47.5 us
    ppermute x28, waiting for transfers between devices, shift(): lax.ppermute(x, 'expert', [(i, (i + by) % size) for i in range(size)])  40.9 us
    all_to_all x1, waiting for transfers between devices, step(): lax.all_to_all(tok_send.reshape(owners, cap, width), 'dp', split_axis=0,...  33.2 us
    pallas_call x2, Pallas kernels, step(): pl.pallas_call(functools.partial(backward_kernel, parts), name='backward'...  12.6 us
    pallas_call x1, Pallas kernels, step(): pl.pallas_call(functools.partial(combine_kernel, cap, parts), name='combi...  8.97 us
    pallas_call x1, Pallas kernels, step(): pl.pallas_call(weight_kernel, name='weight', grid=(parts,), in_specs=[pl....  8.43 us
    pallas_call x1, Pallas kernels, step(): pl.pallas_call(forward_kernel, name='forward', grid_spec=pltpu.PrefetchSc...  8.04 us
    all_to_all x1, starting transfers between devices, step(): lax.all_to_all(input_cols.reshape(owners, cap, share), 'dp', split_axis=0...  7.75 us
  transfers between devices with their start and end apart: 33, of which 13 were waited for; matrix products, arithmetic and copies ran while one was open for 5% of the time, Pallas kernels for 20%

profile of v4, /device:TPU:2, one launch (start us, length us, event | category | flops | bytes accessed | tf_op | source)
XLA Modules:
  0.0 227.4 jit_solution(11904446754792443934)
XLA Ops:
  0.7 2.2 route.1
  2.8 7.6 %all-to-all-start.2 = ((bf16[32,32,256]{2,1,0:T(8,128)(2,1)}), bf16[32,32,256]{2,1,0:T(8,128)(2,1)S(1)}, u32[]{:S(2)}, u32[]{:S(2)}) async-start(bf16[32,32,256]{2,1,0:T(8,128)(2,1)} %bitcast.39), calls=%async_computation.2 | async-start | bytes 1048576 | tf_op jit(solution)/shard_map/all_to_all | solution.py:281
  10.5 4.2 %fusion.2 = bf16[1024,2048]{1,0:T(8,128)(2,1)} fusion(bf16[1024,128]{1,0:T(8,128)(2,1)} %get-tuple-element.38, bf16[128,2048]{1,0:T(8,128)(2,1)S(1)} %copy-done), kind=kOutput, calls=%fused_computation.19 | convolution fusion | flops 536870912 | bytes 4980736 | tf_op jit(solution)/shard_map/dot_general | solution.py:284
  14.7 6.2 %all-to-all-done.2 = bf16[32,32,256]{2,1,0:T(8,128)(2,1)S(1)} async-done(((bf16[32,32,256]{2,1,0:T(8,128)(2,1)}), bf16[32,32,256]{2,1,0:T(8,128)(2,1)S(1)}, u32[]{:S(2)}, u32[]{:S(2)}) %all-to-all-start.2) | async-done | bytes 524320 | tf_op jit(solution)/shard_map/all_to_all | solution.py:281
  20.8 6.0 %all-to-all-start = ((bf16[32,32,2048]{2,1,0:T(8,128)(2,1)}), bf16[32,32,2048]{2,1,0:T(8,128)(2,1)}, u32[]{:S(2)}, u32[]{:S(2)}) async-start(bf16[32,32,2048]{2,1,0:T(8,128)(2,1)} %bitcast.24), calls=%async_computation | async-start | bytes 8388608 | tf_op jit(solution)/shard_map/all_to_all | solution.py:285
  27.0 5.9 %collective-permute-start.10 = (bf16[576,256]{1,0:T(8,128)(2,1)S(1)}, bf16[576,256]{1,0:T(8,128)(2,1)S(1)}, u32[]{:S(2)}, u32[]{:S(2)}) collective-permute-start(bf16[576,256]{1,0:T(8,128)(2,1)S(1)} %pad_maximum_fusion.2.refs_8_.refs_0_), channel_id=1, source_target_pairs={{0,7},{1,0},{2,1},{3,2},{4,3},{5,4},{6,5},{7,6},{8,15},{9,8},{10,9... | collective-permute-start | bytes 884744 | tf_op jit(solution)/shard_map/ppermute | solution.py:200
  33.1 6.3 %collective-permute-done.10.refs_15_.refs_7_ = bf16[576,256]{1,0:T(8,128)(2,1)S(1)} collective-permute-done((bf16[576,256]{1,0:T(8,128)(2,1)S(1)}, bf16[576,256]{1,0:T(8,128)(2,1)S(1)}, u32[]{:S(2)}, u32[]{:S(2)}) %collective-permute-start.10) | collective-permute-done | bytes 294944 | tf_op jit(solution)/shard_map/ppermute | solution.py:200
  39.5 3.7 %collective-permute-start.11 = (bf16[576,256]{1,0:T(8,128)(2,1)S(1)}, bf16[576,256]{1,0:T(8,128)(2,1)S(1)}, u32[]{:S(2)}, u32[]{:S(2)}) collective-permute-start(bf16[576,256]{1,0:T(8,128)(2,1)S(1)} %collective-permute-done.10.refs_15_.refs_7_), channel_id=1, source_target_pairs={{0,7},{1,0},{2,1},{3,2},{4,3},{5,4},{6,5},{7,6},{8,15},{9,8},{10,9... | collective-permute-start | bytes 884744 | tf_op jit(solution)/shard_map/ppermute | solution.py:200
  43.2 0.9 collective-permute-done.refs_1_
  44.1 1.1 collective-permute-start.1
  45.2 33.2 %all-to-all-done = bf16[32,32,2048]{2,1,0:T(8,128)(2,1)} async-done(((bf16[32,32,2048]{2,1,0:T(8,128)(2,1)}), bf16[32,32,2048]{2,1,0:T(8,128)(2,1)}, u32[]{:S(2)}, u32[]{:S(2)}) %all-to-all-start) | async-done | bytes 4194336 | tf_op jit(solution)/shard_map/all_to_all | solution.py:285
  78.4 8.0 %forward.1 = (f32[1024,176]{1,0:T(8,128)}, f32[1024,176]{1,0:T(8,128)}, bf16[1024,176]{1,0:T(8,128)(2,1)}, bf16[1024,2048]{1,0:T(8,128)(2,1)}) custom-call(s32[1]{0:T(128)} %bitcast.1.e_ref, bf16[1024,2048]{1,0:T(8,128)(2,1)} %bitcast.5.x_ref, bf16[176,2048]{1,0:T(8,128)(2,1)} %bitcast.26, bf16[176,2048]{1,0:T(8,128)(2,1)} %bitcast.29, ...), custom_call_target="tpu_custom_call" | custom-call | flops 2214592512 | bytes 8388608 | tf_op jit(solution)/shard_map/forward/pallas_call | solution.py:310
  86.5 7.3 %all-to-all-start.1 = ((bf16[32,32,2048]{2,1,0:T(8,128)(2,1)}), bf16[32,32,2048]{2,1,0:T(8,128)(2,1)}, u32[]{:S(2)}, u32[]{:S(2)}) async-start(bf16[32,32,2048]{2,1,0:T(8,128)(2,1)} %bitcast.25), calls=%async_computation.1 | async-start | bytes 8388608 | tf_op jit(solution)/shard_map/all_to_all | solution.py:330
  93.8 2.0 collective-permute-start.8
  95.8 4.0 %collective-permute-start.12 = (bf16[576,256]{1,0:T(8,128)(2,1)S(1)}, bf16[576,256]{1,0:T(8,128)(2,1)S(1)}, u32[]{:S(2)}, u32[]{:S(2)}) collective-permute-start(bf16[576,256]{1,0:T(8,128)(2,1)S(1)} %collective-permute-done.11.refs_14_.refs_6_), channel_id=1, source_target_pairs={{0,7},{1,0},{2,1},{3,2},{4,3},{5,4},{6,5},{7,6},{8,15},{9,8},{10,9... | collective-permute-start | bytes 884744 | tf_op jit(solution)/shard_map/ppermute | solution.py:200
  99.8 1.9 collective-permute-start.5
  101.9 5.7 %collective-permute-done.8.refs_10_.refs_2_ = bf16[576,256]{1,0:T(8,128)(2,1)S(1)} collective-permute-done((bf16[576,256]{1,0:T(8,128)(2,1)S(1)}, bf16[576,256]{1,0:T(8,128)(2,1)S(1)}, u32[]{:S(2)}, u32[]{:S(2)}) %collective-permute-start.8) | collective-permute-done | bytes 294944 | tf_op jit(solution)/shard_map/ppermute | solution.py:200
  107.6 3.3 %collective-permute-start.13 = (bf16[576,256]{1,0:T(8,128)(2,1)S(1)}, bf16[576,256]{1,0:T(8,128)(2,1)S(1)}, u32[]{:S(2)}, u32[]{:S(2)}) collective-permute-start(bf16[576,256]{1,0:T(8,128)(2,1)S(1)} %collective-permute-done.12.refs_13_.refs_5_), channel_id=1, source_target_pairs={{0,7},{1,0},{2,1},{3,2},{4,3},{5,4},{6,5},{7,6},{8,15},{9,8},{10,9... | collective-permute-start | bytes 884744 | tf_op jit(solution)/shard_map/ppermute | solution.py:200
  110.9 2.6 %collective-permute-done.5.refs_6_ = bf16[576,256]{1,0:T(8,128)(2,1)} collective-permute-done((bf16[576,256]{1,0:T(8,128)(2,1)S(1)}, bf16[576,256]{1,0:T(8,128)(2,1)}, u32[]{:S(2)}, u32[]{:S(2)}) %collective-permute-start.5) | collective-permute-done | bytes 294944 | tf_op jit(solution)/shard_map/ppermute | solution.py:200
  113.6 3.8 %collective-permute-start.6 = (bf16[576,256]{1,0:T(8,128)(2,1)}, bf16[576,256]{1,0:T(8,128)(2,1)S(1)}, u32[]{:S(2)}, u32[]{:S(2)}) collective-permute-start(bf16[576,256]{1,0:T(8,128)(2,1)} %collective-permute-done.5.refs_6_), channel_id=1, source_target_pairs={{0,7},{1,0},{2,1},{3,2},{4,3},{5,4},{6,5},{7,6},{8,15},{9,8},{10,9... | collective-permute-start | bytes 884744 | tf_op jit(solution)/shard_map/ppermute | solution.py:200
  117.4 2.5 %collective-permute-done.9.refs_11_.refs_3_ = bf16[576,256]{1,0:T(8,128)(2,1)S(1)} collective-permute-done((bf16[576,256]{1,0:T(8,128)(2,1)S(1)}, bf16[576,256]{1,0:T(8,128)(2,1)S(1)}, u32[]{:S(2)}, u32[]{:S(2)}) %collective-permute-start.9) | collective-permute-done | bytes 294944 | tf_op jit(solution)/shard_map/ppermute | solution.py:200
  120.8 6.3 %backward.3 = (bf16[512,176]{1,0:T(8,128)(2,1)}, bf16[512,176]{1,0:T(8,128)(2,1)}, bf16[512,256]{1,0:T(8,128)(2,1)}, bf16[512,256]{1,0:T(8,128)(2,1)}, bf16[512,...) custom-call(s32[1]{0:T(128)} %bitcast.col_ref.z_ref, ...), custom_call_target="tpu_custom_call" | custom-call | flops 1107296256 | bytes 4194304 | tf_op jit(solution)/shard_map/backward/pallas_call | solution.py:341
  127.1 3.6 %collective-permute-start.24 = (bf16[512,256]{1,0:T(8,128)(2,1)}, bf16[512,256]{1,0:T(8,128)(2,1)S(1)}, u32[]{:S(2)}, u32[]{:S(2)}) collective-permute-start(bf16[512,256]{1,0:T(8,128)(2,1)} %get-tuple-element.57), channel_id=1, source_target_pairs={{0,7},{1,0},{2,1},{3,2},{4,3},{5,4},{6,5},{7,6},{8,15},{9,8},{10,9... | collective-permute-start | bytes 786440 | tf_op jit(solution)/shard_map/ppermute | solution.py:200
  131.4 0.7 copy-done.6
  132.1 6.3 %backward.2 = (bf16[512,176]{1,0:T(8,128)(2,1)}, bf16[512,176]{1,0:T(8,128)(2,1)}, bf16[512,256]{1,0:T(8,128)(2,1)}, bf16[512,256]{1,0:T(8,128)(2,1)}, bf16[512,...) custom-call(s32[1]{0:T(128)} %bitcast.col_ref.z_ref, ...), custom_call_target="tpu_custom_call" | custom-call | flops 1107296256 | bytes 4194304 | tf_op jit(solution)/shard_map/backward/pallas_call | solution.py:341
  138.5 3.3 %collective-permute-start.18 = (bf16[512,256]{1,0:T(8,128)(2,1)}, bf16[512,256]{1,0:T(8,128)(2,1)S(1)}, u32[]{:S(2)}, u32[]{:S(2)}) collective-permute-start(bf16[512,256]{1,0:T(8,128)(2,1)} %get-tuple-element.50), channel_id=1, source_target_pairs={{0,7},{1,0},{2,1},{3,2},{4,3},{5,4},{6,5},{7,6},{8,15},{9,8},{10,9... | collective-permute-start | bytes 786440 | tf_op jit(solution)/shard_map/ppermute | solution.py:200
  141.9 3.3 %collective-permute-start.25 = (bf16[512,256]{1,0:T(8,128)(2,1)S(1)}, bf16[512,256]{1,0:T(8,128)(2,1)S(1)}, u32[]{:S(2)}, u32[]{:S(2)}) collective-permute-start(bf16[512,256]{1,0:T(8,128)(2,1)S(1)} %add_convert_fusion.3), channel_id=1, source_target_pairs={{0,7},{1,0},{2,1},{3,2},{4,3},{5,4},{6,5},{7,6},{8,15},{9,8},{10,9... | collective-permute-start | bytes 786440 | tf_op jit(solution)/shard_map/ppermute | solution.py:200
  145.4 3.5 %collective-permute-done.18 = bf16[512,256]{1,0:T(8,128)(2,1)S(1)} collective-permute-done((bf16[512,256]{1,0:T(8,128)(2,1)}, bf16[512,256]{1,0:T(8,128)(2,1)S(1)}, u32[]{:S(2)}, u32[]{:S(2)}) %collective-permute-start.18) | collective-permute-done | bytes 262176 | tf_op jit(solution)/shard_map/ppermute | solution.py:200
  148.8 1.0 add_convert_fusion.8
  149.8 3.7 %collective-permute-start.19 = (bf16[512,256]{1,0:T(8,128)(2,1)S(1)}, bf16[512,256]{1,0:T(8,128)(2,1)S(1)}, u32[]{:S(2)}, u32[]{:S(2)}) collective-permute-start(bf16[512,256]{1,0:T(8,128)(2,1)S(1)} %add_convert_fusion.8), channel_id=1, source_target_pairs={{0,7},{1,0},{2,1},{3,2},{4,3},{5,4},{6,5},{7,6},{8,15},{9,8},{10,9... | collective-permute-start | bytes 786440 | tf_op jit(solution)/shard_map/ppermute | solution.py:200
  153.5 1.0 add_convert_fusion.11
  154.7 3.7 %collective-permute-start.26 = (bf16[512,256]{1,0:T(8,128)(2,1)S(1)}, bf16[512,256]{1,0:T(8,128)(2,1)S(1)}, u32[]{:S(2)}, u32[]{:S(2)}) collective-permute-start(bf16[512,256]{1,0:T(8,128)(2,1)S(1)} %add_convert_fusion.2), channel_id=1, source_target_pairs={{0,7},{1,0},{2,1},{3,2},{4,3},{5,4},{6,5},{7,6},{8,15},{9,8},{10,9... | collective-permute-start | bytes 786440 | tf_op jit(solution)/shard_map/ppermute | solution.py:200
  158.6 6.3 %collective-permute-done.15 = bf16[512,256]{1,0:T(8,128)(2,1)S(1)} collective-permute-done((bf16[512,256]{1,0:T(8,128)(2,1)S(1)}, bf16[512,256]{1,0:T(8,128)(2,1)S(1)}, u32[]{:S(2)}, u32[]{:S(2)}) %collective-permute-start.15) | collective-permute-done | bytes 262176 | tf_op jit(solution)/shard_map/ppermute | solution.py:200
  165.2 3.3 %collective-permute-start.27 = (bf16[512,256]{1,0:T(8,128)(2,1)S(1)}, bf16[512,256]{1,0:T(8,128)(2,1)S(1)}, u32[]{:S(2)}, u32[]{:S(2)}) collective-permute-start(bf16[512,256]{1,0:T(8,128)(2,1)S(1)} %add_convert_fusion.1), channel_id=1, source_target_pairs={{0,7},{1,0},{2,1},{3,2},{4,3},{5,4},{6,5},{7,6},{8,15},{9,8},{10,9... | collective-permute-start | bytes 786440 | tf_op jit(solution)/shard_map/ppermute | solution.py:200
  168.6 5.5 %collective-permute-done.16 = bf16[512,256]{1,0:T(8,128)(2,1)S(1)} collective-permute-done((bf16[512,256]{1,0:T(8,128)(2,1)S(1)}, bf16[512,256]{1,0:T(8,128)(2,1)S(1)}, u32[]{:S(2)}, u32[]{:S(2)}) %collective-permute-start.16) | collective-permute-done | bytes 262176 | tf_op jit(solution)/shard_map/ppermute | solution.py:200
  175.2 6.8 %collective-permute-done.17 = bf16[512,256]{1,0:T(8,128)(2,1)S(1)} collective-permute-done((bf16[512,256]{1,0:T(8,128)(2,1)S(1)}, bf16[512,256]{1,0:T(8,128)(2,1)S(1)}, u32[]{:S(2)}, u32[]{:S(2)}) %collective-permute-start.17) | collective-permute-done | bytes 262176 | tf_op jit(solution)/shard_map/ppermute | solution.py:200
  182.0 0.8 pad_maximum_fusion
  182.8 7.7 %all-to-all-start.4 = ((bf16[32,32,256]{2,1,0:T(8,128)(2,1)}), bf16[32,32,256]{2,1,0:T(8,128)(2,1)S(1)}, u32[]{:S(2)}, u32[]{:S(2)}) async-start(bf16[32,32,256]{2,1,0:T(8,128)(2,1)} %bitcast.14), calls=%async_computation.4 | async-start | bytes 1048576 | tf_op jit(solution)/shard_map/all_to_all | solution.py:415
  190.6 0.7 copy.16.re_ref
  191.4 0.7 copy.17.rw_ref
  192.1 2.3 %home.1 = (bf16[128,1024]{1,0:T(8,128)(2,1)}, bf16[256,1024]{1,0:T(8,128)(2,1)}) custom-call(s32[128,4]{1,0:T(8,128)} %copy.16.re_ref, f32[128,4]{1,0:T(8,128)} %copy.17.rw_ref), custom_call_target="tpu_custom_call" | custom-call | flops 25165824 | bytes 786432 | tf_op jit(solution)/shard_map/home/pallas_call | solution.py:297
  194.4 9.0 %combine.1 = bf16[8,136,256]{2,1,0:T(8,128)(2,1)} custom-call(s32[1]{0:T(128)} %bitcast.col_ref.z_ref, bf16[1024,2048]{1,0:T(8,128)(2,1)} %bitcast.10.y_ref, bf16[128,1024]{1,0:T(8,128)(2,1)} %get-tuple-element.40.mt_ref, bf16[256,1024]{1,0:T(8,128)(2,1)} %get-tuple-element.41.mw_ref, s32[4,128]{1,0:T(4,128)} %bitcast.41, bf16[576,256]{1,0:T(8,128)(2,1)} %copy-done.2, ...), custom_call_target="tpu_custom_call" | custom-call | flops 1610612736 | bytes 4194304 | tf_op jit(solution)/shard_map/combine/pallas_call | solution.py:384
  203.4 4.8 %all-to-all-start.3 = ((bf16[8,136,256]{2,1,0:T(8,128)(2,1)}), bf16[8,136,256]{2,1,0:T(8,128)(2,1)S(1)}, u32[]{:S(2)}, u32[]{:S(2)}) async-start(bf16[8,136,256]{2,1,0:T(8,128)(2,1)} %combine.1), calls=%async_computation.3 | async-start | bytes 1114112 | tf_op jit(solution)/shard_map/all_to_all | solution.py:403
  208.2 1.3 add_convert_fusion.12._
  209.5 4.5 %down.1 = f32[176,2048]{1,0:T(8,128)} custom-call(s32[1]{0:T(128)} %bitcast.col_ref.z_ref, bf16[1024,176]{1,0:T(8,128)(2,1)} %get-tuple-element.69.h_ref, bf16[8,128]{1,0:T(8,128)(2,1)} %add_convert_fusion.12._, bf16[576,256]{1,0:T(8,128)(2,1)} %copy-done.2, bf16[576,256]{1,0:T(8,128)(2,1)} %copy-done.8, bf16[576,256]{1,0:T(8,128)(2,1)} %copy-done.12, ...), custom_call_target="tpu_custom_call" | custom-call | flops 738197504 | bytes 5636096 | tf_op jit(solution)/shard_map/down/pallas_call | solution.py:370
  214.0 8.4 %weight.1 = (f32[176,2048]{1,0:T(8,128)}, f32[176,2048]{1,0:T(8,128)}) custom-call(bf16[1024,2048]{1,0:T(8,128)(2,1)} %bitcast.5.x_ref, bf16[512,176]{1,0:T(8,128)(2,1)} %get-tuple-element.63.refs_0_, bf16[512,176]{1,0:T(8,128)(2,1)} %get-tuple-element.64.refs_1_, bf16[512,176]{1,0:T(8,128)(2,1)} %get-tuple-element.65.refs_2_, ...), custom_call_target="tpu_custom_call" | custom-call | flops 1476395008 | bytes 7077888 | tf_op jit(solution)/shard_map/weight/pallas_call | solution.py:361
  222.5 0.9 convolution_convert_fusion
  223.3 3.4 %all-to-all-done.3.x_ref = bf16[8,136,256]{2,1,0:T(8,128)(2,1)S(1)} async-done(((bf16[8,136,256]{2,1,0:T(8,128)(2,1)}), bf16[8,136,256]{2,1,0:T(8,128)(2,1)S(1)}, u32[]{:S(2)}, u32[]{:S(2)}) %all-to-all-start.3) | async-done | bytes 557088 | tf_op jit(solution)/shard_map/all_to_all | solution.py:403
  (109 shorter events, 4.8 us)
Async XLA Ops:
  2.8 18.0 %all-to-all-start.2 = ((bf16[32,32,256]{2,1,0:T(8,128)(2,1)}), bf16[32,32,256]{2,1,0:T(8,128)(2,1)S(1)}, u32[]{:S(2)}, u32[]{:S(2)}) async-start(bf16[32,32,256]{2,1,0:T(8,128)(2,1)} %bitcast.39), calls=%async_computation.2 | async-start | bytes 1048576 | tf_op jit(solution)/shard_map/all_to_all | solution.py:281
  20.8 57.6 %all-to-all-start = ((bf16[32,32,2048]{2,1,0:T(8,128)(2,1)}), bf16[32,32,2048]{2,1,0:T(8,128)(2,1)}, u32[]{:S(2)}, u32[]{:S(2)}) async-start(bf16[32,32,2048]{2,1,0:T(8,128)(2,1)} %bitcast.24), calls=%async_computation | async-start | bytes 8388608 | tf_op jit(solution)/shard_map/all_to_all | solution.py:285
  27.0 59.5 %copy-start.1 = (bf16[576,256]{1,0:T(8,128)(2,1)}, bf16[576,256]{1,0:T(8,128)(2,1)S(1)}, u32[]{:S(2)}) copy-start(bf16[576,256]{1,0:T(8,128)(2,1)S(1)} %pad_maximum_fusion.2.refs_8_.refs_0_) | copy-start | bytes 884740
  27.0 12.5 %collective-permute-start.10 = (bf16[576,256]{1,0:T(8,128)(2,1)S(1)}, bf16[576,256]{1,0:T(8,128)(2,1)S(1)}, u32[]{:S(2)}, u32[]{:S(2)}) collective-permute-start(bf16[576,256]{1,0:T(8,128)(2,1)S(1)} %pad_maximum_fusion.2.refs_8_.refs_0_), channel_id=1, source_target_pairs={{0,7},{1,0},{2,1},{3,2},{4,3},{5,4},{6,5},{7,6},{8,15},{9,8},{10,9... | collective-permute-start | bytes 884744 | tf_op jit(solution)/shard_map/ppermute | solution.py:200
  32.9 53.5 %copy-start.2 = (bf16[576,256]{1,0:T(8,128)(2,1)}, bf16[576,256]{1,0:T(8,128)(2,1)S(1)}, u32[]{:S(2)}) copy-start(bf16[576,256]{1,0:T(8,128)(2,1)S(1)} %pad_maximum_fusion.1.refs_0_) | copy-start | bytes 884740
  32.9 11.2 %collective-permute-start = (bf16[576,256]{1,0:T(8,128)(2,1)S(1)}, bf16[576,256]{1,0:T(8,128)(2,1)S(1)}, u32[]{:S(2)}, u32[]{:S(2)}) collective-permute-start(bf16[576,256]{1,0:T(8,128)(2,1)S(1)} %pad_maximum_fusion.1.refs_0_), channel_id=1, source_target_pairs={{0,1},{1,2},{2,3},{3,4},{4,5},{5,6},{6,7},{7,0},{8,9},{9,10},{10,1... | collective-permute-start | bytes 884744 | tf_op jit(solution)/shard_map/ppermute | solution.py:200
  33.0 60.7 %collective-permute-start.7 = (bf16[576,256]{1,0:T(8,128)(2,1)S(1)}, bf16[576,256]{1,0:T(8,128)(2,1)S(1)}, u32[]{:S(2)}, u32[]{:S(2)}) collective-permute-start(bf16[576,256]{1,0:T(8,128)(2,1)S(1)} %pad_maximum_fusion.2.refs_8_.refs_0_), channel_id=1, source_target_pairs={{0,1},{1,2},{2,3},{3,4},{4,5},{5,6},{6,7},{7,0},{8,9},{9,10},{10,1... | collective-permute-start | bytes 884744 | tf_op jit(solution)/shard_map/ppermute | solution.py:200
  39.5 47.0 %copy-start.7 = (bf16[576,256]{1,0:T(8,128)(2,1)}, bf16[576,256]{1,0:T(8,128)(2,1)S(1)}, u32[]{:S(2)}) copy-start(bf16[576,256]{1,0:T(8,128)(2,1)S(1)} %collective-permute-done.10.refs_15_.refs_7_) | copy-start | bytes 884740
  39.5 56.3 %collective-permute-start.11 = (bf16[576,256]{1,0:T(8,128)(2,1)S(1)}, bf16[576,256]{1,0:T(8,128)(2,1)S(1)}, u32[]{:S(2)}, u32[]{:S(2)}) collective-permute-start(bf16[576,256]{1,0:T(8,128)(2,1)S(1)} %collective-permute-done.10.refs_15_.refs_7_), channel_id=1, source_target_pairs={{0,7},{1,0},{2,1},{3,2},{4,3},{5,4},{6,5},{7,6},{8,15},{9,8},{10,9... | collective-permute-start | bytes 884744 | tf_op jit(solution)/shard_map/ppermute | solution.py:200
  43.2 56.7 %collective-permute-start.4 = (bf16[576,256]{1,0:T(8,128)(2,1)S(1)}, bf16[576,256]{1,0:T(8,128)(2,1)S(1)}, u32[]{:S(2)}, u32[]{:S(2)}) collective-permute-start(bf16[576,256]{1,0:T(8,128)(2,1)S(1)} %pad_maximum_fusion.1.refs_0_), channel_id=1, source_target_pairs={{0,7},{1,0},{2,1},{3,2},{4,3},{5,4},{6,5},{7,6},{8,15},{9,8},{10,9... | collective-permute-start | bytes 884744 | tf_op jit(solution)/shard_map/ppermute | solution.py:200
  44.1 42.4 %copy-start.8 = (bf16[576,256]{1,0:T(8,128)(2,1)}, bf16[576,256]{1,0:T(8,128)(2,1)S(1)}, u32[]{:S(2)}) copy-start(bf16[576,256]{1,0:T(8,128)(2,1)S(1)} %collective-permute-done.refs_1_) | copy-start | bytes 884740
  44.1 57.7 %collective-permute-start.1 = (bf16[576,256]{1,0:T(8,128)(2,1)S(1)}, bf16[576,256]{1,0:T(8,128)(2,1)S(1)}, u32[]{:S(2)}, u32[]{:S(2)}) collective-permute-start(bf16[576,256]{1,0:T(8,128)(2,1)S(1)} %collective-permute-done.refs_1_), channel_id=1, source_target_pairs={{0,1},{1,2},{2,3},{3,4},{4,5},{5,6},{6,7},{7,0},{8,9},{9,10},{10,1... | collective-permute-start | bytes 884744 | tf_op jit(solution)/shard_map/ppermute | solution.py:200
  86.5 96.4 %all-to-all-start.1 = ((bf16[32,32,2048]{2,1,0:T(8,128)(2,1)}), bf16[32,32,2048]{2,1,0:T(8,128)(2,1)}, u32[]{:S(2)}, u32[]{:S(2)}) async-start(bf16[32,32,2048]{2,1,0:T(8,128)(2,1)} %bitcast.25), calls=%async_computation.1 | async-start | bytes 8388608 | tf_op jit(solution)/shard_map/all_to_all | solution.py:330
  93.8 26.2 %copy-start.9 = (bf16[576,256]{1,0:T(8,128)(2,1)}, bf16[576,256]{1,0:T(8,128)(2,1)S(1)}, u32[]{:S(2)}) copy-start(bf16[576,256]{1,0:T(8,128)(2,1)S(1)} %collective-permute-done.7.refs_9_.refs_1_) | copy-start | bytes 884740
  93.8 13.8 %collective-permute-start.8 = (bf16[576,256]{1,0:T(8,128)(2,1)S(1)}, bf16[576,256]{1,0:T(8,128)(2,1)S(1)}, u32[]{:S(2)}, u32[]{:S(2)}) collective-permute-start(bf16[576,256]{1,0:T(8,128)(2,1)S(1)} %collective-permute-done.7.refs_9_.refs_1_), channel_id=1, source_target_pairs={{0,1},{1,2},{2,3},{3,4},{4,5},{5,6},{6,7},{7,0},{8,9},{9,10},{10,1... | collective-permute-start | bytes 884744 | tf_op jit(solution)/shard_map/ppermute | solution.py:200
  95.8 24.2 %copy-start.10 = (bf16[576,256]{1,0:T(8,128)(2,1)}, bf16[576,256]{1,0:T(8,128)(2,1)S(1)}, u32[]{:S(2)}) copy-start(bf16[576,256]{1,0:T(8,128)(2,1)S(1)} %collective-permute-done.11.refs_14_.refs_6_) | copy-start | bytes 884740
  95.8 11.8 %collective-permute-start.12 = (bf16[576,256]{1,0:T(8,128)(2,1)S(1)}, bf16[576,256]{1,0:T(8,128)(2,1)S(1)}, u32[]{:S(2)}, u32[]{:S(2)}) collective-permute-start(bf16[576,256]{1,0:T(8,128)(2,1)S(1)} %collective-permute-done.11.refs_14_.refs_6_), channel_id=1, source_target_pairs={{0,7},{1,0},{2,1},{3,2},{4,3},{5,4},{6,5},{7,6},{8,15},{9,8},{10,9... | collective-permute-start | bytes 884744 | tf_op jit(solution)/shard_map/ppermute | solution.py:200
  99.8 13.7 %collective-permute-start.5 = (bf16[576,256]{1,0:T(8,128)(2,1)S(1)}, bf16[576,256]{1,0:T(8,128)(2,1)}, u32[]{:S(2)}, u32[]{:S(2)}) collective-permute-start(bf16[576,256]{1,0:T(8,128)(2,1)S(1)} %collective-permute-done.4.refs_7_), channel_id=1, source_target_pairs={{0,7},{1,0},{2,1},{3,2},{4,3},{5,4},{6,5},{7,6},{8,15},{9,8},{10,9... | collective-permute-start | bytes 884744 | tf_op jit(solution)/shard_map/ppermute | solution.py:200
  101.8 15.6 %collective-permute-start.2 = (bf16[576,256]{1,0:T(8,128)(2,1)S(1)}, bf16[576,256]{1,0:T(8,128)(2,1)S(1)}, u32[]{:S(2)}, u32[]{:S(2)}) collective-permute-start(bf16[576,256]{1,0:T(8,128)(2,1)S(1)} %collective-permute-done.1.refs_2_), channel_id=1, source_target_pairs={{0,1},{1,2},{2,3},{3,4},{4,5},{5,6},{6,7},{7,0},{8,9},{9,10},{10,1... | collective-permute-start | bytes 884744 | tf_op jit(solution)/shard_map/ppermute | solution.py:200
  107.6 12.4 %collective-permute-start.9 = (bf16[576,256]{1,0:T(8,128)(2,1)S(1)}, bf16[576,256]{1,0:T(8,128)(2,1)S(1)}, u32[]{:S(2)}, u32[]{:S(2)}) collective-permute-start(bf16[576,256]{1,0:T(8,128)(2,1)S(1)} %collective-permute-done.8.refs_10_.refs_2_), channel_id=1, source_target_pairs={{0,1},{1,2},{2,3},{3,4},{4,5},{5,6},{6,7},{7,0},{8,9},{9,10},{10,1... | collective-permute-start | bytes 884744 | tf_op jit(solution)/shard_map/ppermute | solution.py:200
  107.6 12.3 %collective-permute-start.13 = (bf16[576,256]{1,0:T(8,128)(2,1)S(1)}, bf16[576,256]{1,0:T(8,128)(2,1)S(1)}, u32[]{:S(2)}, u32[]{:S(2)}) collective-permute-start(bf16[576,256]{1,0:T(8,128)(2,1)S(1)} %collective-permute-done.12.refs_13_.refs_5_), channel_id=1, source_target_pairs={{0,7},{1,0},{2,1},{3,2},{4,3},{5,4},{6,5},{7,6},{8,15},{9,8},{10,9... | collective-permute-start | bytes 884744 | tf_op jit(solution)/shard_map/ppermute | solution.py:200
  113.6 17.1 %collective-permute-start.6 = (bf16[576,256]{1,0:T(8,128)(2,1)}, bf16[576,256]{1,0:T(8,128)(2,1)S(1)}, u32[]{:S(2)}, u32[]{:S(2)}) collective-permute-start(bf16[576,256]{1,0:T(8,128)(2,1)} %collective-permute-done.5.refs_6_), channel_id=1, source_target_pairs={{0,7},{1,0},{2,1},{3,2},{4,3},{5,4},{6,5},{7,6},{8,15},{9,8},{10,9... | collective-permute-start | bytes 884744 | tf_op jit(solution)/shard_map/ppermute | solution.py:200
  117.4 13.3 %collective-permute-start.3 = (bf16[576,256]{1,0:T(8,128)(2,1)S(1)}, bf16[576,256]{1,0:T(8,128)(2,1)S(1)}, u32[]{:S(2)}, u32[]{:S(2)}) collective-permute-start(bf16[576,256]{1,0:T(8,128)(2,1)S(1)} %collective-permute-done.2.refs_3_), channel_id=1, source_target_pairs={{0,1},{1,2},{2,3},{3,4},{4,5},{5,6},{6,7},{7,0},{8,9},{9,10},{10,1... | collective-permute-start | bytes 884744 | tf_op jit(solution)/shard_map/ppermute | solution.py:200
  127.1 14.7 %collective-permute-start.24 = (bf16[512,256]{1,0:T(8,128)(2,1)}, bf16[512,256]{1,0:T(8,128)(2,1)S(1)}, u32[]{:S(2)}, u32[]{:S(2)}) collective-permute-start(bf16[512,256]{1,0:T(8,128)(2,1)} %get-tuple-element.57), channel_id=1, source_target_pairs={{0,7},{1,0},{2,1},{3,2},{4,3},{5,4},{6,5},{7,6},{8,15},{9,8},{10,9... | collective-permute-start | bytes 786440 | tf_op jit(solution)/shard_map/ppermute | solution.py:200
  130.7 27.7 %copy-start.20 = (bf16[512,256]{1,0:T(8,128)(2,1)S(1)}, bf16[512,256]{1,0:T(8,128)(2,1)}, u32[]{:S(2)}) copy-start(bf16[512,256]{1,0:T(8,128)(2,1)} %get-tuple-element.56) | copy-start | bytes 786436
  130.7 14.5 %collective-permute-start.21 = (bf16[512,256]{1,0:T(8,128)(2,1)}, bf16[512,256]{1,0:T(8,128)(2,1)S(1)}, u32[]{:S(2)}, u32[]{:S(2)}) collective-permute-start(bf16[512,256]{1,0:T(8,128)(2,1)} %get-tuple-element.54), channel_id=1, source_target_pairs={{0,1},{1,2},{2,3},{3,4},{4,5},{5,6},{6,7},{7,0},{8,9},{9,10},{10,1... | collective-permute-start | bytes 786440 | tf_op jit(solution)/shard_map/ppermute | solution.py:200
  138.4 26.5 %copy-start.22 = (bf16[512,256]{1,0:T(8,128)(2,1)S(1)}, bf16[512,256]{1,0:T(8,128)(2,1)}, u32[]{:S(2)}) copy-start(bf16[512,256]{1,0:T(8,128)(2,1)} %get-tuple-element.48) | copy-start | bytes 786436
  138.4 26.6 %copy-start.17 = (bf16[512,256]{1,0:T(8,128)(2,1)S(1)}, bf16[512,256]{1,0:T(8,128)(2,1)}, u32[]{:S(2)}) copy-start(bf16[512,256]{1,0:T(8,128)(2,1)} %get-tuple-element.60) | copy-start | bytes 786436
  138.5 30.0 %copy-start.19 = (bf16[512,256]{1,0:T(8,128)(2,1)S(1)}, bf16[512,256]{1,0:T(8,128)(2,1)}, u32[]{:S(2)}) copy-start(bf16[512,256]{1,0:T(8,128)(2,1)} %get-tuple-element.52) | copy-start | bytes 786436
  138.5 35.7 %copy-start.18 = (bf16[512,256]{1,0:T(8,128)(2,1)S(1)}, bf16[512,256]{1,0:T(8,128)(2,1)}, u32[]{:S(2)}) copy-start(bf16[512,256]{1,0:T(8,128)(2,1)} %get-tuple-element.49) | copy-start | bytes 786436
  138.5 35.9 %copy-start.26 = (bf16[512,256]{1,0:T(8,128)(2,1)S(1)}, bf16[512,256]{1,0:T(8,128)(2,1)}, u32[]{:S(2)}) copy-start(bf16[512,256]{1,0:T(8,128)(2,1)} %get-tuple-element.61) | copy-start | bytes 786436
  138.5 10.3 %collective-permute-start.18 = (bf16[512,256]{1,0:T(8,128)(2,1)}, bf16[512,256]{1,0:T(8,128)(2,1)S(1)}, u32[]{:S(2)}, u32[]{:S(2)}) collective-permute-start(bf16[512,256]{1,0:T(8,128)(2,1)} %get-tuple-element.50), channel_id=1, source_target_pairs={{0,7},{1,0},{2,1},{3,2},{4,3},{5,4},{6,5},{7,6},{8,15},{9,8},{10,9... | collective-permute-start | bytes 786440 | tf_op jit(solution)/shard_map/ppermute | solution.py:200
  141.8 11.7 %collective-permute-start.14 = (bf16[512,256]{1,0:T(8,128)(2,1)}, bf16[512,256]{1,0:T(8,128)(2,1)S(1)}, u32[]{:S(2)}, u32[]{:S(2)}) collective-permute-start(bf16[512,256]{1,0:T(8,128)(2,1)} %get-tuple-element.46), channel_id=1, source_target_pairs={{0,1},{1,2},{2,3},{3,4},{4,5},{5,6},{6,7},{7,0},{8,9},{9,10},{10,1... | collective-permute-start | bytes 786440 | tf_op jit(solution)/shard_map/ppermute | solution.py:200
  141.9 40.0 %copy-start.27 = (bf16[512,256]{1,0:T(8,128)(2,1)S(1)}, bf16[512,256]{1,0:T(8,128)(2,1)}, u32[]{:S(2)}) copy-start(bf16[512,256]{1,0:T(8,128)(2,1)} %get-tuple-element.53) | copy-start | bytes 786436
  141.9 12.7 %collective-permute-start.25 = (bf16[512,256]{1,0:T(8,128)(2,1)S(1)}, bf16[512,256]{1,0:T(8,128)(2,1)S(1)}, u32[]{:S(2)}, u32[]{:S(2)}) collective-permute-start(bf16[512,256]{1,0:T(8,128)(2,1)S(1)} %add_convert_fusion.3), channel_id=1, source_target_pairs={{0,7},{1,0},{2,1},{3,2},{4,3},{5,4},{6,5},{7,6},{8,15},{9,8},{10,9... | collective-permute-start | bytes 786440 | tf_op jit(solution)/shard_map/ppermute | solution.py:200
  145.3 13.1 %collective-permute-start.22 = (bf16[512,256]{1,0:T(8,128)(2,1)S(1)}, bf16[512,256]{1,0:T(8,128)(2,1)S(1)}, u32[]{:S(2)}, u32[]{:S(2)}) collective-permute-start(bf16[512,256]{1,0:T(8,128)(2,1)S(1)} %add_convert_fusion.5), channel_id=1, source_target_pairs={{0,1},{1,2},{2,3},{3,4},{4,5},{5,6},{6,7},{7,0},{8,9},{9,10},{10,1... | collective-permute-start | bytes 786440 | tf_op jit(solution)/shard_map/ppermute | solution.py:200
  149.8 18.6 %collective-permute-start.19 = (bf16[512,256]{1,0:T(8,128)(2,1)S(1)}, bf16[512,256]{1,0:T(8,128)(2,1)S(1)}, u32[]{:S(2)}, u32[]{:S(2)}) collective-permute-start(bf16[512,256]{1,0:T(8,128)(2,1)S(1)} %add_convert_fusion.8), channel_id=1, source_target_pairs={{0,7},{1,0},{2,1},{3,2},{4,3},{5,4},{6,5},{7,6},{8,15},{9,8},{10,9... | collective-permute-start | bytes 786440 | tf_op jit(solution)/shard_map/ppermute | solution.py:200
  154.5 10.4 %collective-permute-start.15 = (bf16[512,256]{1,0:T(8,128)(2,1)S(1)}, bf16[512,256]{1,0:T(8,128)(2,1)S(1)}, u32[]{:S(2)}, u32[]{:S(2)}) collective-permute-start(bf16[512,256]{1,0:T(8,128)(2,1)S(1)} %add_convert_fusion.11), channel_id=1, source_target_pairs={{0,1},{1,2},{2,3},{3,4},{4,5},{5,6},{6,7},{7,0},{8,9},{9,10},{10,1... | collective-permute-start | bytes 786440 | tf_op jit(solution)/shard_map/ppermute | solution.py:200
  154.7 35.9 %copy-start.28 = (s32[128,4]{0,1:T(4,128)S(1)}, s32[128,4]{0,1:T(4,128)}, u32[]{:S(2)}) copy-start(s32[128,4]{0,1:T(4,128)} %param.11) | copy-start | bytes 6148
  154.7 36.6 %copy-start.29 = (f32[128,4]{0,1:T(4,128)S(1)}, f32[128,4]{0,1:T(4,128)}, u32[]{:S(2)}) copy-start(f32[128,4]{0,1:T(4,128)} %param.12) | copy-start | bytes 6148
  154.7 10.3 %collective-permute-start.26 = (bf16[512,256]{1,0:T(8,128)(2,1)S(1)}, bf16[512,256]{1,0:T(8,128)(2,1)S(1)}, u32[]{:S(2)}, u32[]{:S(2)}) collective-permute-start(bf16[512,256]{1,0:T(8,128)(2,1)S(1)} %add_convert_fusion.2), channel_id=1, source_target_pairs={{0,7},{1,0},{2,1},{3,2},{4,3},{5,4},{6,5},{7,6},{8,15},{9,8},{10,9... | collective-permute-start | bytes 786440 | tf_op jit(solution)/shard_map/ppermute | solution.py:200
  158.5 15.9 %collective-permute-start.23 = (bf16[512,256]{1,0:T(8,128)(2,1)S(1)}, bf16[512,256]{1,0:T(8,128)(2,1)S(1)}, u32[]{:S(2)}, u32[]{:S(2)}) collective-permute-start(bf16[512,256]{1,0:T(8,128)(2,1)S(1)} %add_convert_fusion.4), channel_id=1, source_target_pairs={{0,1},{1,2},{2,3},{3,4},{4,5},{5,6},{6,7},{7,0},{8,9},{9,10},{10,1... | collective-permute-start | bytes 786440 | tf_op jit(solution)/shard_map/ppermute | solution.py:200
  165.0 9.2 %collective-permute-start.16 = (bf16[512,256]{1,0:T(8,128)(2,1)S(1)}, bf16[512,256]{1,0:T(8,128)(2,1)S(1)}, u32[]{:S(2)}, u32[]{:S(2)}) collective-permute-start(bf16[512,256]{1,0:T(8,128)(2,1)S(1)} %add_convert_fusion.10), channel_id=1, source_target_pairs={{0,1},{1,2},{2,3},{3,4},{4,5},{5,6},{6,7},{7,0},{8,9},{9,10},{10,1... | collective-permute-start | bytes 786440 | tf_op jit(solution)/shard_map/ppermute | solution.py:200
  165.2 9.2 %collective-permute-start.27 = (bf16[512,256]{1,0:T(8,128)(2,1)S(1)}, bf16[512,256]{1,0:T(8,128)(2,1)S(1)}, u32[]{:S(2)}, u32[]{:S(2)}) collective-permute-start(bf16[512,256]{1,0:T(8,128)(2,1)S(1)} %add_convert_fusion.1), channel_id=1, source_target_pairs={{0,7},{1,0},{2,1},{3,2},{4,3},{5,4},{6,5},{7,6},{8,15},{9,8},{10,9... | collective-permute-start | bytes 786440 | tf_op jit(solution)/shard_map/ppermute | solution.py:200
  168.5 6.6 %collective-permute-start.20 = (bf16[512,256]{1,0:T(8,128)(2,1)S(1)}, bf16[512,256]{1,0:T(8,128)(2,1)S(1)}, u32[]{:S(2)}, u32[]{:S(2)}) collective-permute-start(bf16[512,256]{1,0:T(8,128)(2,1)S(1)} %add_convert_fusion.7), channel_id=1, source_target_pairs={{0,7},{1,0},{2,1},{3,2},{4,3},{5,4},{6,5},{7,6},{8,15},{9,8},{10,9... | collective-permute-start | bytes 786440 | tf_op jit(solution)/shard_map/ppermute | solution.py:200
  174.2 7.7 %collective-permute-start.17 = (bf16[512,256]{1,0:T(8,128)(2,1)S(1)}, bf16[512,256]{1,0:T(8,128)(2,1)S(1)}, u32[]{:S(2)}, u32[]{:S(2)}) collective-permute-start(bf16[512,256]{1,0:T(8,128)(2,1)S(1)} %add_convert_fusion.9), channel_id=1, source_target_pairs={{0,1},{1,2},{2,3},{3,4},{4,5},{5,6},{6,7},{7,0},{8,9},{9,10},{10,1... | collective-permute-start | bytes 786440 | tf_op jit(solution)/shard_map/ppermute | solution.py:200
  182.8 20.5 %all-to-all-start.4 = ((bf16[32,32,256]{2,1,0:T(8,128)(2,1)}), bf16[32,32,256]{2,1,0:T(8,128)(2,1)S(1)}, u32[]{:S(2)}, u32[]{:S(2)}) async-start(bf16[32,32,256]{2,1,0:T(8,128)(2,1)} %bitcast.14), calls=%async_computation.4 | async-start | bytes 1048576 | tf_op jit(solution)/shard_map/all_to_all | solution.py:415
  203.4 23.3 %all-to-all-start.3 = ((bf16[8,136,256]{2,1,0:T(8,128)(2,1)}), bf16[8,136,256]{2,1,0:T(8,128)(2,1)S(1)}, u32[]{:S(2)}, u32[]{:S(2)}) async-start(bf16[8,136,256]{2,1,0:T(8,128)(2,1)} %combine.1), calls=%async_computation.3 | async-start | bytes 1114112 | tf_op jit(solution)/shard_map/all_to_all | solution.py:403
  (15 other events, 148.9 us)

commit v5 on v4

--- a/solution.py
+++ b/solution.py
@@ -99,27 +99,35 @@
 
 
 def backward_kernel(parts, z_ref, *refs):
-    o_refs = refs[:parts]
-    g_ref, u_ref, gw_ref, uw_ref, dw_ref, gs_ref, us_ref, gi_ref, ui_ref = refs[parts:-parts]
-    p_refs = refs[-parts:]
-    share = p_refs[0].shape[1]
+    o_halves = refs[:parts], refs[parts : 2 * parts]
+    g_ref, u_ref, gw_ref, uw_ref, dw_ref, gs_ref, us_ref = refs[2 * parts : -2 * parts - 2]
+    gi_ref, ui_ref = refs[-2 * parts - 2 : -2 * parts]
+    p_halves = refs[-2 * parts : -parts], refs[-parts:]
+    share = p_halves[0][0].shape[1]
+    per = pl.num_programs(0) // 2
 
     def cols(c):
         at = lax.rem(z_ref[0] + c, parts)
         return pl.ds(pl.multiple_of(at * share, share), share)
 
-    hg = dot(o_refs[0][...], dw_ref[:, cols(0)], NT)
-    for c in range(1, parts):
-        hg = hg + dot(o_refs[c][...], dw_ref[:, cols(parts - c)], NT)
-    g = g_ref[...]
-    u = u_ref[...]
-    s = jax.nn.sigmoid(g)
-    gi = (hg * u * s * (1.0 + g * (1.0 - s)) * gs_ref[...]).astype(BF16)
-    ui = (hg * (g * s) * us_ref[...]).astype(BF16)
-    gi_ref[...] = gi
-    ui_ref[...] = ui
-    for c in range(parts):
-        p_refs[c][...] = (dot(gi, gw_ref[:, cols(c)]) + dot(ui, uw_ref[:, cols(c)])).astype(BF16)
+    def run(o_refs, p_refs):
+        hg = dot(o_refs[0][...], dw_ref[:, cols(0)], NT)
+        for c in range(1, parts):
+            hg = hg + dot(o_refs[c][...], dw_ref[:, cols(parts - c)], NT)
+        g = g_ref[...]
+        u = u_ref[...]
+        s = jax.nn.sigmoid(g)
+        gi = (hg * u * s * (1.0 + g * (1.0 - s)) * gs_ref[...]).astype(BF16)
+        ui = (hg * (g * s) * us_ref[...]).astype(BF16)
+        gi_ref[...] = gi
+        ui_ref[...] = ui
+        for c in range(parts):
+            p_refs[c][...] = (dot(gi, gw_ref[:, cols(c)]) + dot(ui, uw_ref[:, cols(c)])).astype(BF16)
+
+    for j in range(2):
+        pl.when(lax.div(pl.program_id(0), per) == j)(
+            functools.partial(run, o_halves[j], p_halves[j])
+        )
 
 
 def combine_kernel(cap, parts, z_ref, y_ref, mt_ref, mw_ref, re_ref, *refs):
@@ -177,11 +185,10 @@
     r_ref[...] = total[toks : toks + choose, :toks]
 
 
-def weight_kernel(x_ref, *refs):
-    gi_refs, ui_refs, gg_ref, ug_ref = refs[:2], refs[2:4], refs[4], refs[5]
+def weight_kernel(x_ref, gi_ref, ui_ref, gg_ref, ug_ref):
     x = x_ref[...]
-    gg_ref[...] = dot(jnp.concatenate([r[...] for r in gi_refs], axis=0), x, TN)
-    ug_ref[...] = dot(jnp.concatenate([r[...] for r in ui_refs], axis=0), x, TN)
+    gg_ref[...] = dot(gi_ref[...], x, TN)
+    ug_ref[...] = dot(ui_ref[...], x, TN)
 
 
 def down_kernel(parts, z_ref, h_ref, _, *refs):
@@ -304,7 +311,7 @@
         cost_estimate=cost(6 * slots * toks * owners, 6 * slots * toks),
     )(route_expert, route_weight)
 
-    block = 256
+    block = 512
     row_hid = pl.BlockSpec((block, hid), lambda i, *_: (i, 0))
     row_wide = pl.BlockSpec((block, width), lambda i, *_: (i, 0))
     g, u, h, out_rows = pl.pallas_call(
@@ -333,40 +340,33 @@
 
     block = 256
     per = rows // block
-    halves = []
-    for j in range(2):
-        row_in = pl.BlockSpec((block, hid), lambda i, z, j=j: (i + j * per, 0))
-        row_out = pl.BlockSpec((block, hid), lambda i, z: (i, 0))
-        halves.append(
-            pl.pallas_call(
-                functools.partial(backward_kernel, parts),
-                name="backward",
-                grid_spec=pltpu.PrefetchScalarGridSpec(
-                    num_scalar_prefetch=1,
-                    grid=(per,),
-                    in_specs=[pl.BlockSpec((block, share), lambda i, z: (i, 0))] * parts
-                    + [row_in] * 2
-                    + [full(hid, width)] * 3
-                    + [full(1, hid)] * 2,
-                    out_specs=[row_out] * 2
-                    + [pl.BlockSpec((block, share), lambda i, z: (i, 0))] * parts,
-                ),
-                out_shape=[sds((rows, hid), BF16)] * 2 + [sds((rows, share), BF16)] * parts,
-                cost_estimate=cost(3 * slots * width * hid, 2 * slots * width),
-            )(col, *out_grad[j], g, u, gw, uw, dw, gate_scale, up_scale)
-        )
-    input_cols = ring_scatter([half[2:] for half in halves])
+    row_hid = pl.BlockSpec((block, hid), lambda i, z: (i, 0))
+    row_share = [pl.BlockSpec((block, share), lambda i, z: (jnp.minimum(i, per - 1), 0))] * parts
+    row_share += [pl.BlockSpec((block, share), lambda i, z: (jnp.maximum(i - per, 0), 0))] * parts
+    gate_in, up_in, *shares = pl.pallas_call(
+        functools.partial(backward_kernel, parts),
+        name="backward",
+        grid_spec=pltpu.PrefetchScalarGridSpec(
+            num_scalar_prefetch=1,
+            grid=(2 * per,),
+            in_specs=row_share + [row_hid] * 2 + [full(hid, width)] * 3 + [full(1, hid)] * 2,
+            out_specs=[row_hid] * 2 + row_share,
+        ),
+        out_shape=[sds((slots, hid), BF16)] * 2 + [sds((rows, share), BF16)] * (2 * parts),
+        cost_estimate=cost(6 * slots * width * hid, 4 * slots * width),
+    )(col, *out_grad[0], *out_grad[1], g, u, gw, uw, dw, gate_scale, up_scale)
+    input_cols = ring_scatter([shares[:parts], shares[parts:]])
 
     col_hid = pl.BlockSpec((hid, share), lambda i: (0, i))
     gate_grad, up_grad = pl.pallas_call(
         weight_kernel,
         name="weight",
         grid=(parts,),
-        in_specs=[pl.BlockSpec((slots, share), lambda i: (0, i))] + [full(rows, hid)] * 4,
+        in_specs=[pl.BlockSpec((slots, share), lambda i: (0, i))] + [full(slots, hid)] * 2,
         out_specs=[col_hid] * 2,
         out_shape=[sds((hid, width), F32)] * 2,
         cost_estimate=cost(4 * slots * width * hid, 2 * slots * width + 8 * hid * width),
-    )(arrived, halves[0][0], halves[1][0], halves[0][1], halves[1][1])
+    )(arrived, gate_in, up_in)
     down_grad = pl.pallas_call(
         functools.partial(down_kernel, parts),
         name="down",

time: 229 us -> 220 us (0.961)
  starting transfers between devices: 81.1 us -> 73.4 us
  other arithmetic: 4.93 us -> 8.73 us
  waiting for transfers between devices: 83.6 us -> 81.2 us
    all_to_all x1, waiting for transfers between devices: 33.2 us -> 21.6 us  [step(): lax.all_to_all(tok_send.reshape(owners, cap, width), 'dp', split_axis=0,...]
    ppermute x28, waiting for transfers between devices: 40.9 us -> 49.8 us  [shift(): lax.ppermute(x, 'expert', [(i, (i + by) % size) for i in range(size)])]
    ppermute x28, starting transfers between devices: 47.5 us -> 41.2 us  [shift(): lax.ppermute(x, 'expert', [(i, (i + by) % size) for i in range(size)])]
    convert_element_type x13, other arithmetic: 4.06 us -> 7.86 us  [add(): return sum((t.astype(F32) for t in terms)).astype(BF16)]
    pallas_call x2 -> x1, Pallas kernels: 12.6 us -> 11.2 us  [step(): pl.pallas_call(functools.partial(backward_kernel, parts), name='backward'...]
  transfers between devices with their start and end apart: 33 -> 33, of which waited for: 13 -> 18; matrix products, arithmetic and copies ran while one was open for 5% -> 7% of each run, Pallas kernels for 20% -> 20%
where the time goes in v5:
time: 220 us; the launch traced here: 218 us
  waiting for transfers between devices  81.2 us (37%)
  starting transfers between devices  73.4 us (33%)
  Pallas kernels  45.9 us (21%)
  other arithmetic  8.73 us (4%)
  matrix products  5.07 us (2%)
  local copies, waits for them, and re-layouts  2.41 us (1%)
    ppermute x28, waiting for transfers between devices, shift(): lax.ppermute(x, 'expert', [(i, (i + by) % size) for i in range(size)])  49.8 us
    ppermute x28, starting transfers between devices, shift(): lax.ppermute(x, 'expert', [(i, (i + by) % size) for i in range(size)])  41.2 us
    all_to_all x1, waiting for transfers between devices, step(): lax.all_to_all(tok_send.reshape(owners, cap, width), 'dp', split_axis=0,...  21.6 us
    pallas_call x1, Pallas kernels, step(): pl.pallas_call(functools.partial(backward_kernel, parts), name='backward'...  11.2 us
    pallas_call x1, Pallas kernels, step(): pl.pallas_call(functools.partial(combine_kernel, cap, parts), name='combi...  8.97 us
    pallas_call x1, Pallas kernels, step(): pl.pallas_call(weight_kernel, name='weight', grid=(parts,), in_specs=[pl....  8.44 us
    convert_element_type x13, other arithmetic, add(): return sum((t.astype(F32) for t in terms)).astype(BF16)  7.86 us
    all_to_all x1, starting transfers between devices, step(): lax.all_to_all(cot_send.reshape(owners, cap, share), 'dp', split_axis=0,...  7.62 us
  transfers between devices with their start and end apart: 33, of which 18 were waited for; matrix products, arithmetic and copies ran while one was open for 7% of the time, Pallas kernels for 20%

profile of v5, /device:TPU:2, one launch (start us, length us, event | category | flops | bytes accessed | tf_op | source)
XLA Modules:
  0.0 217.6 jit_solution(13374764808459197977)
XLA Ops:
  0.7 2.2 route.1
  2.8 7.6 %all-to-all-start.2 = ((bf16[32,32,256]{2,1,0:T(8,128)(2,1)}), bf16[32,32,256]{2,1,0:T(8,128)(2,1)S(1)}, u32[]{:S(2)}, u32[]{:S(2)}) async-start(bf16[32,32,256]{2,1,0:T(8,128)(2,1)} %bitcast.36), calls=%async_computation.2 | async-start | bytes 1048576 | tf_op jit(solution)/shard_map/all_to_all | solution.py:288
  10.5 4.2 %fusion.2 = bf16[1024,2048]{1,0:T(8,128)(2,1)} fusion(bf16[1024,128]{1,0:T(8,128)(2,1)} %get-tuple-element.36, bf16[128,2048]{1,0:T(8,128)(2,1)S(1)} %copy-done), kind=kOutput, calls=%fused_computation.19 | convolution fusion | flops 536870912 | bytes 4980736 | tf_op jit(solution)/shard_map/dot_general | solution.py:291
  14.7 6.2 %all-to-all-done.2 = bf16[32,32,256]{2,1,0:T(8,128)(2,1)S(1)} async-done(((bf16[32,32,256]{2,1,0:T(8,128)(2,1)}), bf16[32,32,256]{2,1,0:T(8,128)(2,1)S(1)}, u32[]{:S(2)}, u32[]{:S(2)}) %all-to-all-start.2) | async-done | bytes 524320 | tf_op jit(solution)/shard_map/all_to_all | solution.py:288
  20.8 6.0 %all-to-all-start = ((bf16[32,32,2048]{2,1,0:T(8,128)(2,1)}), bf16[32,32,2048]{2,1,0:T(8,128)(2,1)}, u32[]{:S(2)}, u32[]{:S(2)}) async-start(bf16[32,32,2048]{2,1,0:T(8,128)(2,1)} %bitcast.24), calls=%async_computation | async-start | bytes 8388608 | tf_op jit(solution)/shard_map/all_to_all | solution.py:292
  27.0 2.0 collective-permute-start
  29.0 4.0 %collective-permute-start.10 = (bf16[576,256]{1,0:T(8,128)(2,1)S(1)}, bf16[576,256]{1,0:T(8,128)(2,1)S(1)}, u32[]{:S(2)}, u32[]{:S(2)}) collective-permute-start(bf16[576,256]{1,0:T(8,128)(2,1)S(1)} %pad_maximum_fusion.2.refs_8_), channel_id=1, source_target_pairs={{0,7},{1,0},{2,1},{3,2},{4,3},{5,4},{6,5},{7,6},{8,15},{9,8},{10,9... | collective-permute-start | bytes 884744 | tf_op jit(solution)/shard_map/ppermute | solution.py:207
  33.0 2.0 collective-permute-start.4
  35.1 5.7 %collective-permute-done.refs_1_ = bf16[576,256]{1,0:T(8,128)(2,1)S(1)} collective-permute-done((bf16[576,256]{1,0:T(8,128)(2,1)S(1)}, bf16[576,256]{1,0:T(8,128)(2,1)S(1)}, u32[]{:S(2)}, u32[]{:S(2)}) %collective-permute-start) | collective-permute-done | bytes 294944 | tf_op jit(solution)/shard_map/ppermute | solution.py:207
  40.8 3.3 %collective-permute-start.11 = (bf16[576,256]{1,0:T(8,128)(2,1)S(1)}, bf16[576,256]{1,0:T(8,128)(2,1)S(1)}, u32[]{:S(2)}, u32[]{:S(2)}) collective-permute-start(bf16[576,256]{1,0:T(8,128)(2,1)S(1)} %collective-permute-done.10.refs_15_), channel_id=1, source_target_pairs={{0,7},{1,0},{2,1},{3,2},{4,3},{5,4},{6,5},{7,6},{8,15},{9,8},{10,9... | collective-permute-start | bytes 884744 | tf_op jit(solution)/shard_map/ppermute | solution.py:207
  44.1 2.6 %collective-permute-done.4.refs_7_ = bf16[576,256]{1,0:T(8,128)(2,1)S(1)} collective-permute-done((bf16[576,256]{1,0:T(8,128)(2,1)S(1)}, bf16[576,256]{1,0:T(8,128)(2,1)S(1)}, u32[]{:S(2)}, u32[]{:S(2)}) %collective-permute-start.4) | collective-permute-done | bytes 294944 | tf_op jit(solution)/shard_map/ppermute | solution.py:207
  46.8 3.7 %collective-permute-start.5 = (bf16[576,256]{1,0:T(8,128)(2,1)S(1)}, bf16[576,256]{1,0:T(8,128)(2,1)}, u32[]{:S(2)}, u32[]{:S(2)}) collective-permute-start(bf16[576,256]{1,0:T(8,128)(2,1)S(1)} %collective-permute-done.4.refs_7_), channel_id=1, source_target_pairs={{0,7},{1,0},{2,1},{3,2},{4,3},{5,4},{6,5},{7,6},{8,15},{9,8},{10,9... | collective-permute-start | bytes 884744 | tf_op jit(solution)/shard_map/ppermute | solution.py:207
  50.5 2.7 %collective-permute-done.1.refs_2_ = bf16[576,256]{1,0:T(8,128)(2,1)S(1)} collective-permute-done((bf16[576,256]{1,0:T(8,128)(2,1)S(1)}, bf16[576,256]{1,0:T(8,128)(2,1)S(1)}, u32[]{:S(2)}, u32[]{:S(2)}) %collective-permute-start.1) | collective-permute-done | bytes 294944 | tf_op jit(solution)/shard_map/ppermute | solution.py:207
  53.2 3.6 %collective-permute-start.12 = (bf16[576,256]{1,0:T(8,128)(2,1)S(1)}, bf16[576,256]{1,0:T(8,128)(2,1)}, u32[]{:S(2)}, u32[]{:S(2)}) collective-permute-start(bf16[576,256]{1,0:T(8,128)(2,1)S(1)} %collective-permute-done.11.refs_14_), channel_id=1, source_target_pairs={{0,7},{1,0},{2,1},{3,2},{4,3},{5,4},{6,5},{7,6},{8,15},{9,8},{10,9... | collective-permute-start | bytes 884744 | tf_op jit(solution)/shard_map/ppermute | solution.py:207
  56.8 21.6 %all-to-all-done = bf16[32,32,2048]{2,1,0:T(8,128)(2,1)} async-done(((bf16[32,32,2048]{2,1,0:T(8,128)(2,1)}), bf16[32,32,2048]{2,1,0:T(8,128)(2,1)}, u32[]{:S(2)}, u32[]{:S(2)}) %all-to-all-start) | async-done | bytes 4194336 | tf_op jit(solution)/shard_map/all_to_all | solution.py:292
  78.4 7.5 %forward.1 = (f32[1024,176]{1,0:T(8,128)}, f32[1024,176]{1,0:T(8,128)}, bf16[1024,176]{1,0:T(8,128)(2,1)}, bf16[1024,2048]{1,0:T(8,128)(2,1)}) custom-call(s32[1]{0:T(128)} %bitcast.1.e_ref, bf16[1024,2048]{1,0:T(8,128)(2,1)} %bitcast.5.x_ref, bf16[176,2048]{1,0:T(8,128)(2,1)} %bitcast.30, bf16[176,2048]{1,0:T(8,128)(2,1)} %bitcast.32, ...), custom_call_target="tpu_custom_call" | custom-call | flops 2214592512 | bytes 8388608 | tf_op jit(solution)/shard_map/forward/pallas_call | solution.py:317
  86.0 7.5 %all-to-all-start.1 = ((bf16[32,32,2048]{2,1,0:T(8,128)(2,1)}), bf16[32,32,2048]{2,1,0:T(8,128)(2,1)}, u32[]{:S(2)}, u32[]{:S(2)}) async-start(bf16[32,32,2048]{2,1,0:T(8,128)(2,1)} %bitcast.25), calls=%async_computation.1 | async-start | bytes 8388608 | tf_op jit(solution)/shard_map/all_to_all | solution.py:337
  93.5 5.9 %collective-permute-start.6 = (bf16[576,256]{1,0:T(8,128)(2,1)}, bf16[576,256]{1,0:T(8,128)(2,1)S(1)}, u32[]{:S(2)}, u32[]{:S(2)}) collective-permute-start(bf16[576,256]{1,0:T(8,128)(2,1)} %collective-permute-done.5.refs_6_), channel_id=1, source_target_pairs={{0,7},{1,0},{2,1},{3,2},{4,3},{5,4},{6,5},{7,6},{8,15},{9,8},{10,9... | collective-permute-start | bytes 884744 | tf_op jit(solution)/shard_map/ppermute | solution.py:207
  99.5 3.2 %collective-permute-start.13 = (bf16[576,256]{1,0:T(8,128)(2,1)}, bf16[576,256]{1,0:T(8,128)(2,1)S(1)}, u32[]{:S(2)}, u32[]{:S(2)}) collective-permute-start(bf16[576,256]{1,0:T(8,128)(2,1)} %collective-permute-done.12.refs_13_), channel_id=1, source_target_pairs={{0,7},{1,0},{2,1},{3,2},{4,3},{5,4},{6,5},{7,6},{8,15},{9,8},{10,9... | collective-permute-start | bytes 884744 | tf_op jit(solution)/shard_map/ppermute | solution.py:207
  102.7 4.4 %collective-permute-done.6.refs_5_ = bf16[576,256]{1,0:T(8,128)(2,1)S(1)} collective-permute-done((bf16[576,256]{1,0:T(8,128)(2,1)}, bf16[576,256]{1,0:T(8,128)(2,1)S(1)}, u32[]{:S(2)}, u32[]{:S(2)}) %collective-permute-start.6) | collective-permute-done | bytes 294944 | tf_op jit(solution)/shard_map/ppermute | solution.py:207
  107.1 3.6 %collective-permute-done.9.refs_11_ = bf16[576,256]{1,0:T(8,128)(2,1)S(1)} collective-permute-done((bf16[576,256]{1,0:T(8,128)(2,1)}, bf16[576,256]{1,0:T(8,128)(2,1)S(1)}, u32[]{:S(2)}, u32[]{:S(2)}) %collective-permute-start.9) | collective-permute-done | bytes 294944 | tf_op jit(solution)/shard_map/ppermute | solution.py:207
  110.7 5.2 %collective-permute-done.3.refs_4_ = bf16[576,256]{1,0:T(8,128)(2,1)S(1)} collective-permute-done((bf16[576,256]{1,0:T(8,128)(2,1)}, bf16[576,256]{1,0:T(8,128)(2,1)S(1)}, u32[]{:S(2)}, u32[]{:S(2)}) %collective-permute-start.3) | collective-permute-done | bytes 294944 | tf_op jit(solution)/shard_map/ppermute | solution.py:207
  116.7 11.2 %backward.1 = (bf16[1024,176]{1,0:T(8,128)(2,1)}, bf16[1024,176]{1,0:T(8,128)(2,1)}, bf16[512,256]{1,0:T(8,128)(2,1)}, bf16[512,256]{1,0:T(8,128)(2,1)}, bf16[51...) custom-call(s32[1]{0:T(128)} %bitcast.col_ref.z_ref, ...), custom_call_target="tpu_custom_call" | custom-call | flops 2214592512 | bytes 8388608 | tf_op jit(solution)/shard_map/backward/pallas_call | solution.py:346
  128.3 1.8 collective-permute-start.21
  130.1 1.4 collective-permute-start.18
  132.1 5.3 %collective-permute-done.24 = bf16[512,256]{1,0:T(8,128)(2,1)S(1)} collective-permute-done((bf16[512,256]{1,0:T(8,128)(2,1)}, bf16[512,256]{1,0:T(8,128)(2,1)S(1)}, u32[]{:S(2)}, u32[]{:S(2)}) %collective-permute-start.24) | collective-permute-done | bytes 262176 | tf_op jit(solution)/shard_map/ppermute | solution.py:207
  138.5 1.5 collective-permute-start.25
  140.0 1.0 add_convert_fusion.5
  141.7 1.4 collective-permute-done.18
  144.1 1.5 collective-permute-start.19
  145.6 1.0 add_convert_fusion.11
  147.5 1.2 collective-permute-done.25
  149.8 1.7 collective-permute-start.26
  153.0 3.5 %collective-permute-done.15 = bf16[512,256]{1,0:T(8,128)(2,1)S(1)} collective-permute-done((bf16[512,256]{1,0:T(8,128)(2,1)S(1)}, bf16[512,256]{1,0:T(8,128)(2,1)S(1)}, u32[]{:S(2)}, u32[]{:S(2)}) %collective-permute-start.15) | collective-permute-done | bytes 262176 | tf_op jit(solution)/shard_map/ppermute | solution.py:207
  156.9 1.2 collective-permute-done.26
  158.1 1.9 collective-permute-start.27
  160.2 5.5 %collective-permute-done.16 = bf16[512,256]{1,0:T(8,128)(2,1)S(1)} collective-permute-done((bf16[512,256]{1,0:T(8,128)(2,1)S(1)}, bf16[512,256]{1,0:T(8,128)(2,1)S(1)}, u32[]{:S(2)}, u32[]{:S(2)}) %collective-permute-start.16) | collective-permute-done | bytes 262176 | tf_op jit(solution)/shard_map/ppermute | solution.py:207
  165.9 1.5 collective-permute-done.27
  167.5 2.8 %collective-permute-done.20 = bf16[512,256]{1,0:T(8,128)(2,1)S(1)} collective-permute-done((bf16[512,256]{1,0:T(8,128)(2,1)S(1)}, bf16[512,256]{1,0:T(8,128)(2,1)S(1)}, u32[]{:S(2)}, u32[]{:S(2)}) %collective-permute-start.20) | collective-permute-done | bytes 262176 | tf_op jit(solution)/shard_map/ppermute | solution.py:207
  170.3 3.2 %collective-permute-done.17 = bf16[512,256]{1,0:T(8,128)(2,1)S(1)} collective-permute-done((bf16[512,256]{1,0:T(8,128)(2,1)S(1)}, bf16[512,256]{1,0:T(8,128)(2,1)S(1)}, u32[]{:S(2)}, u32[]{:S(2)}) %collective-permute-start.17) | collective-permute-done | bytes 262176 | tf_op jit(solution)/shard_map/ppermute | solution.py:207
  174.4 7.5 %all-to-all-start.4 = ((bf16[32,32,256]{2,1,0:T(8,128)(2,1)}), bf16[32,32,256]{2,1,0:T(8,128)(2,1)S(1)}, u32[]{:S(2)}, u32[]{:S(2)}) async-start(bf16[32,32,256]{2,1,0:T(8,128)(2,1)} %bitcast.14), calls=%async_computation.4 | async-start | bytes 1048576 | tf_op jit(solution)/shard_map/all_to_all | solution.py:415
  183.4 2.3 %home.1 = (bf16[128,1024]{1,0:T(8,128)(2,1)}, bf16[256,1024]{1,0:T(8,128)(2,1)}) custom-call(s32[128,4]{1,0:T(8,128)} %copy.16.re_ref, f32[128,4]{1,0:T(8,128)} %copy.17.rw_ref), custom_call_target="tpu_custom_call" | custom-call | flops 25165824 | bytes 786432 | tf_op jit(solution)/shard_map/home/pallas_call | solution.py:304
  185.7 9.0 %combine.1 = bf16[8,136,256]{2,1,0:T(8,128)(2,1)} custom-call(s32[1]{0:T(128)} %bitcast.col_ref.z_ref, bf16[1024,2048]{1,0:T(8,128)(2,1)} %bitcast.10.y_ref, bf16[128,1024]{1,0:T(8,128)(2,1)} %get-tuple-element.38.mt_ref, bf16[256,1024]{1,0:T(8,128)(2,1)} %get-tuple-element.39.mw_ref, s32[4,128]{1,0:T(4,128)} %bitcast.38, bf16[576,256]{1,0:T(8,128)(2,1)} %copy-done.1, ...), custom_call_target="tpu_custom_call" | custom-call | flops 1610612736 | bytes 4194304 | tf_op jit(solution)/shard_map/combine/pallas_call | solution.py:384
  194.7 3.5 %all-to-all-start.3 = ((bf16[8,136,256]{2,1,0:T(8,128)(2,1)}), bf16[8,136,256]{2,1,0:T(8,128)(2,1)S(1)}, u32[]{:S(2)}, u32[]{:S(2)}) async-start(bf16[8,136,256]{2,1,0:T(8,128)(2,1)} %combine.1), calls=%async_computation.3 | async-start | bytes 1114112 | tf_op jit(solution)/shard_map/all_to_all | solution.py:403
  198.2 1.3 add_convert_fusion.12._
  199.5 4.5 %down.1 = f32[176,2048]{1,0:T(8,128)} custom-call(s32[1]{0:T(128)} %bitcast.col_ref.z_ref, bf16[1024,176]{1,0:T(8,128)(2,1)} %get-tuple-element.65.h_ref, bf16[8,128]{1,0:T(8,128)(2,1)} %add_convert_fusion.12._, bf16[576,256]{1,0:T(8,128)(2,1)} %copy-done.1, bf16[576,256]{1,0:T(8,128)(2,1)} %copy-done.7, bf16[576,256]{1,0:T(8,128)(2,1)} %copy-done.11, ...), custom_call_target="tpu_custom_call" | custom-call | flops 738197504 | bytes 5636096 | tf_op jit(solution)/shard_map/down/pallas_call | solution.py:370
  204.0 8.4 %weight.1 = (f32[176,2048]{1,0:T(8,128)}, f32[176,2048]{1,0:T(8,128)}) custom-call(bf16[1024,2048]{1,0:T(8,128)(2,1)} %bitcast.5.x_ref, bf16[1024,176]{1,0:T(8,128)(2,1)} %get-tuple-element.61.gi_ref, bf16[1024,176]{1,0:T(8,128)(2,1)} %get-tuple-element.62.ui_ref), custom_call_target="tpu_custom_call" | custom-call | flops 1476395008 | bytes 7077888 | tf_op jit(solution)/shard_map/weight/pallas_call | solution.py:361
  213.4 3.6 %all-to-all-done.3.x_ref = bf16[8,136,256]{2,1,0:T(8,128)(2,1)S(1)} async-done(((bf16[8,136,256]{2,1,0:T(8,128)(2,1)}), bf16[8,136,256]{2,1,0:T(8,128)(2,1)S(1)}, u32[]{:S(2)}, u32[]{:S(2)}) %all-to-all-start.3) | async-done | bytes 557088 | tf_op jit(solution)/shard_map/all_to_all | solution.py:403
  (94 shorter events, 13.1 us)
Async XLA Ops:
  2.8 18.0 %all-to-all-start.2 = ((bf16[32,32,256]{2,1,0:T(8,128)(2,1)}), bf16[32,32,256]{2,1,0:T(8,128)(2,1)S(1)}, u32[]{:S(2)}, u32[]{:S(2)}) async-start(bf16[32,32,256]{2,1,0:T(8,128)(2,1)} %bitcast.36), calls=%async_computation.2 | async-start | bytes 1048576 | tf_op jit(solution)/shard_map/all_to_all | solution.py:288
  20.8 57.6 %all-to-all-start = ((bf16[32,32,2048]{2,1,0:T(8,128)(2,1)}), bf16[32,32,2048]{2,1,0:T(8,128)(2,1)}, u32[]{:S(2)}, u32[]{:S(2)}) async-start(bf16[32,32,2048]{2,1,0:T(8,128)(2,1)} %bitcast.24), calls=%async_computation | async-start | bytes 8388608 | tf_op jit(solution)/shard_map/all_to_all | solution.py:292
  27.0 58.9 %copy-start.1 = (bf16[576,256]{1,0:T(8,128)(2,1)}, bf16[576,256]{1,0:T(8,128)(2,1)S(1)}, u32[]{:S(2)}) copy-start(bf16[576,256]{1,0:T(8,128)(2,1)S(1)} %pad_maximum_fusion.1.refs_0_) | copy-start | bytes 884740
  27.0 13.8 %collective-permute-start = (bf16[576,256]{1,0:T(8,128)(2,1)S(1)}, bf16[576,256]{1,0:T(8,128)(2,1)S(1)}, u32[]{:S(2)}, u32[]{:S(2)}) collective-permute-start(bf16[576,256]{1,0:T(8,128)(2,1)S(1)} %pad_maximum_fusion.1.refs_0_), channel_id=1, source_target_pairs={{0,1},{1,2},{2,3},{3,4},{4,5},{5,6},{6,7},{7,0},{8,9},{9,10},{10,1... | collective-permute-start | bytes 884744 | tf_op jit(solution)/shard_map/ppermute | solution.py:207
  29.0 56.9 %copy-start.2 = (bf16[576,256]{1,0:T(8,128)(2,1)}, bf16[576,256]{1,0:T(8,128)(2,1)S(1)}, u32[]{:S(2)}) copy-start(bf16[576,256]{1,0:T(8,128)(2,1)S(1)} %pad_maximum_fusion.2.refs_8_) | copy-start | bytes 884740
  29.0 11.8 %collective-permute-start.10 = (bf16[576,256]{1,0:T(8,128)(2,1)S(1)}, bf16[576,256]{1,0:T(8,128)(2,1)S(1)}, u32[]{:S(2)}, u32[]{:S(2)}) collective-permute-start(bf16[576,256]{1,0:T(8,128)(2,1)S(1)} %pad_maximum_fusion.2.refs_8_), channel_id=1, source_target_pairs={{0,7},{1,0},{2,1},{3,2},{4,3},{5,4},{6,5},{7,6},{8,15},{9,8},{10,9... | collective-permute-start | bytes 884744 | tf_op jit(solution)/shard_map/ppermute | solution.py:207
  33.0 13.7 %collective-permute-start.4 = (bf16[576,256]{1,0:T(8,128)(2,1)S(1)}, bf16[576,256]{1,0:T(8,128)(2,1)S(1)}, u32[]{:S(2)}, u32[]{:S(2)}) collective-permute-start(bf16[576,256]{1,0:T(8,128)(2,1)S(1)} %pad_maximum_fusion.1.refs_0_), channel_id=1, source_target_pairs={{0,7},{1,0},{2,1},{3,2},{4,3},{5,4},{6,5},{7,6},{8,15},{9,8},{10,9... | collective-permute-start | bytes 884744 | tf_op jit(solution)/shard_map/ppermute | solution.py:207
  35.0 15.4 %collective-permute-start.7 = (bf16[576,256]{1,0:T(8,128)(2,1)S(1)}, bf16[576,256]{1,0:T(8,128)(2,1)S(1)}, u32[]{:S(2)}, u32[]{:S(2)}) collective-permute-start(bf16[576,256]{1,0:T(8,128)(2,1)S(1)} %pad_maximum_fusion.2.refs_8_), channel_id=1, source_target_pairs={{0,1},{1,2},{2,3},{3,4},{4,5},{5,6},{6,7},{7,0},{8,9},{9,10},{10,1... | collective-permute-start | bytes 884744 | tf_op jit(solution)/shard_map/ppermute | solution.py:207
  40.8 45.1 %copy-start.7 = (bf16[576,256]{1,0:T(8,128)(2,1)}, bf16[576,256]{1,0:T(8,128)(2,1)S(1)}, u32[]{:S(2)}) copy-start(bf16[576,256]{1,0:T(8,128)(2,1)S(1)} %collective-permute-done.refs_1_) | copy-start | bytes 884740
  40.8 12.4 %collective-permute-start.1 = (bf16[576,256]{1,0:T(8,128)(2,1)S(1)}, bf16[576,256]{1,0:T(8,128)(2,1)S(1)}, u32[]{:S(2)}, u32[]{:S(2)}) collective-permute-start(bf16[576,256]{1,0:T(8,128)(2,1)S(1)} %collective-permute-done.refs_1_), channel_id=1, source_target_pairs={{0,1},{1,2},{2,3},{3,4},{4,5},{5,6},{6,7},{7,0},{8,9},{9,10},{10,1... | collective-permute-start | bytes 884744 | tf_op jit(solution)/shard_map/ppermute | solution.py:207
  40.8 45.1 %copy-start.8 = (bf16[576,256]{1,0:T(8,128)(2,1)}, bf16[576,256]{1,0:T(8,128)(2,1)S(1)}, u32[]{:S(2)}) copy-start(bf16[576,256]{1,0:T(8,128)(2,1)S(1)} %collective-permute-done.10.refs_15_) | copy-start | bytes 884740
  40.8 12.4 %collective-permute-start.11 = (bf16[576,256]{1,0:T(8,128)(2,1)S(1)}, bf16[576,256]{1,0:T(8,128)(2,1)S(1)}, u32[]{:S(2)}, u32[]{:S(2)}) collective-permute-start(bf16[576,256]{1,0:T(8,128)(2,1)S(1)} %collective-permute-done.10.refs_15_), channel_id=1, source_target_pairs={{0,7},{1,0},{2,1},{3,2},{4,3},{5,4},{6,5},{7,6},{8,15},{9,8},{10,9... | collective-permute-start | bytes 884744 | tf_op jit(solution)/shard_map/ppermute | solution.py:207
  46.8 39.2 %copy-start.9 = (bf16[576,256]{1,0:T(8,128)(2,1)}, bf16[576,256]{1,0:T(8,128)(2,1)S(1)}, u32[]{:S(2)}) copy-start(bf16[576,256]{1,0:T(8,128)(2,1)S(1)} %collective-permute-done.4.refs_7_) | copy-start | bytes 884740
  46.8 46.7 %collective-permute-start.5 = (bf16[576,256]{1,0:T(8,128)(2,1)S(1)}, bf16[576,256]{1,0:T(8,128)(2,1)}, u32[]{:S(2)}, u32[]{:S(2)}) collective-permute-start(bf16[576,256]{1,0:T(8,128)(2,1)S(1)} %collective-permute-done.4.refs_7_), channel_id=1, source_target_pairs={{0,7},{1,0},{2,1},{3,2},{4,3},{5,4},{6,5},{7,6},{8,15},{9,8},{10,9... | collective-permute-start | bytes 884744 | tf_op jit(solution)/shard_map/ppermute | solution.py:207
  50.5 35.5 %copy-start.10 = (bf16[576,256]{1,0:T(8,128)(2,1)}, bf16[576,256]{1,0:T(8,128)(2,1)S(1)}, u32[]{:S(2)}) copy-start(bf16[576,256]{1,0:T(8,128)(2,1)S(1)} %collective-permute-done.7.refs_9_) | copy-start | bytes 884740
  50.5 49.0 %collective-permute-start.8 = (bf16[576,256]{1,0:T(8,128)(2,1)S(1)}, bf16[576,256]{1,0:T(8,128)(2,1)}, u32[]{:S(2)}, u32[]{:S(2)}) collective-permute-start(bf16[576,256]{1,0:T(8,128)(2,1)S(1)} %collective-permute-done.7.refs_9_), channel_id=1, source_target_pairs={{0,1},{1,2},{2,3},{3,4},{4,5},{5,6},{6,7},{7,0},{8,9},{9,10},{10,1... | collective-permute-start | bytes 884744 | tf_op jit(solution)/shard_map/ppermute | solution.py:207
  53.2 32.8 %copy-start.11 = (bf16[576,256]{1,0:T(8,128)(2,1)}, bf16[576,256]{1,0:T(8,128)(2,1)S(1)}, u32[]{:S(2)}) copy-start(bf16[576,256]{1,0:T(8,128)(2,1)S(1)} %collective-permute-done.1.refs_2_) | copy-start | bytes 884740
  53.2 46.2 %collective-permute-start.2 = (bf16[576,256]{1,0:T(8,128)(2,1)S(1)}, bf16[576,256]{1,0:T(8,128)(2,1)}, u32[]{:S(2)}, u32[]{:S(2)}) collective-permute-start(bf16[576,256]{1,0:T(8,128)(2,1)S(1)} %collective-permute-done.1.refs_2_), channel_id=1, source_target_pairs={{0,1},{1,2},{2,3},{3,4},{4,5},{5,6},{6,7},{7,0},{8,9},{9,10},{10,1... | collective-permute-start | bytes 884744 | tf_op jit(solution)/shard_map/ppermute | solution.py:207
  53.2 32.8 %copy-start.12 = (bf16[576,256]{1,0:T(8,128)(2,1)}, bf16[576,256]{1,0:T(8,128)(2,1)S(1)}, u32[]{:S(2)}) copy-start(bf16[576,256]{1,0:T(8,128)(2,1)S(1)} %collective-permute-done.11.refs_14_) | copy-start | bytes 884740
  53.2 46.3 %collective-permute-start.12 = (bf16[576,256]{1,0:T(8,128)(2,1)S(1)}, bf16[576,256]{1,0:T(8,128)(2,1)}, u32[]{:S(2)}, u32[]{:S(2)}) collective-permute-start(bf16[576,256]{1,0:T(8,128)(2,1)S(1)} %collective-permute-done.11.refs_14_), channel_id=1, source_target_pairs={{0,7},{1,0},{2,1},{3,2},{4,3},{5,4},{6,5},{7,6},{8,15},{9,8},{10,9... | collective-permute-start | bytes 884744 | tf_op jit(solution)/shard_map/ppermute | solution.py:207
  86.0 88.4 %all-to-all-start.1 = ((bf16[32,32,2048]{2,1,0:T(8,128)(2,1)}), bf16[32,32,2048]{2,1,0:T(8,128)(2,1)}, u32[]{:S(2)}, u32[]{:S(2)}) async-start(bf16[32,32,2048]{2,1,0:T(8,128)(2,1)} %bitcast.25), calls=%async_computation.1 | async-start | bytes 8388608 | tf_op jit(solution)/shard_map/all_to_all | solution.py:337
  93.5 13.6 %collective-permute-start.6 = (bf16[576,256]{1,0:T(8,128)(2,1)}, bf16[576,256]{1,0:T(8,128)(2,1)S(1)}, u32[]{:S(2)}, u32[]{:S(2)}) collective-permute-start(bf16[576,256]{1,0:T(8,128)(2,1)} %collective-permute-done.5.refs_6_), channel_id=1, source_target_pairs={{0,7},{1,0},{2,1},{3,2},{4,3},{5,4},{6,5},{7,6},{8,15},{9,8},{10,9... | collective-permute-start | bytes 884744 | tf_op jit(solution)/shard_map/ppermute | solution.py:207
  99.4 11.3 %collective-permute-start.9 = (bf16[576,256]{1,0:T(8,128)(2,1)}, bf16[576,256]{1,0:T(8,128)(2,1)S(1)}, u32[]{:S(2)}, u32[]{:S(2)}) collective-permute-start(bf16[576,256]{1,0:T(8,128)(2,1)} %collective-permute-done.8.refs_10_), channel_id=1, source_target_pairs={{0,1},{1,2},{2,3},{3,4},{4,5},{5,6},{6,7},{7,0},{8,9},{9,10},{10,1... | collective-permute-start | bytes 884744 | tf_op jit(solution)/shard_map/ppermute | solution.py:207
  99.4 16.5 %collective-permute-start.3 = (bf16[576,256]{1,0:T(8,128)(2,1)}, bf16[576,256]{1,0:T(8,128)(2,1)S(1)}, u32[]{:S(2)}, u32[]{:S(2)}) collective-permute-start(bf16[576,256]{1,0:T(8,128)(2,1)} %collective-permute-done.2.refs_3_), channel_id=1, source_target_pairs={{0,1},{1,2},{2,3},{3,4},{4,5},{5,6},{6,7},{7,0},{8,9},{9,10},{10,1... | collective-permute-start | bytes 884744 | tf_op jit(solution)/shard_map/ppermute | solution.py:207
  99.5 16.4 %collective-permute-start.13 = (bf16[576,256]{1,0:T(8,128)(2,1)}, bf16[576,256]{1,0:T(8,128)(2,1)S(1)}, u32[]{:S(2)}, u32[]{:S(2)}) collective-permute-start(bf16[576,256]{1,0:T(8,128)(2,1)} %collective-permute-done.12.refs_13_), channel_id=1, source_target_pairs={{0,7},{1,0},{2,1},{3,2},{4,3},{5,4},{6,5},{7,6},{8,15},{9,8},{10,9... | collective-permute-start | bytes 884744 | tf_op jit(solution)/shard_map/ppermute | solution.py:207
  128.0 30.1 %copy-start.16 = (bf16[512,256]{1,0:T(8,128)(2,1)S(1)}, bf16[512,256]{1,0:T(8,128)(2,1)}, u32[]{:S(2)}) copy-start(bf16[512,256]{1,0:T(8,128)(2,1)} %get-tuple-element.58) | copy-start | bytes 786436
  128.0 32.0 %copy-start.15 = (bf16[512,256]{1,0:T(8,128)(2,1)S(1)}, bf16[512,256]{1,0:T(8,128)(2,1)}, u32[]{:S(2)}) copy-start(bf16[512,256]{1,0:T(8,128)(2,1)} %get-tuple-element.50) | copy-start | bytes 786436
  128.0 37.7 %copy-start.14 = (bf16[512,256]{1,0:T(8,128)(2,1)S(1)}, bf16[512,256]{1,0:T(8,128)(2,1)}, u32[]{:S(2)}) copy-start(bf16[512,256]{1,0:T(8,128)(2,1)} %get-tuple-element.47) | copy-start | bytes 786436
  128.0 39.4 %copy-start.20 = (bf16[512,256]{1,0:T(8,128)(2,1)S(1)}, bf16[512,256]{1,0:T(8,128)(2,1)}, u32[]{:S(2)}) copy-start(bf16[512,256]{1,0:T(8,128)(2,1)} %get-tuple-element.59) | copy-start | bytes 786436
  128.0 9.5 %collective-permute-start.24 = (bf16[512,256]{1,0:T(8,128)(2,1)}, bf16[512,256]{1,0:T(8,128)(2,1)S(1)}, u32[]{:S(2)}, u32[]{:S(2)}) collective-permute-start(bf16[512,256]{1,0:T(8,128)(2,1)} %get-tuple-element.55), channel_id=1, source_target_pairs={{0,7},{1,0},{2,1},{3,2},{4,3},{5,4},{6,5},{7,6},{8,15},{9,8},{10,9... | collective-permute-start | bytes 786440 | tf_op jit(solution)/shard_map/ppermute | solution.py:207
  128.3 11.7 %collective-permute-start.21 = (bf16[512,256]{1,0:T(8,128)(2,1)}, bf16[512,256]{1,0:T(8,128)(2,1)S(1)}, u32[]{:S(2)}, u32[]{:S(2)}) collective-permute-start(bf16[512,256]{1,0:T(8,128)(2,1)} %get-tuple-element.52), channel_id=1, source_target_pairs={{0,1},{1,2},{2,3},{3,4},{4,5},{5,6},{6,7},{7,0},{8,9},{9,10},{10,1... | collective-permute-start | bytes 786440 | tf_op jit(solution)/shard_map/ppermute | solution.py:207
  130.1 13.0 %collective-permute-start.18 = (bf16[512,256]{1,0:T(8,128)(2,1)}, bf16[512,256]{1,0:T(8,128)(2,1)S(1)}, u32[]{:S(2)}, u32[]{:S(2)}) collective-permute-start(bf16[512,256]{1,0:T(8,128)(2,1)} %get-tuple-element.48), channel_id=1, source_target_pairs={{0,7},{1,0},{2,1},{3,2},{4,3},{5,4},{6,5},{7,6},{8,15},{9,8},{10,9... | collective-permute-start | bytes 786440 | tf_op jit(solution)/shard_map/ppermute | solution.py:207
  131.5 14.1 %collective-permute-start.14 = (bf16[512,256]{1,0:T(8,128)(2,1)}, bf16[512,256]{1,0:T(8,128)(2,1)S(1)}, u32[]{:S(2)}, u32[]{:S(2)}) collective-permute-start(bf16[512,256]{1,0:T(8,128)(2,1)} %get-tuple-element.44), channel_id=1, source_target_pairs={{0,1},{1,2},{2,3},{3,4},{4,5},{5,6},{6,7},{7,0},{8,9},{9,10},{10,1... | collective-permute-start | bytes 786440 | tf_op jit(solution)/shard_map/ppermute | solution.py:207
  138.5 35.0 %copy-start.19 = (bf16[512,256]{1,0:T(8,128)(2,1)S(1)}, bf16[512,256]{1,0:T(8,128)(2,1)}, u32[]{:S(2)}) copy-start(bf16[512,256]{1,0:T(8,128)(2,1)} %get-tuple-element.51) | copy-start | bytes 786436
  138.5 10.2 %collective-permute-start.25 = (bf16[512,256]{1,0:T(8,128)(2,1)S(1)}, bf16[512,256]{1,0:T(8,128)(2,1)S(1)}, u32[]{:S(2)}, u32[]{:S(2)}) collective-permute-start(bf16[512,256]{1,0:T(8,128)(2,1)S(1)} %add_convert_fusion.3), channel_id=1, source_target_pairs={{0,7},{1,0},{2,1},{3,2},{4,3},{5,4},{6,5},{7,6},{8,15},{9,8},{10,9... | collective-permute-start | bytes 786440 | tf_op jit(solution)/shard_map/ppermute | solution.py:207
  141.0 10.5 %collective-permute-start.22 = (bf16[512,256]{1,0:T(8,128)(2,1)S(1)}, bf16[512,256]{1,0:T(8,128)(2,1)S(1)}, u32[]{:S(2)}, u32[]{:S(2)}) collective-permute-start(bf16[512,256]{1,0:T(8,128)(2,1)S(1)} %add_convert_fusion.5), channel_id=1, source_target_pairs={{0,1},{1,2},{2,3},{3,4},{4,5},{5,6},{6,7},{7,0},{8,9},{9,10},{10,1... | collective-permute-start | bytes 786440 | tf_op jit(solution)/shard_map/ppermute | solution.py:207
  144.1 15.9 %collective-permute-start.19 = (bf16[512,256]{1,0:T(8,128)(2,1)S(1)}, bf16[512,256]{1,0:T(8,128)(2,1)S(1)}, u32[]{:S(2)}, u32[]{:S(2)}) collective-permute-start(bf16[512,256]{1,0:T(8,128)(2,1)S(1)} %add_convert_fusion.8), channel_id=1, source_target_pairs={{0,7},{1,0},{2,1},{3,2},{4,3},{5,4},{6,5},{7,6},{8,15},{9,8},{10,9... | collective-permute-start | bytes 786440 | tf_op jit(solution)/shard_map/ppermute | solution.py:207
  146.6 9.9 %collective-permute-start.15 = (bf16[512,256]{1,0:T(8,128)(2,1)S(1)}, bf16[512,256]{1,0:T(8,128)(2,1)S(1)}, u32[]{:S(2)}, u32[]{:S(2)}) collective-permute-start(bf16[512,256]{1,0:T(8,128)(2,1)S(1)} %add_convert_fusion.11), channel_id=1, source_target_pairs={{0,1},{1,2},{2,3},{3,4},{4,5},{5,6},{6,7},{7,0},{8,9},{9,10},{10,1... | collective-permute-start | bytes 786440 | tf_op jit(solution)/shard_map/ppermute | solution.py:207
  149.7 32.2 %copy-start.21 = (s32[128,4]{0,1:T(4,128)S(1)}, s32[128,4]{0,1:T(4,128)}, u32[]{:S(2)}) copy-start(s32[128,4]{0,1:T(4,128)} %param.11) | copy-start | bytes 6148
  149.7 32.9 %copy-start.22 = (f32[128,4]{0,1:T(4,128)S(1)}, f32[128,4]{0,1:T(4,128)}, u32[]{:S(2)}) copy-start(f32[128,4]{0,1:T(4,128)} %param.12) | copy-start | bytes 6148
  149.8 8.3 %collective-permute-start.26 = (bf16[512,256]{1,0:T(8,128)(2,1)S(1)}, bf16[512,256]{1,0:T(8,128)(2,1)S(1)}, u32[]{:S(2)}, u32[]{:S(2)}) collective-permute-start(bf16[512,256]{1,0:T(8,128)(2,1)S(1)} %add_convert_fusion.2), channel_id=1, source_target_pairs={{0,7},{1,0},{2,1},{3,2},{4,3},{5,4},{6,5},{7,6},{8,15},{9,8},{10,9... | collective-permute-start | bytes 786440 | tf_op jit(solution)/shard_map/ppermute | solution.py:207
  152.5 13.4 %collective-permute-start.23 = (bf16[512,256]{1,0:T(8,128)(2,1)S(1)}, bf16[512,256]{1,0:T(8,128)(2,1)S(1)}, u32[]{:S(2)}, u32[]{:S(2)}) collective-permute-start(bf16[512,256]{1,0:T(8,128)(2,1)S(1)} %add_convert_fusion.4), channel_id=1, source_target_pairs={{0,1},{1,2},{2,3},{3,4},{4,5},{5,6},{6,7},{7,0},{8,9},{9,10},{10,1... | collective-permute-start | bytes 786440 | tf_op jit(solution)/shard_map/ppermute | solution.py:207
  156.5 9.2 %collective-permute-start.16 = (bf16[512,256]{1,0:T(8,128)(2,1)S(1)}, bf16[512,256]{1,0:T(8,128)(2,1)S(1)}, u32[]{:S(2)}, u32[]{:S(2)}) collective-permute-start(bf16[512,256]{1,0:T(8,128)(2,1)S(1)} %add_convert_fusion.10), channel_id=1, source_target_pairs={{0,1},{1,2},{2,3},{3,4},{4,5},{5,6},{6,7},{7,0},{8,9},{9,10},{10,1... | collective-permute-start | bytes 786440 | tf_op jit(solution)/shard_map/ppermute | solution.py:207
  158.1 9.3 %collective-permute-start.27 = (bf16[512,256]{1,0:T(8,128)(2,1)S(1)}, bf16[512,256]{1,0:T(8,128)(2,1)S(1)}, u32[]{:S(2)}, u32[]{:S(2)}) collective-permute-start(bf16[512,256]{1,0:T(8,128)(2,1)S(1)} %add_convert_fusion.1), channel_id=1, source_target_pairs={{0,7},{1,0},{2,1},{3,2},{4,3},{5,4},{6,5},{7,6},{8,15},{9,8},{10,9... | collective-permute-start | bytes 786440 | tf_op jit(solution)/shard_map/ppermute | solution.py:207
  160.1 10.2 %collective-permute-start.20 = (bf16[512,256]{1,0:T(8,128)(2,1)S(1)}, bf16[512,256]{1,0:T(8,128)(2,1)S(1)}, u32[]{:S(2)}, u32[]{:S(2)}) collective-permute-start(bf16[512,256]{1,0:T(8,128)(2,1)S(1)} %add_convert_fusion.7), channel_id=1, source_target_pairs={{0,7},{1,0},{2,1},{3,2},{4,3},{5,4},{6,5},{7,6},{8,15},{9,8},{10,9... | collective-permute-start | bytes 786440 | tf_op jit(solution)/shard_map/ppermute | solution.py:207
  165.8 7.7 %collective-permute-start.17 = (bf16[512,256]{1,0:T(8,128)(2,1)S(1)}, bf16[512,256]{1,0:T(8,128)(2,1)S(1)}, u32[]{:S(2)}, u32[]{:S(2)}) collective-permute-start(bf16[512,256]{1,0:T(8,128)(2,1)S(1)} %add_convert_fusion.9), channel_id=1, source_target_pairs={{0,1},{1,2},{2,3},{3,4},{4,5},{5,6},{6,7},{7,0},{8,9},{9,10},{10,1... | collective-permute-start | bytes 786440 | tf_op jit(solution)/shard_map/ppermute | solution.py:207
  174.4 20.3 %all-to-all-start.4 = ((bf16[32,32,256]{2,1,0:T(8,128)(2,1)}), bf16[32,32,256]{2,1,0:T(8,128)(2,1)S(1)}, u32[]{:S(2)}, u32[]{:S(2)}) async-start(bf16[32,32,256]{2,1,0:T(8,128)(2,1)} %bitcast.14), calls=%async_computation.4 | async-start | bytes 1048576 | tf_op jit(solution)/shard_map/all_to_all | solution.py:415
  194.7 22.3 %all-to-all-start.3 = ((bf16[8,136,256]{2,1,0:T(8,128)(2,1)}), bf16[8,136,256]{2,1,0:T(8,128)(2,1)S(1)}, u32[]{:S(2)}, u32[]{:S(2)}) async-start(bf16[8,136,256]{2,1,0:T(8,128)(2,1)} %combine.1), calls=%async_computation.3 | async-start | bytes 1114112 | tf_op jit(solution)/shard_map/all_to_all | solution.py:403
  (8 other events, 68.4 us)
